TPU v7x, 256 devices: a whole 4x4x8 slice. The times are simulated.
256 devices in a mesh: vocab: 256 (over z, x, y, core).
Axes of the slice: x: 4, y: 4, z: 8, core: 2. Of those that a mesh axis runs over, the one named last changes fastest.
Arguments:
- hidden: bfloat16 [4096, 2560], P('vocab'), may hold values from -3 to 3
- norm_gain: float32 [2560], replicated, may hold values from 0.1 to 1.9
- head: bfloat16 [2560, 73728], P(None, 'vocab'), may hold values from -50 to 50
- token_ids: int32 [4096], P('vocab'), may hold values from 0 to 73447
- req_len: int32 [512], replicated, may hold values from 1 to 8, as said below
- req_owner: int32 [512], replicated, may hold values from 0 to 255, as said below
Outputs:
- logprob: float32 [4096], P('vocab')
- entropy: float32 [4096], P('vocab')
Inputs may be any that keep to these rules, and one draw needn't show every extreme that they name: `req_len`: each device owns exactly 2 requests; the lengths of one device's requests sum to at most 16, and to exactly 16 on some device. `req_owner`: each device index appears exactly 2 times.
All inputs are finite; a program needn't handle non-finite values.
Results may differ from a plain program's by a relative error of at most 0.0037.
Values may be sent and summed in bfloat16 or wider, within the bound.
A program may use at most 128 MiB of HBM per device.

v0:
```python
import jax
import jax.numpy as jnp
from jax import lax
from jax.sharding import PartitionSpec as P

VOCAB_REAL = 73448


EPS = 1e-05
NEG = -1e30


def slice_stats(rows, chosen, head, col_index, real_cols):
    logits = jnp.dot(rows, head, preferred_element_type=jnp.float32) / 10.0
    logits = jnp.where(real_cols[None, :], logits, NEG)
    rowmax = jnp.max(logits, axis=1)
    expo = jnp.where(real_cols[None, :], jnp.exp(logits - rowmax[:, None]), 0.0)
    total = jnp.sum(expo, axis=1)
    weighted = jnp.sum(jnp.where(real_cols[None, :], expo * logits, 0.0), axis=1)
    picked = jnp.sum(jnp.where(col_index[None, :] == chosen[:, None], logits, 0.0), axis=1)
    return (rowmax, total, weighted, picked)


def body(hidden, norm_gain, head, token_ids, req_len, req_owner):
    local_rows = hidden.shape[0]
    columns = head.shape[1]
    me = lax.axis_index("vocab")
    values = hidden.astype(jnp.float32)
    scale = lax.rsqrt(jnp.mean(values * values, axis=-1, keepdims=True) + EPS)
    normed = (values * scale * norm_gain[None, :]).astype(jnp.bfloat16)
    col_index = me * columns + jnp.arange(columns, dtype=jnp.int32)
    real_cols = col_index < VOCAB_REAL
    all_rows, all_ids = (
        lax.all_gather(normed, "vocab", axis=0, tiled=True),
        lax.all_gather(token_ids, "vocab", axis=0, tiled=True),
    )
    stats = slice_stats(all_rows, all_ids, head, col_index, real_cols)
    rowmax, total, weighted, picked = stats

    def own_part(whole):
        return lax.dynamic_slice_in_dim(whole, me * local_rows, local_rows)

    top_full = lax.pmax(rowmax, "vocab")
    factor = jnp.exp(rowmax - top_full)
    sums = lax.psum((total * factor, weighted * factor, picked), "vocab")
    total_all, weighted_all, picked_all = [own_part(item) for item in sums]
    top = own_part(top_full)
    load = jnp.sum(jnp.where(req_owner == me, req_len, 0))
    live = jnp.arange(local_rows, dtype=jnp.int32) < load
    log_total = jnp.log(total_all)
    logprob = jnp.where(live, picked_all - top - log_total, 0.0)
    entropy = jnp.where(live, top + log_total - weighted_all / total_all, 0.0)
    return (logprob, entropy)


def solution(mesh):
    placed = (P("vocab", None), P(), P(None, "vocab"), P("vocab"), P(), P())
    return jax.shard_map(
        body, mesh=mesh, in_specs=placed, out_specs=(P("vocab"), P("vocab")), check_vma=False
    )
```

profile of v0, /device:TPU:2, one launch (start us, length us, event | category | flops | bytes accessed | tf_op | source)
XLA Modules:
  0.0 318.0 jit_solution(3615898307131070533)
XLA Ops:
  7.2 0.0 copy-start
  7.2 0.0 all-gather.2.cloned.1.call-start
  7.2 1.1 fusion.2
  8.4 1.6 fusion.4
  10.0 0.0 all-gather.2.cloned.1.call-update
  10.0 0.9 dynamic-update-slice
  10.9 79.1 %all-reduce = s32[4096]{0:T(1024)S(1)} all-reduce(s32[4096]{0:T(1024)S(1)} %dynamic-update-slice), channel_id=1, replica_groups=mesh['vocab'=256] {'vocab'}, use_global_device_ids=true, to_apply=%add | all-reduce | flops 4096 | bytes 32768
  90.0 1.4 select_reduce_fusion.2
  91.4 53.8 %all-gather.2.cloned.1.call-done = bf16[4096,2560]{1,0:T(8,128)(2,1)} async-done(((bf16[16,2560]{1,0:T(8,128)(2,1)}), bf16[4096,2560]{1,0:T(8,128)(2,1)}) %all-gather.2.cloned.1.call-update) | async-done | bytes 20971536 | tf_op jit(solution)/shard_map/all_gather | solution.py:34
  145.2 0.0 copy-done
  145.2 12.0 %fusion.7 = (f32[4096]{0:T(1024)S(1)}, f32[4096,288]{0,1:T(8,128)}) fusion(bf16[4096,2560]{1,0:T(8,128)(2,1)} %all-gather.2.cloned.1.call-done, bf16[2560,288]{0,1:T(8,128)(2,1)S(1)} %copy-done, pred[288]{0:T(512)(128)(4,1)S(1)} %broadcast_compare_fusion), kind=kOutput, calls=%fused_computation.20 | convolution fusion | flops 6043332608 | bytes 27181344 | tf_op jit(solution)/shard_map/dot_general | solution.py:14
  157.2 75.1 %pmax.7 = f32[4096]{0:T(1024)S(1)} all-reduce(f32[4096]{0:T(1024)S(1)} %get-tuple-element.12), channel_id=1, replica_groups=mesh['vocab'=256] {'vocab'}, use_global_device_ids=true, to_apply=%region_5.6 | all-reduce | flops 4096 | bytes 32768 | tf_op jit(solution)/shard_map/pmax | solution.py:43
  232.4 3.7 %select_reduce_fusion = (f32[4096]{0:T(1024)S(1)}, f32[4096]{0:T(1024)S(1)}, f32[4096]{0:T(1024)S(1)}) fusion(f32[4096,288]{0,1:T(8,128)} %get-tuple-element.13, f32[4096]{0:T(1024)S(1)} %get-tuple-element.12, pred[288]{0:T(512)(128)(4,1)S(1)} %broadcast_compare_fusion, s32[4096]{0:T(1024)S(1)} %all-reduce, s32[288]{0:T(512)S(1)} %iota_add_fusion), kind=kLoop, calls=%fused_computation.2 | loop fusion | flops 10604544 | bytes 4801952 | tf_op jit(solution)/shard_map/reduce_sum | solution.py:19
  236.1 73.8 %all-reduce.1 = (f32[4096]{0:T(1024)S(1)}, f32[4096]{0:T(1024)S(1)}, f32[4096]{0:T(1024)S(1)}) all-reduce(f32[4096]{0:T(1024)S(1)} %get-tuple-element.4, f32[4096]{0:T(1024)S(1)} %get-tuple-element.11, f32[4096]{0:T(1024)S(1)} %get-tuple-element.10), channel_id=1, replica_groups=mesh['vocab'=256] {'vocab'}, use_global_device_ids=true, to_apply=%region_3.4 | all-reduce | flops 12288 | bytes 98304 | tf_op jit(solution)/shard_map/psum | solution.py:45
  309.9 1.2 compare_select_fusion
  (5 shorter events, 0.0 us)
Async XLA Ops:
  7.2 138.1 %copy-start = (bf16[2560,288]{0,1:T(8,128)(2,1)S(1)}, bf16[2560,288]{0,1:T(8,128)(2,1)}, u32[]{:S(2)}) copy-start(bf16[2560,288]{0,1:T(8,128)(2,1)} %param.8) | copy-start | bytes 4423684
  7.2 138.0 %all-gather.2.cloned.1.call-start = ((), (), s32[]{:S(2)}) async-start(), calls=%async_computation | async-start | bytes 21053440 | tf_op jit(solution)/shard_map/all_gather | solution.py:34
Sparse Core Ops, SparseCore 0:
  11.6 133.5 all-gather.1
where the time goes:
time: 320 us; the launch traced here: 318 us
  blocking collectives  228 us (71%)
  waiting for transfers between devices  53.8 us (17%)
  between operations  14.1 us (4%)
  matrix products  12 us (4%)
  other arithmetic  9.06 us (3%)
    unnamed x1, blocking collectives  79.1 us
    pmax x1, blocking collectives, body(): top_full = lax.pmax(rowmax, 'vocab')  75.1 us
    psum x1, blocking collectives, body(): sums = lax.psum((total * factor, weighted * factor, picked), 'vocab')  73.8 us
    all_gather x1, waiting for transfers between devices, body(): lax.all_gather(normed, 'vocab', axis=0, tiled=True)  53.8 us
    dot_general x1, matrix products, slice_stats(): logits = jnp.dot(rows, head, preferred_element_type=jnp.float32) / 10.0  12 us
  transfers between devices with their start and end apart: 1, of which 1 were waited for; matrix products, arithmetic and copies ran while one was open for 1% of the time, Pallas kernels for 0%

commit v1 on v0

--- a/solution.py
+++ b/solution.py
@@ -8,6 +8,7 @@
 
 EPS = 1e-05
 NEG = -1e30
+DIGIT = 64
 
 
 def slice_stats(rows, chosen, head, col_index, real_cols):
@@ -21,30 +22,42 @@
     return (rowmax, total, weighted, picked)
 
 
+def code_ids(ids):
+    digits = [ids // (DIGIT * DIGIT), (ids // DIGIT) % DIGIT, ids % DIGIT]
+    return jnp.stack(digits, axis=1).astype(jnp.bfloat16)
+
+
+def decode_ids(coded):
+    d = coded.astype(jnp.int32)
+    return (d[:, 0] * DIGIT + d[:, 1]) * DIGIT + d[:, 2]
+
+
 def body(hidden, norm_gain, head, token_ids, req_len, req_owner):
-    local_rows = hidden.shape[0]
+    local_rows, width = hidden.shape
     columns = head.shape[1]
+    n_dev = lax.axis_size("vocab")
     me = lax.axis_index("vocab")
     values = hidden.astype(jnp.float32)
     scale = lax.rsqrt(jnp.mean(values * values, axis=-1, keepdims=True) + EPS)
     normed = (values * scale * norm_gain[None, :]).astype(jnp.bfloat16)
+    packed = jnp.concatenate([normed, code_ids(token_ids)], axis=1)
     col_index = me * columns + jnp.arange(columns, dtype=jnp.int32)
     real_cols = col_index < VOCAB_REAL
-    all_rows, all_ids = (
-        lax.all_gather(normed, "vocab", axis=0, tiled=True),
-        lax.all_gather(token_ids, "vocab", axis=0, tiled=True),
-    )
-    stats = slice_stats(all_rows, all_ids, head, col_index, real_cols)
-    rowmax, total, weighted, picked = stats
+    gathered = lax.all_gather(packed, "vocab", axis=0, tiled=True)
+    all_rows = gathered[:, :width]
+    all_ids = decode_ids(gathered[:, width:])
+    rowmax, total, weighted, picked = slice_stats(all_rows, all_ids, head, col_index, real_cols)
 
-    def own_part(whole):
-        return lax.dynamic_slice_in_dim(whole, me * local_rows, local_rows)
+    stats = jnp.stack([rowmax, total, weighted, picked], axis=0).reshape(4, n_dev, local_rows)
+    stats = jnp.transpose(stats, (1, 0, 2))
+    got = lax.all_to_all(stats, "vocab", 0, 0, tiled=True)
+    m_i, s_i, w_i, p_i = got[:, 0], got[:, 1], got[:, 2], got[:, 3]
+    top = jnp.max(m_i, axis=0)
+    factor = jnp.exp(m_i - top[None, :])
+    total_all = jnp.sum(s_i * factor, axis=0)
+    weighted_all = jnp.sum(w_i * factor, axis=0)
+    picked_all = jnp.sum(p_i, axis=0)
 
-    top_full = lax.pmax(rowmax, "vocab")
-    factor = jnp.exp(rowmax - top_full)
-    sums = lax.psum((total * factor, weighted * factor, picked), "vocab")
-    total_all, weighted_all, picked_all = [own_part(item) for item in sums]
-    top = own_part(top_full)
     load = jnp.sum(jnp.where(req_owner == me, req_len, 0))
     live = jnp.arange(local_rows, dtype=jnp.int32) < load
     log_total = jnp.log(total_all)

time: 320 us -> 206 us (0.64)
  blocking collectives: 228 us -> 0 us
  waiting for transfers between devices: 53.8 us -> 156 us
  starting transfers between devices: 0.04 us -> 8.85 us
    all_gather x1, waiting for transfers between devices: 53.8 us -> 136 us  [body(): gathered = lax.all_gather(packed, 'vocab', axis=0, tiled=True)]
    unnamed x1 -> x0, blocking collectives: 79.1 us -> none
    pmax x1 -> x0, blocking collectives: 75.1 us -> none  [body(): top_full = lax.pmax(rowmax, 'vocab')]
    psum x1 -> x0, blocking collectives: 73.8 us -> none  [body(): sums = lax.psum((total * factor, weighted * factor, picked), 'vocab')]
    all_to_all x0 -> x1, waiting for transfers between devices: none -> 19.4 us  [body(): got = lax.all_to_all(stats, 'vocab', 0, 0, tiled=True)]
    all_to_all x0 -> x1, starting transfers between devices: none -> 8.82 us  [body(): got = lax.all_to_all(stats, 'vocab', 0, 0, tiled=True)]
  transfers between devices with their start and end apart: 1 -> 2, of which waited for: 1 -> 2; matrix products, arithmetic and copies ran while one was open for 1% -> 0% of each run, Pallas kernels for 0% -> 0%
where the time goes in v1:
time: 206 us; the launch traced here: 205 us
  waiting for transfers between devices  156 us (76%)
  between operations  14.1 us (7%)
  other arithmetic  12.1 us (6%)
  matrix products  12 us (6%)
  starting transfers between devices  8.85 us (4%)
  local copies, waits for them, and re-layouts  2.52 us (1%)
    all_gather x1, waiting for transfers between devices, body(): gathered = lax.all_gather(packed, 'vocab', axis=0, tiled=True)  136 us
    all_to_all x1, waiting for transfers between devices, body(): got = lax.all_to_all(stats, 'vocab', 0, 0, tiled=True)  19.4 us
    dot_general x1, matrix products, slice_stats(): logits = jnp.dot(rows, head, preferred_element_type=jnp.float32) / 10.0  12 us
    all_to_all x1, starting transfers between devices, body(): got = lax.all_to_all(stats, 'vocab', 0, 0, tiled=True)  8.82 us
  transfers between devices with their start and end apart: 2, of which 2 were waited for; matrix products, arithmetic and copies ran while one was open for 0% of the time, Pallas kernels for 0%

profile of v1, /device:TPU:2, one launch (start us, length us, event | category | flops | bytes accessed | tf_op | source)
XLA Modules:
  0.0 205.2 jit_solution(8663673299165401494)
XLA Ops:
  7.2 0.0 copy-start
  7.2 0.0 all-gather.2.cloned.1.call-start
  7.2 0.8 fusion.17
  8.0 0.1 copy.24
  8.1 0.1 copy.25
  8.2 0.1 copy.26
  8.3 1.0 fusion.11
  9.3 1.0 fusion.13
  10.3 0.7 concatenate.5
  11.0 0.0 all-gather.2.cloned.1.call-update
  11.1 136.2 %all-gather.2.cloned.1.call-done = bf16[4096,2563]{1,0:T(8,128)(2,1)} async-done(((bf16[16,2563]{1,0:T(8,128)(2,1)}), bf16[4096,2563]{1,0:T(8,128)(2,1)}) %all-gather.2.cloned.1.call-update) | async-done | bytes 20996112 | tf_op jit(solution)/shard_map/all_gather | solution.py:46
  147.3 1.4 slice_convert_fusion
  148.8 1.7 fusion.9
  150.5 0.0 copy-done
  150.5 12.0 %fusion.20 = (f32[4096]{0:T(1024)S(1)}, f32[4096,288]{0,1:T(8,128)}) fusion(bf16[2560,288]{0,1:T(8,128)(2,1)S(1)} %copy-done, bf16[4096,2563]{1,0:T(8,128)(2,1)} %all-gather.2.cloned.1.call-done, pred[288]{0:T(512)(128)(4,1)S(1)} %broadcast_compare_fusion), kind=kOutput, calls=%fused_computation.49 | convolution fusion | flops 6043332608 | bytes 27181344 | tf_op jit(solution)/shard_map/dot_general | solution.py:15
  162.5 0.0 copy-start.1
  162.5 0.0 copy-start.2
  162.5 0.1 stack.32
  162.6 3.7 %fusion.8 = (f32[4096]{0:T(1024)S(1)}, f32[4096]{0:T(1024)S(1)}, f32[4096]{0:T(1024)S(1)}) fusion(f32[4096,288]{0,1:T(8,128)} %get-tuple-element.17, f32[4096]{0:T(1024)S(1)} %get-tuple-element.16, pred[288]{0:T(512)(128)(4,1)S(1)} %broadcast_compare_fusion, s32[4096]{0:T(1024)S(1)} %fusion.9, s32[288]{0:T(512)S(1)} %iota_add_fusion), kind=kLoop, calls=%fused_computation.7 | loop fusion | flops 10604544 | bytes 4801952 | tf_op jit(solution)/shard_map/reduce_sum | solution.py:19
  166.2 0.1 stack.33
  166.3 0.1 stack.34
  166.4 0.1 stack.35
  166.6 1.1 copy.27
  167.7 8.8 %all-to-all-start = ((f32[256,4,16]{2,1,0:T(4,128)}), f32[256,4,16]{2,1,0:T(4,128)S(1)}, u32[]{:S(2)}, u32[]{:S(2)}) async-start(f32[256,4,16]{2,1,0:T(4,128)} %copy.27), calls=%async_computation | async-start | bytes 1048576 | tf_op jit(solution)/shard_map/all_to_all | solution.py:53
  176.5 0.0 copy-done.1
  176.6 0.0 copy-done.2
  176.6 0.7 select_reduce_fusion.2
  177.3 19.4 %all-to-all-done = f32[256,4,16]{2,1,0:T(4,128)S(1)} async-done(((f32[256,4,16]{2,1,0:T(4,128)}), f32[256,4,16]{2,1,0:T(4,128)S(1)}, u32[]{:S(2)}, u32[]{:S(2)}) %all-to-all-start) | async-done | bytes 65568 | tf_op jit(solution)/shard_map/all_to_all | solution.py:53
  196.6 0.4 fusion.19
  197.0 0.1 reduce_max.19
  197.1 0.1 multiply_reduce_fusion
  197.2 1.2 compare_select_fusion.2
  (4 shorter events, 0.1 us)
Async XLA Ops:
  7.2 143.3 %copy-start = (bf16[2560,288]{0,1:T(8,128)(2,1)S(1)}, bf16[2560,288]{0,1:T(8,128)(2,1)}, u32[]{:S(2)}) copy-start(bf16[2560,288]{0,1:T(8,128)(2,1)} %param.8) | copy-start | bytes 4423684
  7.2 140.1 %all-gather.2.cloned.1.call-start = ((), (), s32[]{:S(2)}) async-start(), calls=%async_computation.1 | async-start | bytes 22106112 | tf_op jit(solution)/shard_map/all_gather | solution.py:46
  162.5 14.1 %copy-start.1 = (s32[512]{0:T(512)S(1)}, s32[512]{0:T(512)}, u32[]{:S(2)}) copy-start(s32[512]{0:T(512)} %param.10) | copy-start | bytes 6148
  162.5 14.1 %copy-start.2 = (s32[512]{0:T(512)S(1)}, s32[512]{0:T(512)}, u32[]{:S(2)}) copy-start(s32[512]{0:T(512)} %param.11) | copy-start | bytes 6148
  167.7 28.9 %all-to-all-start = ((f32[256,4,16]{2,1,0:T(4,128)}), f32[256,4,16]{2,1,0:T(4,128)S(1)}, u32[]{:S(2)}, u32[]{:S(2)}) async-start(f32[256,4,16]{2,1,0:T(4,128)} %copy.27), calls=%async_computation | async-start | bytes 1048576 | tf_op jit(solution)/shard_map/all_to_all | solution.py:53
Sparse Core Ops, SparseCore 0:
  11.9 135.4 all-gather.1

commit v2 on v1

--- a/solution.py
+++ b/solution.py
@@ -1,7 +1,7 @@
 import jax
 import jax.numpy as jnp
 from jax import lax
-from jax.sharding import PartitionSpec as P
+from jax.sharding import Mesh, PartitionSpec as P
 
 VOCAB_REAL = 73448
 
@@ -35,22 +35,24 @@
 def body(hidden, norm_gain, head, token_ids, req_len, req_owner):
     local_rows, width = hidden.shape
     columns = head.shape[1]
-    n_dev = lax.axis_size("vocab")
-    me = lax.axis_index("vocab")
+    chips = lax.axis_size("chip")
+    cores = lax.axis_size("core")
+    me = lax.axis_index("chip") * cores + lax.axis_index("core")
     values = hidden.astype(jnp.float32)
     scale = lax.rsqrt(jnp.mean(values * values, axis=-1, keepdims=True) + EPS)
     normed = (values * scale * norm_gain[None, :]).astype(jnp.bfloat16)
     packed = jnp.concatenate([normed, code_ids(token_ids)], axis=1)
     col_index = me * columns + jnp.arange(columns, dtype=jnp.int32)
     real_cols = col_index < VOCAB_REAL
-    gathered = lax.all_gather(packed, "vocab", axis=0, tiled=True)
+    by_chip = lax.all_gather(packed, "chip", axis=0, tiled=True)
+    gathered = lax.all_gather(by_chip, "core", axis=0, tiled=True)
     all_rows = gathered[:, :width]
     all_ids = decode_ids(gathered[:, width:])
     rowmax, total, weighted, picked = slice_stats(all_rows, all_ids, head, col_index, real_cols)
 
-    stats = jnp.stack([rowmax, total, weighted, picked], axis=0).reshape(4, n_dev, local_rows)
-    stats = jnp.transpose(stats, (1, 0, 2))
-    got = lax.all_to_all(stats, "vocab", 0, 0, tiled=True)
+    stats = jnp.stack([rowmax, total, weighted, picked], axis=0).reshape(4, cores, chips, local_rows)
+    stats = jnp.transpose(stats, (2, 1, 0, 3)).reshape(chips * cores, 4, local_rows)
+    got = lax.all_to_all(stats, ("chip", "core"), 0, 0, tiled=True)
     m_i, s_i, w_i, p_i = got[:, 0], got[:, 1], got[:, 2], got[:, 3]
     top = jnp.max(m_i, axis=0)
     factor = jnp.exp(m_i - top[None, :])
@@ -67,7 +69,9 @@
 
 
 def solution(mesh):
-    placed = (P("vocab", None), P(), P(None, "vocab"), P("vocab"), P(), P())
+    split = Mesh(mesh.devices.reshape(-1, 2), ("chip", "core"))
+    rows = ("chip", "core")
+    placed = (P(rows, None), P(), P(None, rows), P(rows), P(), P())
     return jax.shard_map(
-        body, mesh=mesh, in_specs=placed, out_specs=(P("vocab"), P("vocab")), check_vma=False
+        body, mesh=split, in_specs=placed, out_specs=(P(rows), P(rows)), check_vma=False
     )

time: 206 us -> 250 us (1.21)
  waiting for transfers between devices: 156 us -> 195 us
  starting transfers between devices: 8.85 us -> 13.1 us
    all_gather x1 -> x2, waiting for transfers between devices: 136 us -> 176 us  [the longest x1 134 us: body(): by_chip = lax.all_gather(packed, 'chip', axis=0, tiled=True)]
    all_to_all x1, starting transfers between devices: 8.82 us -> 13 us  [body(): got = lax.all_to_all(stats, ('chip', 'core'), 0, 0, tiled=True)]
  transfers between devices with their start and end apart: 2 -> 3, of which waited for: 2 -> 3; matrix products, arithmetic and copies ran while one was open for 0% -> 0% of each run, Pallas kernels for 0% -> 0%
where the time goes in v2:
time: 250 us; the launch traced here: 249 us
  waiting for transfers between devices  195 us (78%)
  between operations  14.2 us (6%)
  starting transfers between devices  13.1 us (5%)
  other arithmetic  12.1 us (5%)
  matrix products  12 us (5%)
  local copies, waits for them, and re-layouts  3.05 us (1%)
    all_gather x1, waiting for transfers between devices, body(): by_chip = lax.all_gather(packed, 'chip', axis=0, tiled=True)  134 us
    all_gather x1, waiting for transfers between devices, body(): gathered = lax.all_gather(by_chip, 'core', axis=0, tiled=True)  41.1 us
    all_to_all x1, waiting for transfers between devices, body(): got = lax.all_to_all(stats, ('chip', 'core'), 0, 0, tiled=True)  19.4 us
    all_to_all x1, starting transfers between devices, body(): got = lax.all_to_all(stats, ('chip', 'core'), 0, 0, tiled=True)  13 us
    dot_general x1, matrix products, slice_stats(): logits = jnp.dot(rows, head, preferred_element_type=jnp.float32) / 10.0  12 us
  transfers between devices with their start and end apart: 3, of which 3 were waited for; matrix products, arithmetic and copies ran while one was open for 0% of the time, Pallas kernels for 0%

profile of v2, /device:TPU:2, one launch (start us, length us, event | category | flops | bytes accessed | tf_op | source)
XLA Modules:
  0.0 249.4 jit_solution(5600415826657068683)
XLA Ops:
  7.2 0.0 all-gather.3.cloned.1.call-start
  7.2 0.8 fusion.17
  8.0 0.1 copy.17
  8.1 0.1 copy.18
  8.2 0.1 copy.19
  8.3 1.0 fusion.11
  9.3 1.0 fusion.13
  10.3 0.7 concatenate.5
  11.0 0.0 all-gather.5.cloned.1.call-start
  11.1 134.5 %all-gather.3.cloned.1.call-done = bf16[2048,2563]{1,0:T(8,128)(2,1)} async-done(((bf16[16,2563]{1,0:T(8,128)(2,1)}), bf16[2048,2563]{1,0:T(8,128)(2,1)}) %all-gather.3.cloned.1.call-update) | async-done | bytes 10498064 | tf_op jit(solution)/shard_map/all_gather | solution.py:47
  145.6 41.1 %all-gather.5.cloned.1.call-done = bf16[4096,2563]{1,0:T(8,128)(2,1)} async-done(((bf16[2048,2563]{1,0:T(8,128)(2,1)}), bf16[4096,2563]{1,0:T(8,128)(2,1)}) %all-gather.5.cloned.1.call-update) | async-done | bytes 20996112 | tf_op jit(solution)/shard_map/all_gather | solution.py:48
  186.7 1.4 slice_convert_fusion
  188.2 1.7 fusion.9
  189.9 12.0 %fusion.20 = (f32[4096]{0:T(1024)S(1)}, f32[4096,288]{0,1:T(8,128)}) fusion(bf16[2560,288]{0,1:T(8,128)(2,1)S(1)} %copy-done, bf16[4096,2563]{1,0:T(8,128)(2,1)} %all-gather.5.cloned.1.call-done, pred[288]{0:T(512)(128)(4,1)S(1)} %broadcast_compare_fusion), kind=kOutput, calls=%fused_computation.49 | convolution fusion | flops 6043332608 | bytes 27181344 | tf_op jit(solution)/shard_map/dot_general | solution.py:15
  201.9 0.1 stack.32
  202.0 3.7 %fusion.8 = (f32[4096]{0:T(1024)S(1)}, f32[4096]{0:T(1024)S(1)}, f32[4096]{0:T(1024)S(1)}) fusion(f32[4096,288]{0,1:T(8,128)} %get-tuple-element.17, f32[4096]{0:T(1024)S(1)} %get-tuple-element.16, pred[288]{0:T(512)(128)(4,1)S(1)} %broadcast_compare_fusion, s32[4096]{0:T(1024)S(1)} %fusion.9, s32[288]{0:T(512)S(1)} %iota_add_fusion), kind=kLoop, calls=%fused_computation.7 | loop fusion | flops 10604544 | bytes 4801952 | tf_op jit(solution)/shard_map/reduce_sum | solution.py:19
  205.7 0.1 stack.33
  205.8 0.1 copy.21
  205.8 0.1 stack.34
  205.9 0.1 copy.22
  206.0 0.1 stack.35
  206.1 0.1 copy.23
  206.2 0.1 copy.20
  206.2 0.3 copy.24
  206.5 1.1 copy.25
  207.7 13.0 %all-to-all-start = ((f32[256,4,16]{2,1,0:T(4,128)}), f32[256,4,16]{2,1,0:T(4,128)S(1)}, u32[]{:S(2)}, u32[]{:S(2)}) async-start(f32[256,4,16]{2,1,0:T(4,128)} %copy.25), calls=%async_computation | async-start | bytes 1048576 | tf_op jit(solution)/shard_map/all_to_all | solution.py:55
  220.7 0.7 select_reduce_fusion.2
  221.4 19.4 %all-to-all-done = f32[256,4,16]{2,1,0:T(4,128)S(1)} async-done(((f32[256,4,16]{2,1,0:T(4,128)}), f32[256,4,16]{2,1,0:T(4,128)S(1)}, u32[]{:S(2)}, u32[]{:S(2)}) %all-to-all-start) | async-done | bytes 65568 | tf_op jit(solution)/shard_map/all_to_all | solution.py:55
  240.8 0.4 fusion.19
  241.2 0.1 reduce_max.19
  241.3 0.1 multiply_reduce_fusion
  241.3 1.2 compare_select_fusion.2
  (12 shorter events, 0.1 us)
Async XLA Ops:
  7.2 182.7 %copy-start = (bf16[2560,288]{0,1:T(8,128)(2,1)S(1)}, bf16[2560,288]{0,1:T(8,128)(2,1)}, u32[]{:S(2)}) copy-start(bf16[2560,288]{0,1:T(8,128)(2,1)} %param.8) | copy-start | bytes 4423684
  7.2 138.4 %all-gather.3.cloned.1.call-start = ((), (), s32[]{:S(2)}) async-start(), calls=%async_computation.1 | async-start | bytes 11096064 | tf_op jit(solution)/shard_map/all_gather | solution.py:47
  11.0 175.7 %all-gather.5.cloned.1.call-start = ((), (), s32[]{:S(2)}) async-start(), calls=%async_computation.2 | async-start | bytes 33030144 | tf_op jit(solution)/shard_map/all_gather | solution.py:48
  201.9 18.8 %copy-start.1 = (s32[512]{0:T(512)S(1)}, s32[512]{0:T(512)}, u32[]{:S(2)}) copy-start(s32[512]{0:T(512)} %param.10) | copy-start | bytes 6148
  201.9 18.8 %copy-start.2 = (s32[512]{0:T(512)S(1)}, s32[512]{0:T(512)}, u32[]{:S(2)}) copy-start(s32[512]{0:T(512)} %param.11) | copy-start | bytes 6148
  207.7 33.1 %all-to-all-start = ((f32[256,4,16]{2,1,0:T(4,128)}), f32[256,4,16]{2,1,0:T(4,128)S(1)}, u32[]{:S(2)}, u32[]{:S(2)}) async-start(f32[256,4,16]{2,1,0:T(4,128)} %copy.25), calls=%async_computation | async-start | bytes 1048576 | tf_op jit(solution)/shard_map/all_to_all | solution.py:55
Sparse Core Ops, SparseCore 0:
  11.7 133.8 all-gather.2
  147.4 39.2 all-gather.4

commit v3 on v1

--- a/solution.py
+++ b/solution.py
@@ -1,7 +1,11 @@
+import functools
+
 import jax
 import jax.numpy as jnp
 from jax import lax
-from jax.sharding import PartitionSpec as P
+from jax.experimental import pallas as pl
+from jax.experimental.pallas import tpu as pltpu
+from jax.sharding import Mesh, PartitionSpec as P
 
 VOCAB_REAL = 73448
 
@@ -9,6 +13,8 @@
 EPS = 1e-05
 NEG = -1e30
 DIGIT = 64
+AXES = ("z", "x", "y", "core")
+CHIP_AXES = ("z", "x", "y")
 
 
 def slice_stats(rows, chosen, head, col_index, real_cols):
@@ -32,25 +38,139 @@
     return (d[:, 0] * DIGIT + d[:, 1]) * DIGIT + d[:, 2]
 
 
+STREAMS = (("z", "x", "y"), ("x", "y", "z"), ("y", "z", "x"))
+LANES = 128
+
+
+def gather_kernel(sizes, spans, x_ref, g_ref, send_sem, recv_sem, own_sem):
+    pos = {a: lax.axis_index(a) for a in AXES}
+    core = pos["core"]
+
+    def peer(axis, k):
+        at = dict(pos)
+        at[axis] = lax.rem(pos[axis] + k, sizes[axis])
+        return tuple(at[a] for a in AXES)
+
+    def view(ref, held, axis_at, cols):
+        idx = []
+        for a in ("y", "x", "z"):
+            if a in held:
+                idx.append(slice(None))
+            elif a in axis_at:
+                idx.append(axis_at[a])
+            else:
+                idx.append(pos[a])
+        return ref.at[tuple(idx) + (slice(None), cols)]
+
+    barrier = pltpu.get_barrier_semaphore()
+    count = 0
+    for axis in CHIP_AXES:
+        for k in range(1, sizes[axis]):
+            pl.semaphore_signal(barrier, inc=1, device_id=peer(axis, k), device_id_type=pl.DeviceIdType.MESH)
+            count += 1
+    pl.semaphore_wait(barrier, count)
+
+    own = pltpu.make_async_copy(x_ref, g_ref.at[pos["y"], pos["x"], pos["z"]], own_sem)
+    own.start()
+    sends = []
+    for t in range(3):
+        for s, order in enumerate(STREAMS):
+            cols = pl.ds(spans[s][0], spans[s][1])
+            axis = order[t]
+            n = sizes[axis]
+            held = order[:t]
+            if t > 0:
+                prev = order[t - 1]
+                for j in range(1, sizes[prev]):
+                    src_at = {prev: lax.rem(pos[prev] + j, sizes[prev])}
+                    slot = view(g_ref, order[:t - 1], src_at, cols)
+                    pltpu.make_async_remote_copy(
+                        src_ref=slot, dst_ref=slot, send_sem=send_sem.at[s, t - 1, j],
+                        recv_sem=recv_sem.at[s, t - 1, j], device_id=peer(prev, j),
+                        device_id_type=pl.DeviceIdType.MESH,
+                    ).wait_recv()
+                if t == 1 and s == 0:
+                    own.wait()
+            src = x_ref.at[:, cols] if t == 0 else view(g_ref, held, {}, cols)
+            dst = view(g_ref, held, {}, cols)
+            for k in range(1, n):
+                copy = pltpu.make_async_remote_copy(
+                    src_ref=src, dst_ref=dst, send_sem=send_sem.at[s, t, k],
+                    recv_sem=recv_sem.at[s, t, (n - k) % n], device_id=peer(axis, k),
+                    device_id_type=pl.DeviceIdType.MESH,
+                )
+                copy.start()
+                sends.append(copy)
+    for s, order in enumerate(STREAMS):
+        cols = pl.ds(spans[s][0], spans[s][1])
+        last = order[2]
+        for j in range(1, sizes[last]):
+            slot = view(g_ref, order[:2], {last: lax.rem(pos[last] + j, sizes[last])}, cols)
+            pltpu.make_async_remote_copy(
+                src_ref=slot, dst_ref=slot, send_sem=send_sem.at[s, 2, j],
+                recv_sem=recv_sem.at[s, 2, j], device_id=peer(last, j),
+                device_id_type=pl.DeviceIdType.MESH,
+            ).wait_recv()
+    for copy in sends:
+        copy.wait_send()
+
+
+def gather_rows(packed, sizes):
+    rows, width = packed.shape
+    tiles = width // LANES
+    part = tiles * 3 // 7
+    counts = [part, tiles - 2 * part, part]
+    spans, at = [], 0
+    for c in counts:
+        spans.append((at * LANES, c * LANES))
+        at += c
+    shape = (sizes["y"], sizes["x"], sizes["z"], rows, width)
+    longest = max(sizes[a] for a in CHIP_AXES)
+    return pl.pallas_call(
+        functools.partial(gather_kernel, sizes, spans),
+        out_shape=jax.ShapeDtypeStruct(shape, packed.dtype),
+        in_specs=[pl.BlockSpec(memory_space=pl.ANY)],
+        out_specs=pl.BlockSpec(memory_space=pl.ANY),
+        scratch_shapes=[
+            pltpu.SemaphoreType.DMA((3, 3, longest)),
+            pltpu.SemaphoreType.DMA((3, 3, longest)),
+            pltpu.SemaphoreType.DMA(()),
+        ],
+        compiler_params=pltpu.CompilerParams(collective_id=0, has_side_effects=True),
+    )(packed)
+
+
 def body(hidden, norm_gain, head, token_ids, req_len, req_owner):
     local_rows, width = hidden.shape
     columns = head.shape[1]
-    n_dev = lax.axis_size("vocab")
-    me = lax.axis_index("vocab")
+    size = {a: lax.axis_size(a) for a in AXES}
+    pos = {a: lax.axis_index(a) for a in AXES}
+    chip = (pos["z"] * size["x"] + pos["x"]) * size["y"] + pos["y"]
+    core = pos["core"]
+    me = chip * size["core"] + core
+
     values = hidden.astype(jnp.float32)
     scale = lax.rsqrt(jnp.mean(values * values, axis=-1, keepdims=True) + EPS)
     normed = (values * scale * norm_gain[None, :]).astype(jnp.bfloat16)
-    packed = jnp.concatenate([normed, code_ids(token_ids)], axis=1)
-    col_index = me * columns + jnp.arange(columns, dtype=jnp.int32)
+    coded = code_ids(token_ids)
+    pad = jnp.zeros((local_rows, LANES - coded.shape[1]), jnp.bfloat16)
+    packed = jnp.concatenate([normed, coded, pad], axis=1)
+
+    other = lax.ppermute(head, "core", [(0, 1), (1, 0)])
+    chip_head = jnp.where(core == 0, jnp.concatenate([head, other], axis=1), jnp.concatenate([other, head], axis=1))
+    col_index = chip * (2 * columns) + jnp.arange(2 * columns, dtype=jnp.int32)
     real_cols = col_index < VOCAB_REAL
-    gathered = lax.all_gather(packed, "vocab", axis=0, tiled=True)
+
+    gathered = gather_rows(packed, size).reshape(-1, packed.shape[1])
     all_rows = gathered[:, :width]
-    all_ids = decode_ids(gathered[:, width:])
-    rowmax, total, weighted, picked = slice_stats(all_rows, all_ids, head, col_index, real_cols)
+    all_ids = decode_ids(gathered[:, width:width + 3])
+    stats = jnp.stack(slice_stats(all_rows, all_ids, chip_head, col_index, real_cols), axis=0)
 
-    stats = jnp.stack([rowmax, total, weighted, picked], axis=0).reshape(4, n_dev, local_rows)
-    stats = jnp.transpose(stats, (1, 0, 2))
-    got = lax.all_to_all(stats, "vocab", 0, 0, tiled=True)
+    stats = stats.reshape(4, size["y"], size["x"], size["z"], local_rows)
+    chips = size["z"] * size["x"] * size["y"]
+    send = jnp.transpose(stats, (3, 2, 1, 0, 4)).reshape(chips, 4, local_rows)
+    got = lax.all_to_all(send, CHIP_AXES, 0, 0, tiled=True)
+
     m_i, s_i, w_i, p_i = got[:, 0], got[:, 1], got[:, 2], got[:, 3]
     top = jnp.max(m_i, axis=0)
     factor = jnp.exp(m_i - top[None, :])
@@ -67,7 +187,8 @@
 
 
 def solution(mesh):
-    placed = (P("vocab", None), P(), P(None, "vocab"), P("vocab"), P(), P())
+    split = Mesh(mesh.devices.reshape(8, 4, 4, 2), AXES)
+    placed = (P(AXES, None), P(), P(None, AXES), P(AXES), P(), P())
     return jax.shard_map(
-        body, mesh=mesh, in_specs=placed, out_specs=(P("vocab"), P("vocab")), check_vma=False
+        body, mesh=split, in_specs=placed, out_specs=(P(AXES), P(AXES)), check_vma=False
     )

time: 206 us -> 150 us (0.73)
  waiting for transfers between devices: 156 us -> 12.5 us
  Pallas kernels: 0 us -> 96.6 us
  between operations: 14.1 us -> 0.81 us
  starting transfers between devices: 8.85 us -> 14.5 us
  other arithmetic: 12.1 us -> 8.78 us
    all_gather x1 -> x0, waiting for transfers between devices: 136 us -> none  [body(): gathered = lax.all_gather(packed, 'vocab', axis=0, tiled=True)]
    pallas_call x0 -> x1, Pallas kernels: none -> 96.6 us  [gather_rows(): pl.pallas_call(functools.partial(gather_kernel, sizes, spans), out_shape=...]
    all_to_all x1, waiting for transfers between devices: 19.4 us -> 12.5 us  [body(): got = lax.all_to_all(send, CHIP_AXES, 0, 0, tiled=True)]
    all_to_all x1, starting transfers between devices: 8.82 us -> 14.4 us  [body(): got = lax.all_to_all(send, CHIP_AXES, 0, 0, tiled=True)]
  transfers between devices with their start and end apart: 2 -> 2, of which waited for: 2 -> 1; matrix products, arithmetic and copies ran while one was open for 0% -> 4% of each run, Pallas kernels for 0% -> 65%
where the time goes in v3:
time: 150 us; the launch traced here: 149 us
  Pallas kernels  96.6 us (64%)
  starting transfers between devices  14.5 us (10%)
  waiting for transfers between devices  12.5 us (8%)
  matrix products  12.5 us (8%)
  other arithmetic  8.78 us (6%)
  local copies, waits for them, and re-layouts  3.65 us (2%)
    pallas_call x1, Pallas kernels, gather_rows(): pl.pallas_call(functools.partial(gather_kernel, sizes, spans), out_shape=...  96.6 us
    all_to_all x1, starting transfers between devices, body(): got = lax.all_to_all(send, CHIP_AXES, 0, 0, tiled=True)  14.4 us
    dot_general x1, matrix products, slice_stats(): logits = jnp.dot(rows, head, preferred_element_type=jnp.float32) / 10.0  12.5 us
    all_to_all x1, waiting for transfers between devices, body(): got = lax.all_to_all(send, CHIP_AXES, 0, 0, tiled=True)  12.5 us
    reduce_sum x1, other arithmetic, slice_stats(): total = jnp.sum(expo, axis=1)  3.88 us
  transfers between devices with their start and end apart: 2, of which 1 were waited for; matrix products, arithmetic and copies ran while one was open for 4% of the time, Pallas kernels for 65%

profile of v3, /device:TPU:2, one launch (start us, length us, event | category | flops | bytes accessed | tf_op | source)
XLA Modules:
  0.0 149.3 jit_solution(4717889388947681430)
XLA Ops:
  0.6 0.1 collective-permute-start
  0.7 0.7 fusion.18
  1.4 0.1 copy.22
  1.5 0.1 copy.23
  1.6 0.1 copy.24
  1.7 1.0 fusion.11
  2.7 1.0 fusion.13
  3.7 0.7 concatenate.11.x_ref
  4.4 0.0 copy-start.2
  4.5 96.6 %shard_map.77 = bf16[4,4,8,16,2688]{4,3,2,1,0:T(8,128)(2,1)} custom-call(bf16[16,2688]{1,0:T(8,128)(2,1)} %concatenate.11.x_ref), custom_call_target="tpu_custom_call" | custom-call | tf_op jit(solution)/shard_map/pallas_call | solution.py:129
  101.1 1.1 slice.37
  102.2 0.2 copy.30
  102.5 0.0 collective-permute-done
  102.5 0.0 copy-done.2
  102.5 12.5 %fusion.22 = (f32[2048]{0:T(1024)S(1)}, f32[2048,576]{0,1:T(8,128)}) fusion(bf16[2560,288]{0,1:T(8,128)(2,1)S(1)} %collective-permute-done, bf16[2560,288]{0,1:T(8,128)(2,1)S(1)} %copy-done.2, pred[]{:T(512)S(6)} %eq.29, bf16[2048,2688]{1,0:T(8,128)(2,1)} %bitcast.19, pred[576]{0:T(1024)(128)(4,1)S(1)} %broadcast_compare_fusion), kind=kOutput, calls=%fused_computation.54 | convolution fusion | flops 6056605696 | bytes 18162240 | tf_op jit(solution)/shard_map/dot_general | solution.py:21
  115.0 0.0 copy-start
  115.1 0.0 copy-start.1
  115.1 0.1 stack.32
  115.1 3.9 %fusion.2 = (f32[2048]{0:T(1024)S(1)}, f32[2048]{0:T(1024)S(1)}, f32[2048]{0:T(1024)S(1)}) fusion(f32[2048,576]{0,1:T(8,128)} %get-tuple-element.17, f32[2048]{0:T(1024)S(1)} %get-tuple-element.16, pred[576]{0:T(1024)(128)(4,1)S(1)} %broadcast_compare_fusion, s32[2048]{0:T(1024)S(1)} %bitcast.25, s32[576]{0:T(1024)S(1)} %iota_add_fusion), kind=kLoop, calls=%fused_computation.5 | loop fusion | flops 10610688 | bytes 4762432 | tf_op jit(solution)/shard_map/reduce_sum | solution.py:25
  119.0 0.1 stack.33
  119.1 0.1 stack.34
  119.2 0.1 stack.35
  119.3 0.2 copy.26
  119.5 0.9 copy.27
  120.4 14.4 %all-to-all-start = ((f32[128,4,16]{2,1,0:T(4,128)}), f32[128,4,16]{2,1,0:T(4,128)S(1)}, u32[]{:S(2)}, u32[]{:S(2)}) async-start(f32[128,4,16]{2,1,0:T(4,128)} %copy.27), calls=%async_computation | async-start | bytes 524288 | tf_op jit(solution)/shard_map/all_to_all | solution.py:172
  134.7 0.0 copy-done
  134.7 0.0 copy-done.1
  134.7 0.7 select_reduce_fusion.2
  135.4 12.5 %all-to-all-done = f32[128,4,16]{2,1,0:T(4,128)S(1)} async-done(((f32[128,4,16]{2,1,0:T(4,128)}), f32[128,4,16]{2,1,0:T(4,128)S(1)}, u32[]{:S(2)}, u32[]{:S(2)}) %all-to-all-start) | async-done | bytes 32800 | tf_op jit(solution)/shard_map/all_to_all | solution.py:172
  147.9 0.2 fusion.21
  148.2 1.1 compare_select_fusion.2
  (9 shorter events, 0.2 us)
Async XLA Ops:
  0.6 101.9 %collective-permute-start = (bf16[2560,288]{0,1:T(8,128)(2,1)}, bf16[2560,288]{0,1:T(8,128)(2,1)S(1)}, u32[]{:S(2)}, u32[]{:S(2)}) collective-permute-start(bf16[2560,288]{0,1:T(8,128)(2,1)} %param.8), channel_id=1, source_target_pairs={{0,1},{1,0},{2,3},{3,2},{4,5},{5,4},{6,7},{7,6},{8,9},{9,8},{10,11... | collective-permute-start | bytes 4423688 | tf_op jit(solution)/shard_map/ppermute | solution.py:159
  4.4 98.1 %copy-start.2 = (bf16[2560,288]{0,1:T(8,128)(2,1)S(1)}, bf16[2560,288]{0,1:T(8,128)(2,1)}, u32[]{:S(2)}) copy-start(bf16[2560,288]{0,1:T(8,128)(2,1)} %param.8) | copy-start | bytes 4423684
  115.0 19.7 %copy-start = (s32[512]{0:T(512)S(1)}, s32[512]{0:T(512)}, u32[]{:S(2)}) copy-start(s32[512]{0:T(512)} %param.10) | copy-start | bytes 6148
  115.1 19.7 %copy-start.1 = (s32[512]{0:T(512)S(1)}, s32[512]{0:T(512)}, u32[]{:S(2)}) copy-start(s32[512]{0:T(512)} %param.11) | copy-start | bytes 6148
  120.4 27.6 %all-to-all-start = ((f32[128,4,16]{2,1,0:T(4,128)}), f32[128,4,16]{2,1,0:T(4,128)S(1)}, u32[]{:S(2)}, u32[]{:S(2)}) async-start(f32[128,4,16]{2,1,0:T(4,128)} %copy.27), calls=%async_computation | async-start | bytes 524288 | tf_op jit(solution)/shard_map/all_to_all | solution.py:172

commit v4 on v3

--- a/solution.py
+++ b/solution.py
@@ -44,20 +44,19 @@
 
 def gather_kernel(sizes, spans, x_ref, g_ref, send_sem, recv_sem, own_sem):
     pos = {a: lax.axis_index(a) for a in AXES}
-    core = pos["core"]
 
     def peer(axis, k):
         at = dict(pos)
-        at[axis] = lax.rem(pos[axis] + k, sizes[axis])
+        at[axis] = lax.rem(pos[axis] + k + sizes[axis], sizes[axis])
         return tuple(at[a] for a in AXES)
 
-    def view(ref, held, axis_at, cols):
+    def view(ref, held, axis, k, cols):
         idx = []
         for a in ("y", "x", "z"):
             if a in held:
                 idx.append(slice(None))
-            elif a in axis_at:
-                idx.append(axis_at[a])
+            elif a == axis:
+                idx.append(lax.rem(pos[a] + k + sizes[a], sizes[a]))
             else:
                 idx.append(pos[a])
         return ref.at[tuple(idx) + (slice(None), cols)]
@@ -65,52 +64,67 @@
     barrier = pltpu.get_barrier_semaphore()
     count = 0
     for axis in CHIP_AXES:
-        for k in range(1, sizes[axis]):
+        for k in (1, -1):
             pl.semaphore_signal(barrier, inc=1, device_id=peer(axis, k), device_id_type=pl.DeviceIdType.MESH)
             count += 1
     pl.semaphore_wait(barrier, count)
 
     own = pltpu.make_async_copy(x_ref, g_ref.at[pos["y"], pos["x"], pos["z"]], own_sem)
     own.start()
+
+    plans = []
+    for order in STREAMS:
+        plan = []
+        for t, axis in enumerate(order):
+            n = sizes[axis]
+            for q in range(1, n // 2 + 1):
+                plan.append((t, axis, q, n % 2 == 0 and q == n // 2))
+        plans.append(plan)
+
+    def step_copies(s, step, sending):
+        t, axis, q, split = plans[s][step]
+        c0, w = spans[s]
+        order = STREAMS[s]
+        held = order[:t]
+        if split:
+            cut = (w // LANES // 2) * LANES
+            col_of = [pl.ds(c0, cut), pl.ds(c0 + cut, w - cut)]
+        else:
+            col_of = [pl.ds(c0, w), pl.ds(c0, w)]
+        out = []
+        for d, sign in enumerate((1, -1)):
+            cols = col_of[d]
+            if sending:
+                k = -sign * (q - 1)
+                dst = view(g_ref, held, axis, k, cols)
+                src = x_ref.at[:, cols] if (t == 0 and q == 1) else dst
+                target = peer(axis, sign)
+            else:
+                k = -sign * q
+                src = dst = view(g_ref, held, axis, k, cols)
+                target = peer(axis, -sign)
+            out.append(pltpu.make_async_remote_copy(
+                src_ref=src, dst_ref=dst, send_sem=send_sem.at[s, step, d],
+                recv_sem=recv_sem.at[s, step, d], device_id=target,
+                device_id_type=pl.DeviceIdType.MESH,
+            ))
+        return out
+
+    steps = len(plans[0])
     sends = []
-    for t in range(3):
-        for s, order in enumerate(STREAMS):
-            cols = pl.ds(spans[s][0], spans[s][1])
-            axis = order[t]
-            n = sizes[axis]
-            held = order[:t]
-            if t > 0:
-                prev = order[t - 1]
-                for j in range(1, sizes[prev]):
-                    src_at = {prev: lax.rem(pos[prev] + j, sizes[prev])}
-                    slot = view(g_ref, order[:t - 1], src_at, cols)
-                    pltpu.make_async_remote_copy(
-                        src_ref=slot, dst_ref=slot, send_sem=send_sem.at[s, t - 1, j],
-                        recv_sem=recv_sem.at[s, t - 1, j], device_id=peer(prev, j),
-                        device_id_type=pl.DeviceIdType.MESH,
-                    ).wait_recv()
-                if t == 1 and s == 0:
-                    own.wait()
-            src = x_ref.at[:, cols] if t == 0 else view(g_ref, held, {}, cols)
-            dst = view(g_ref, held, {}, cols)
-            for k in range(1, n):
-                copy = pltpu.make_async_remote_copy(
-                    src_ref=src, dst_ref=dst, send_sem=send_sem.at[s, t, k],
-                    recv_sem=recv_sem.at[s, t, (n - k) % n], device_id=peer(axis, k),
-                    device_id_type=pl.DeviceIdType.MESH,
-                )
+    for g in range(steps):
+        for s in range(len(STREAMS)):
+            if g > 0:
+                for copy in step_copies(s, g - 1, False):
+                    copy.wait_recv()
+            if g == 1 and s == 0:
+                own.wait()
+            for copy in step_copies(s, g, True):
                 copy.start()
                 sends.append(copy)
-    for s, order in enumerate(STREAMS):
-        cols = pl.ds(spans[s][0], spans[s][1])
-        last = order[2]
-        for j in range(1, sizes[last]):
-            slot = view(g_ref, order[:2], {last: lax.rem(pos[last] + j, sizes[last])}, cols)
-            pltpu.make_async_remote_copy(
-                src_ref=slot, dst_ref=slot, send_sem=send_sem.at[s, 2, j],
-                recv_sem=recv_sem.at[s, 2, j], device_id=peer(last, j),
-                device_id_type=pl.DeviceIdType.MESH,
-            ).wait_recv()
+    for s in range(len(STREAMS)):
+        for copy in step_copies(s, steps - 1, False):
+            copy.wait_recv()
     for copy in sends:
         copy.wait_send()
 
@@ -118,22 +132,22 @@
 def gather_rows(packed, sizes):
     rows, width = packed.shape
     tiles = width // LANES
-    part = tiles * 3 // 7
-    counts = [part, tiles - 2 * part, part]
+    counts = [tiles * 8 // 21, tiles * 6 // 21]
+    counts.append(tiles - sum(counts))
     spans, at = [], 0
     for c in counts:
         spans.append((at * LANES, c * LANES))
         at += c
     shape = (sizes["y"], sizes["x"], sizes["z"], rows, width)
-    longest = max(sizes[a] for a in CHIP_AXES)
+    steps = sum(sizes[a] // 2 for a in CHIP_AXES)
     return pl.pallas_call(
         functools.partial(gather_kernel, sizes, spans),
         out_shape=jax.ShapeDtypeStruct(shape, packed.dtype),
         in_specs=[pl.BlockSpec(memory_space=pl.ANY)],
         out_specs=pl.BlockSpec(memory_space=pl.ANY),
         scratch_shapes=[
-            pltpu.SemaphoreType.DMA((3, 3, longest)),
-            pltpu.SemaphoreType.DMA((3, 3, longest)),
+            pltpu.SemaphoreType.DMA((3, steps, 2)),
+            pltpu.SemaphoreType.DMA((3, steps, 2)),
             pltpu.SemaphoreType.DMA(()),
         ],
         compiler_params=pltpu.CompilerParams(collective_id=0, has_side_effects=True),

time: 150 us -> 126 us (0.84)
  Pallas kernels: 96.6 us -> 77.4 us
  starting transfers between devices: 14.5 us -> 10 us
    pallas_call x1, Pallas kernels: 96.6 us -> 77.4 us  [gather_rows(): pl.pallas_call(functools.partial(gather_kernel, sizes, spans), out_shape=...]
    all_to_all x1, starting transfers between devices: 14.4 us -> 9.9 us  [body(): got = lax.all_to_all(send, CHIP_AXES, 0, 0, tiled=True)]
  transfers between devices with their start and end apart: 2 -> 2, of which waited for: 1 -> 1; matrix products, arithmetic and copies ran while one was open for 4% -> 5% of each run, Pallas kernels for 65% -> 62%
where the time goes in v4:
time: 126 us
  Pallas kernels  77.4 us (61%)
  waiting for transfers between devices  12.5 us (10%)
  matrix products  12.5 us (10%)
  starting transfers between devices  10 us (8%)
  other arithmetic  8.78 us (7%)
  local copies, waits for them, and re-layouts  3.65 us (3%)
    pallas_call x1, Pallas kernels, gather_rows(): pl.pallas_call(functools.partial(gather_kernel, sizes, spans), out_shape=...  77.4 us
    dot_general x1, matrix products, slice_stats(): logits = jnp.dot(rows, head, preferred_element_type=jnp.float32) / 10.0  12.5 us
    all_to_all x1, waiting for transfers between devices, body(): got = lax.all_to_all(send, CHIP_AXES, 0, 0, tiled=True)  12.5 us
    all_to_all x1, starting transfers between devices, body(): got = lax.all_to_all(send, CHIP_AXES, 0, 0, tiled=True)  9.9 us
    reduce_sum x1, other arithmetic, slice_stats(): total = jnp.sum(expo, axis=1)  3.88 us
  transfers between devices with their start and end apart: 2, of which 1 were waited for; matrix products, arithmetic and copies ran while one was open for 5% of the time, Pallas kernels for 62%

profile of v4, /device:TPU:2, one launch (start us, length us, event | category | flops | bytes accessed | tf_op | source)
XLA Modules:
  0.0 125.6 jit_solution(13480952485970678305)
XLA Ops:
  0.6 0.1 collective-permute-start
  0.7 0.7 fusion.18
  1.4 0.1 copy.22
  1.5 0.1 copy.23
  1.6 0.1 copy.24
  1.7 1.0 fusion.11
  2.7 1.0 fusion.13
  3.7 0.7 concatenate.11.x_ref
  4.4 0.0 copy-start.2
  4.5 77.4 %shard_map.77 = bf16[4,4,8,16,2688]{4,3,2,1,0:T(8,128)(2,1)} custom-call(bf16[16,2688]{1,0:T(8,128)(2,1)} %concatenate.11.x_ref), custom_call_target="tpu_custom_call" | custom-call | tf_op jit(solution)/shard_map/pallas_call | solution.py:143
  81.8 1.1 slice.37
  82.9 0.2 copy.30
  83.2 0.0 collective-permute-done
  83.2 0.0 copy-done.2
  83.3 12.5 %fusion.22 = (f32[2048]{0:T(1024)S(1)}, f32[2048,576]{0,1:T(8,128)}) fusion(bf16[2560,288]{0,1:T(8,128)(2,1)S(1)} %collective-permute-done, bf16[2560,288]{0,1:T(8,128)(2,1)S(1)} %copy-done.2, pred[]{:T(512)S(6)} %eq.29, bf16[2048,2688]{1,0:T(8,128)(2,1)} %bitcast.19, pred[576]{0:T(1024)(128)(4,1)S(1)} %broadcast_compare_fusion), kind=kOutput, calls=%fused_computation.54 | convolution fusion | flops 6056605696 | bytes 18162240 | tf_op jit(solution)/shard_map/dot_general | solution.py:21
  95.8 0.0 copy-start
  95.8 0.0 copy-start.1
  95.8 0.1 stack.32
  95.9 3.9 %fusion.2 = (f32[2048]{0:T(1024)S(1)}, f32[2048]{0:T(1024)S(1)}, f32[2048]{0:T(1024)S(1)}) fusion(f32[2048,576]{0,1:T(8,128)} %get-tuple-element.17, f32[2048]{0:T(1024)S(1)} %get-tuple-element.16, pred[576]{0:T(1024)(128)(4,1)S(1)} %broadcast_compare_fusion, s32[2048]{0:T(1024)S(1)} %bitcast.25, s32[576]{0:T(1024)S(1)} %iota_add_fusion), kind=kLoop, calls=%fused_computation.5 | loop fusion | flops 10610688 | bytes 4762432 | tf_op jit(solution)/shard_map/reduce_sum | solution.py:25
  99.8 0.1 stack.33
  99.8 0.1 stack.34
  99.9 0.1 stack.35
  100.0 0.2 copy.26
  100.2 0.9 copy.27
  101.1 9.9 %all-to-all-start = ((f32[128,4,16]{2,1,0:T(4,128)}), f32[128,4,16]{2,1,0:T(4,128)S(1)}, u32[]{:S(2)}, u32[]{:S(2)}) async-start(f32[128,4,16]{2,1,0:T(4,128)} %copy.27), calls=%async_computation | async-start | bytes 524288 | tf_op jit(solution)/shard_map/all_to_all | solution.py:186
  111.0 0.0 copy-done
  111.0 0.0 copy-done.1
  111.0 0.7 select_reduce_fusion.2
  111.7 12.5 %all-to-all-done = f32[128,4,16]{2,1,0:T(4,128)S(1)} async-done(((f32[128,4,16]{2,1,0:T(4,128)}), f32[128,4,16]{2,1,0:T(4,128)S(1)}, u32[]{:S(2)}, u32[]{:S(2)}) %all-to-all-start) | async-done | bytes 32800 | tf_op jit(solution)/shard_map/all_to_all | solution.py:186
  124.2 0.2 fusion.21
  124.5 1.1 compare_select_fusion.2
  (9 shorter events, 0.2 us)
Async XLA Ops:
  0.6 82.6 %collective-permute-start = (bf16[2560,288]{0,1:T(8,128)(2,1)}, bf16[2560,288]{0,1:T(8,128)(2,1)S(1)}, u32[]{:S(2)}, u32[]{:S(2)}) collective-permute-start(bf16[2560,288]{0,1:T(8,128)(2,1)} %param.8), channel_id=1, source_target_pairs={{0,1},{1,0},{2,3},{3,2},{4,5},{5,4},{6,7},{7,6},{8,9},{9,8},{10,11... | collective-permute-start | bytes 4423688 | tf_op jit(solution)/shard_map/ppermute | solution.py:173
  4.4 78.8 %copy-start.2 = (bf16[2560,288]{0,1:T(8,128)(2,1)S(1)}, bf16[2560,288]{0,1:T(8,128)(2,1)}, u32[]{:S(2)}) copy-start(bf16[2560,288]{0,1:T(8,128)(2,1)} %param.8) | copy-start | bytes 4423684
  95.8 15.2 %copy-start = (s32[512]{0:T(512)S(1)}, s32[512]{0:T(512)}, u32[]{:S(2)}) copy-start(s32[512]{0:T(512)} %param.10) | copy-start | bytes 6148
  95.8 15.2 %copy-start.1 = (s32[512]{0:T(512)S(1)}, s32[512]{0:T(512)}, u32[]{:S(2)}) copy-start(s32[512]{0:T(512)} %param.11) | copy-start | bytes 6148
  101.1 23.1 %all-to-all-start = ((f32[128,4,16]{2,1,0:T(4,128)}), f32[128,4,16]{2,1,0:T(4,128)S(1)}, u32[]{:S(2)}, u32[]{:S(2)}) async-start(f32[128,4,16]{2,1,0:T(4,128)} %copy.27), calls=%async_computation | async-start | bytes 524288 | tf_op jit(solution)/shard_map/all_to_all | solution.py:186

commit v5 on v4

--- a/solution.py
+++ b/solution.py
@@ -154,6 +154,84 @@
     )(packed)
 
 
+def combine(parts):
+    top = jnp.max(parts[:, 0], axis=0)
+    factor = jnp.exp(parts[:, 0] - top[None])
+    total = jnp.sum(parts[:, 1] * factor, axis=0)
+    weighted = jnp.sum(parts[:, 2] * factor, axis=0)
+    picked = jnp.sum(parts[:, 3], axis=0)
+    return jnp.stack([top, total, weighted, picked], axis=0)
+
+
+def reduce_kernel(sizes, a_ref, out_ref, r1, c1, r2, c2, r3, send_sem, recv_sem):
+    pos = {a: lax.axis_index(a) for a in AXES}
+
+    def peer(axis, k):
+        at = dict(pos)
+        at[axis] = lax.rem(pos[axis] + k, sizes[axis])
+        return tuple(at[a] for a in AXES)
+
+    barrier = pltpu.get_barrier_semaphore()
+    count = 0
+    for axis in CHIP_AXES:
+        for k in range(1, sizes[axis]):
+            pl.semaphore_signal(barrier, inc=1, device_id=peer(axis, k), device_id_type=pl.DeviceIdType.MESH)
+            count += 1
+    pl.semaphore_wait(barrier, count)
+
+    sends = []
+
+    def stage(t, axis, src_of, land):
+        n = sizes[axis]
+        for k in range(1, n):
+            copy = pltpu.make_async_remote_copy(
+                src_ref=src_of(lax.rem(pos[axis] + k, n)), dst_ref=land.at[pos[axis]],
+                send_sem=send_sem.at[t, k], recv_sem=recv_sem.at[t, (n - k) % n],
+                device_id=peer(axis, k), device_id_type=pl.DeviceIdType.MESH,
+            )
+            copy.start()
+            sends.append(copy)
+        for j in range(1, n):
+            slot = land.at[lax.rem(pos[axis] + j, n)]
+            pltpu.make_async_remote_copy(
+                src_ref=slot, dst_ref=slot, send_sem=send_sem.at[t, j], recv_sem=recv_sem.at[t, j],
+                device_id=peer(axis, j), device_id_type=pl.DeviceIdType.MESH,
+            ).wait_recv()
+
+    r1[pos["y"]] = a_ref[pos["y"]]
+    stage(0, "y", lambda i: a_ref.at[i], r1)
+    c1[...] = combine(r1[...])
+    own_x = pl.multiple_of(pos["x"] * LANES, LANES)
+    r2[pos["x"]] = c1[:, pl.ds(own_x, LANES)]
+    stage(1, "x", lambda i: c1.at[:, pl.ds(pl.multiple_of(i * LANES, LANES), LANES)], r2)
+    c2[...] = combine(r2[...])
+    r3[pos["z"]] = c2[...]
+    stage(2, "z", lambda i: c2, r3)
+    out_ref[...] = combine(r3[...])
+    for copy in sends:
+        copy.wait_send()
+
+
+def reduce_stats(parts, sizes):
+    ny, nx, nz = sizes["y"], sizes["x"], sizes["z"]
+    longest = max(ny, nx, nz)
+    width = parts.shape[-1]
+    return pl.pallas_call(
+        functools.partial(reduce_kernel, sizes),
+        out_shape=jax.ShapeDtypeStruct((4, LANES), jnp.float32),
+        scratch_shapes=[
+            pltpu.VMEM((ny, 4, width), jnp.float32),
+            pltpu.VMEM((4, width), jnp.float32),
+            pltpu.VMEM((nx, 4, LANES), jnp.float32),
+            pltpu.VMEM((4, LANES), jnp.float32),
+            pltpu.VMEM((nz, 4, LANES), jnp.float32),
+            pltpu.SemaphoreType.DMA((3, longest)),
+            pltpu.SemaphoreType.DMA((3, longest)),
+        ],
+        compiler_params=pltpu.CompilerParams(collective_id=1, has_side_effects=True),
+    )(parts)
+
+
 def body(hidden, norm_gain, head, token_ids, req_len, req_owner):
     local_rows, width = hidden.shape
     columns = head.shape[1]
@@ -180,17 +258,10 @@
     all_ids = decode_ids(gathered[:, width:width + 3])
     stats = jnp.stack(slice_stats(all_rows, all_ids, chip_head, col_index, real_cols), axis=0)
 
-    stats = stats.reshape(4, size["y"], size["x"], size["z"], local_rows)
-    chips = size["z"] * size["x"] * size["y"]
-    send = jnp.transpose(stats, (3, 2, 1, 0, 4)).reshape(chips, 4, local_rows)
-    got = lax.all_to_all(send, CHIP_AXES, 0, 0, tiled=True)
-
-    m_i, s_i, w_i, p_i = got[:, 0], got[:, 1], got[:, 2], got[:, 3]
-    top = jnp.max(m_i, axis=0)
-    factor = jnp.exp(m_i - top[None, :])
-    total_all = jnp.sum(s_i * factor, axis=0)
-    weighted_all = jnp.sum(w_i * factor, axis=0)
-    picked_all = jnp.sum(p_i, axis=0)
+    parts = jnp.transpose(stats.reshape(4, size["y"], -1), (1, 0, 2))
+    reduced = reduce_stats(parts, size)
+    mine = lax.dynamic_slice_in_dim(reduced, pos["z"] * local_rows, local_rows, axis=1)
+    top, total_all, weighted_all, picked_all = mine[0], mine[1], mine[2], mine[3]
 
     load = jnp.sum(jnp.where(req_owner == me, req_len, 0))
     live = jnp.arange(local_rows, dtype=jnp.int32) < load

time: 126 us -> 116 us (0.921)
  Pallas kernels: 77.4 us -> 94.2 us
  waiting for transfers between devices: 12.5 us -> 0.01 us
  starting transfers between devices: 10 us -> 0.09 us
  matrix products: 12.5 us -> 10.3 us
  other arithmetic: 8.78 us -> 7.38 us
    pallas_call x0 -> x1, Pallas kernels: none -> 16.7 us  [reduce_stats(): pl.pallas_call(functools.partial(reduce_kernel, sizes), out_shape=jax.Sha...]
    all_to_all x1 -> x0, waiting for transfers between devices: 12.5 us -> none  [body(): got = lax.all_to_all(send, CHIP_AXES, 0, 0, tiled=True)]
    all_to_all x1 -> x0, starting transfers between devices: 9.9 us -> none  [body(): got = lax.all_to_all(send, CHIP_AXES, 0, 0, tiled=True)]
    dot_general x1, matrix products: 12.5 us -> 10.3 us  [slice_stats(): logits = jnp.dot(rows, head, preferred_element_type=jnp.float32) / 10.0]
    reduce_sum x1, other arithmetic: 3.88 us -> 2.34 us  [slice_stats(): total = jnp.sum(expo, axis=1)]
  transfers between devices with their start and end apart: 2 -> 1, of which waited for: 1 -> 0; matrix products, arithmetic and copies ran while one was open for 5% -> 5% of each run, Pallas kernels for 62% -> 67%
where the time goes in v5:
time: 116 us
  Pallas kernels  94.2 us (81%)
  matrix products  10.3 us (9%)
  other arithmetic  7.38 us (6%)
  local copies, waits for them, and re-layouts  3.05 us (3%)
    pallas_call x1, Pallas kernels, gather_rows(): pl.pallas_call(functools.partial(gather_kernel, sizes, spans), out_shape=...  77.5 us
    pallas_call x1, Pallas kernels, reduce_stats(): pl.pallas_call(functools.partial(reduce_kernel, sizes), out_shape=jax.Sha...  16.7 us
    dot_general x1, matrix products, slice_stats(): logits = jnp.dot(rows, head, preferred_element_type=jnp.float32) / 10.0  10.3 us
    reduce_sum x1, other arithmetic, slice_stats(): total = jnp.sum(expo, axis=1)  2.34 us
  transfers between devices with their start and end apart: 1, of which 0 were waited for; matrix products, arithmetic and copies ran while one was open for 5% of the time, Pallas kernels for 67%

profile of v5, /device:TPU:2, one launch (start us, length us, event | category | flops | bytes accessed | tf_op | source)
XLA Modules:
  0.0 115.9 jit_solution(6967914920541260539)
XLA Ops:
  0.6 0.1 collective-permute-start
  0.7 0.7 fusion.18
  1.4 1.0 fusion.11
  2.4 0.1 copy.11
  2.5 0.1 copy.12
  2.6 0.1 copy.13
  2.7 1.0 fusion.13
  3.7 0.7 concatenate.11.x_ref
  4.4 0.0 copy-start
  4.4 0.0 copy-start.1
  4.4 0.0 copy-start.2
  4.4 77.5 %shard_map.77 = bf16[4,4,8,16,2688]{4,3,2,1,0:T(8,128)(2,1)} custom-call(bf16[16,2688]{1,0:T(8,128)(2,1)} %concatenate.11.x_ref), custom_call_target="tpu_custom_call" | custom-call | tf_op jit(solution)/shard_map/pallas_call | solution.py:143
  81.9 1.1 slice.37
  83.0 0.2 copy.15
  83.3 0.0 copy-done
  83.3 0.0 copy-done.1
  83.3 0.6 select_reduce_fusion.2
  83.9 0.0 collective-permute-done
  84.0 0.0 copy-done.2
  84.0 10.3 %fusion.21 = (f32[2048]{0:T(1024)S(1)}, f32[2048,576]{0,1:T(8,128)S(1)}) fusion(bf16[2560,288]{0,1:T(8,128)(2,1)S(1)} %collective-permute-done, bf16[2560,288]{0,1:T(8,128)(2,1)S(1)} %copy-done.2, pred[]{:T(512)S(6)} %eq.29, bf16[2048,2688]{1,0:T(8,128)(2,1)} %bitcast.33, pred[576]{0:T(1024)(128)(4,1)S(1)} %broadcast_compare_fusion), kind=kOutput, calls=%fused_computation.55 | convolution fusion | flops 6056605696 | bytes 18162240 | tf_op jit(solution)/shard_map/dot_general | solution.py:21
  94.3 2.3 %fusion.2 = (f32[2048]{0:T(1024)S(1)}, f32[2048]{0:T(1024)S(1)}, f32[2048]{0:T(1024)S(1)}) fusion(f32[2048,576]{0,1:T(8,128)S(1)} %get-tuple-element.11, f32[2048]{0:T(1024)S(1)} %get-tuple-element.10, pred[576]{0:T(1024)(128)(4,1)S(1)} %broadcast_compare_fusion, s32[2048]{0:T(1024)S(1)} %bitcast.34, s32[576]{0:T(1024)S(1)} %iota_add_fusion), kind=kLoop, calls=%fused_computation.5 | loop fusion | flops 10610688 | bytes 4762432 | tf_op jit(solution)/shard_map/reduce_sum | solution.py:25
  96.7 0.6 maximum_bitcast_fusion.a_ref
  97.3 16.7 %shard_map.78 = f32[4,128]{1,0:T(4,128)} custom-call(f32[4,4,512]{2,1,0:T(4,128)} %maximum_bitcast_fusion.a_ref), custom_call_target="tpu_custom_call" | custom-call | tf_op jit(solution)/shard_map/pallas_call | solution.py:219
  114.1 0.7 constant_dynamic-slice_fusion
  114.8 1.1 compare_select_fusion.2
  (6 shorter events, 0.1 us)
Async XLA Ops:
  0.6 83.3 %collective-permute-start = (bf16[2560,288]{0,1:T(8,128)(2,1)}, bf16[2560,288]{0,1:T(8,128)(2,1)S(1)}, u32[]{:S(2)}, u32[]{:S(2)}) collective-permute-start(bf16[2560,288]{0,1:T(8,128)(2,1)} %param.8), channel_id=1, source_target_pairs={{0,1},{1,0},{2,3},{3,2},{4,5},{5,4},{6,7},{7,6},{8,9},{9,8},{10,11... | collective-permute-start | bytes 4423688 | tf_op jit(solution)/shard_map/ppermute | solution.py:251
  4.4 78.9 %copy-start = (s32[512]{0:T(512)S(1)}, s32[512]{0:T(512)}, u32[]{:S(2)}) copy-start(s32[512]{0:T(512)} %param.10) | copy-start | bytes 6148
  4.4 78.9 %copy-start.1 = (s32[512]{0:T(512)S(1)}, s32[512]{0:T(512)}, u32[]{:S(2)}) copy-start(s32[512]{0:T(512)} %param.11) | copy-start | bytes 6148
  4.4 79.5 %copy-start.2 = (bf16[2560,288]{0,1:T(8,128)(2,1)S(1)}, bf16[2560,288]{0,1:T(8,128)(2,1)}, u32[]{:S(2)}) copy-start(bf16[2560,288]{0,1:T(8,128)(2,1)} %param.8) | copy-start | bytes 4423684

commit v6 on v5

--- a/solution.py
+++ b/solution.py
@@ -64,7 +64,7 @@
     barrier = pltpu.get_barrier_semaphore()
     count = 0
     for axis in CHIP_AXES:
-        for k in (1, -1):
+        for k in range(1, sizes[axis]):
             pl.semaphore_signal(barrier, inc=1, device_id=peer(axis, k), device_id_type=pl.DeviceIdType.MESH)
             count += 1
     pl.semaphore_wait(barrier, count)
@@ -74,8 +74,8 @@
 
     plans = []
     for order in STREAMS:
-        plan = []
-        for t, axis in enumerate(order):
+        plan = [(0, order[0], 0, False)]
+        for t, axis in enumerate(order[1:], start=1):
             n = sizes[axis]
             for q in range(1, n // 2 + 1):
                 plan.append((t, axis, q, n % 2 == 0 and q == n // 2))
@@ -86,12 +86,29 @@
         c0, w = spans[s]
         order = STREAMS[s]
         held = order[:t]
+        n = sizes[axis]
+        out = []
+        if q == 0:
+            cols = pl.ds(c0, w)
+            for k in range(1, n):
+                if sending:
+                    dst = view(g_ref, held, axis, 0, cols)
+                    src = x_ref.at[:, cols] if t == 0 else dst
+                    target, label = peer(axis, k), (n - k) % n
+                else:
+                    src = dst = view(g_ref, held, axis, k, cols)
+                    target, label = peer(axis, k), k
+                out.append(pltpu.make_async_remote_copy(
+                    src_ref=src, dst_ref=dst, send_sem=send_sem.at[s, step, k if sending else label],
+                    recv_sem=recv_sem.at[s, step, label], device_id=target,
+                    device_id_type=pl.DeviceIdType.MESH,
+                ))
+            return out
         if split:
             cut = (w // LANES // 2) * LANES
             col_of = [pl.ds(c0, cut), pl.ds(c0 + cut, w - cut)]
         else:
             col_of = [pl.ds(c0, w), pl.ds(c0, w)]
-        out = []
         for d, sign in enumerate((1, -1)):
             cols = col_of[d]
             if sending:
@@ -110,10 +127,12 @@
             ))
         return out
 
-    steps = len(plans[0])
+    steps = max(len(p) for p in plans)
     sends = []
     for g in range(steps):
         for s in range(len(STREAMS)):
+            if g >= len(plans[s]):
+                continue
             if g > 0:
                 for copy in step_copies(s, g - 1, False):
                     copy.wait_recv()
@@ -123,7 +142,7 @@
                 copy.start()
                 sends.append(copy)
     for s in range(len(STREAMS)):
-        for copy in step_copies(s, steps - 1, False):
+        for copy in step_copies(s, len(plans[s]) - 1, False):
             copy.wait_recv()
     for copy in sends:
         copy.wait_send()
@@ -139,15 +158,16 @@
         spans.append((at * LANES, c * LANES))
         at += c
     shape = (sizes["y"], sizes["x"], sizes["z"], rows, width)
-    steps = sum(sizes[a] // 2 for a in CHIP_AXES)
+    steps = 1 + max(sizes[a] // 2 for a in CHIP_AXES) + max(sizes[a] // 2 for a in CHIP_AXES)
+    longest = max(sizes[a] for a in CHIP_AXES)
     return pl.pallas_call(
         functools.partial(gather_kernel, sizes, spans),
         out_shape=jax.ShapeDtypeStruct(shape, packed.dtype),
         in_specs=[pl.BlockSpec(memory_space=pl.ANY)],
         out_specs=pl.BlockSpec(memory_space=pl.ANY),
         scratch_shapes=[
-            pltpu.SemaphoreType.DMA((3, steps, 2)),
-            pltpu.SemaphoreType.DMA((3, steps, 2)),
+            pltpu.SemaphoreType.DMA((3, steps, longest)),
+            pltpu.SemaphoreType.DMA((3, steps, longest)),
             pltpu.SemaphoreType.DMA(()),
         ],
         compiler_params=pltpu.CompilerParams(collective_id=0, has_side_effects=True),

time: 116 us -> 139 us (1.20)
  Pallas kernels: 94.2 us -> 117 us
    pallas_call x1, Pallas kernels: 77.5 us -> 101 us  [gather_rows(): pl.pallas_call(functools.partial(gather_kernel, sizes, spans), out_shape=...]
  transfers between devices with their start and end apart: 1 -> 1, of which waited for: 0 -> 0; matrix products, arithmetic and copies ran while one was open for 5% -> 4% of each run, Pallas kernels for 67% -> 73%
where the time goes in v6:
time: 139 us
  Pallas kernels  117 us (84%)
  matrix products  10.3 us (7%)
  other arithmetic  7.38 us (5%)
  local copies, waits for them, and re-layouts  3.05 us (2%)
    pallas_call x1, Pallas kernels, gather_rows(): pl.pallas_call(functools.partial(gather_kernel, sizes, spans), out_shape=...  101 us
    pallas_call x1, Pallas kernels, reduce_stats(): pl.pallas_call(functools.partial(reduce_kernel, sizes), out_shape=jax.Sha...  16.6 us
    dot_general x1, matrix products, slice_stats(): logits = jnp.dot(rows, head, preferred_element_type=jnp.float32) / 10.0  10.3 us
  transfers between devices with their start and end apart: 1, of which 0 were waited for; matrix products, arithmetic and copies ran while one was open for 4% of the time, Pallas kernels for 73%

profile of v6, /device:TPU:2, one launch (start us, length us, event | category | flops | bytes accessed | tf_op | source)
XLA Modules:
  0.0 139.1 jit_solution(11481670306633196111)
XLA Ops:
  0.6 0.1 collective-permute-start
  0.7 0.7 fusion.18
  1.4 1.0 fusion.11
  2.4 0.1 copy.11
  2.5 0.1 copy.12
  2.6 0.1 copy.13
  2.7 1.0 fusion.13
  3.7 0.7 concatenate.11.x_ref
  4.4 0.0 copy-start
  4.4 0.0 copy-start.1
  4.4 0.0 copy-start.2
  4.4 100.9 %shard_map.77 = bf16[4,4,8,16,2688]{4,3,2,1,0:T(8,128)(2,1)} custom-call(bf16[16,2688]{1,0:T(8,128)(2,1)} %concatenate.11.x_ref), custom_call_target="tpu_custom_call" | custom-call | tf_op jit(solution)/shard_map/pallas_call | solution.py:163
  105.3 1.1 slice.37
  106.4 0.2 copy.15
  106.7 0.0 copy-done
  106.7 0.0 copy-done.1
  106.7 0.6 select_reduce_fusion.2
  107.4 0.0 collective-permute-done
  107.4 0.0 copy-done.2
  107.4 10.3 %fusion.21 = (f32[2048]{0:T(1024)S(1)}, f32[2048,576]{0,1:T(8,128)S(1)}) fusion(bf16[2560,288]{0,1:T(8,128)(2,1)S(1)} %collective-permute-done, bf16[2560,288]{0,1:T(8,128)(2,1)S(1)} %copy-done.2, pred[]{:T(512)S(6)} %eq.29, bf16[2048,2688]{1,0:T(8,128)(2,1)} %bitcast.33, pred[576]{0:T(1024)(128)(4,1)S(1)} %broadcast_compare_fusion), kind=kOutput, calls=%fused_computation.55 | convolution fusion | flops 6056605696 | bytes 18162240 | tf_op jit(solution)/shard_map/dot_general | solution.py:21
  117.7 2.3 %fusion.2 = (f32[2048]{0:T(1024)S(1)}, f32[2048]{0:T(1024)S(1)}, f32[2048]{0:T(1024)S(1)}) fusion(f32[2048,576]{0,1:T(8,128)S(1)} %get-tuple-element.11, f32[2048]{0:T(1024)S(1)} %get-tuple-element.10, pred[576]{0:T(1024)(128)(4,1)S(1)} %broadcast_compare_fusion, s32[2048]{0:T(1024)S(1)} %bitcast.34, s32[576]{0:T(1024)S(1)} %iota_add_fusion), kind=kLoop, calls=%fused_computation.5 | loop fusion | flops 10610688 | bytes 4762432 | tf_op jit(solution)/shard_map/reduce_sum | solution.py:25
  120.1 0.6 maximum_bitcast_fusion.a_ref
  120.7 16.6 %shard_map.78 = f32[4,128]{1,0:T(4,128)} custom-call(f32[4,4,512]{2,1,0:T(4,128)} %maximum_bitcast_fusion.a_ref), custom_call_target="tpu_custom_call" | custom-call | tf_op jit(solution)/shard_map/pallas_call | solution.py:239
  137.3 0.7 constant_dynamic-slice_fusion
  138.0 1.1 compare_select_fusion.2
  (6 shorter events, 0.1 us)
Async XLA Ops:
  0.6 106.7 %collective-permute-start = (bf16[2560,288]{0,1:T(8,128)(2,1)}, bf16[2560,288]{0,1:T(8,128)(2,1)S(1)}, u32[]{:S(2)}, u32[]{:S(2)}) collective-permute-start(bf16[2560,288]{0,1:T(8,128)(2,1)} %param.8), channel_id=1, source_target_pairs={{0,1},{1,0},{2,3},{3,2},{4,5},{5,4},{6,7},{7,6},{8,9},{9,8},{10,11... | collective-permute-start | bytes 4423688 | tf_op jit(solution)/shard_map/ppermute | solution.py:271
  4.4 102.3 %copy-start = (s32[512]{0:T(512)S(1)}, s32[512]{0:T(512)}, u32[]{:S(2)}) copy-start(s32[512]{0:T(512)} %param.10) | copy-start | bytes 6148
  4.4 102.3 %copy-start.1 = (s32[512]{0:T(512)S(1)}, s32[512]{0:T(512)}, u32[]{:S(2)}) copy-start(s32[512]{0:T(512)} %param.11) | copy-start | bytes 6148
  4.4 102.9 %copy-start.2 = (bf16[2560,288]{0,1:T(8,128)(2,1)S(1)}, bf16[2560,288]{0,1:T(8,128)(2,1)}, u32[]{:S(2)}) copy-start(bf16[2560,288]{0,1:T(8,128)(2,1)} %param.8) | copy-start | bytes 4423684

commit v7 on v5

--- a/solution.py
+++ b/solution.py
@@ -132,7 +132,7 @@
 def gather_rows(packed, sizes):
     rows, width = packed.shape
     tiles = width // LANES
-    counts = [tiles * 8 // 21, tiles * 6 // 21]
+    counts = [tiles * 7 // 21, tiles * 8 // 21]
     counts.append(tiles - sum(counts))
     spans, at = [], 0
     for c in counts:

time: 116 us -> 118 us (1.017)
  Pallas kernels: 94.2 us -> 96 us
    pallas_call x1, Pallas kernels: 16.7 us -> 18.8 us  [reduce_stats(): pl.pallas_call(functools.partial(reduce_kernel, sizes), out_shape=jax.Sha...]
  transfers between devices with their start and end apart: 1 -> 1, of which waited for: 0 -> 0; matrix products, arithmetic and copies ran while one was open for 5% -> 5% of each run, Pallas kernels for 67% -> 66%
where the time goes in v7:
time: 118 us
  Pallas kernels  96 us (81%)
  matrix products  10.3 us (9%)
  other arithmetic  7.38 us (6%)
  local copies, waits for them, and re-layouts  3.05 us (3%)
    pallas_call x1, Pallas kernels, gather_rows(): pl.pallas_call(functools.partial(gather_kernel, sizes, spans), out_shape=...  77.2 us
    pallas_call x1, Pallas kernels, reduce_stats(): pl.pallas_call(functools.partial(reduce_kernel, sizes), out_shape=jax.Sha...  18.8 us
    dot_general x1, matrix products, slice_stats(): logits = jnp.dot(rows, head, preferred_element_type=jnp.float32) / 10.0  10.3 us
  transfers between devices with their start and end apart: 1, of which 0 were waited for; matrix products, arithmetic and copies ran while one was open for 5% of the time, Pallas kernels for 66%

profile of v7, /device:TPU:2, one launch (start us, length us, event | category | flops | bytes accessed | tf_op | source)
XLA Modules:
  0.0 117.6 jit_solution(17770923597605374055)
XLA Ops:
  0.6 0.1 collective-permute-start
  0.7 0.7 fusion.18
  1.4 1.0 fusion.11
  2.4 0.1 copy.11
  2.5 0.1 copy.12
  2.6 0.1 copy.13
  2.7 1.0 fusion.13
  3.7 0.7 concatenate.11.x_ref
  4.4 0.0 copy-start
  4.4 0.0 copy-start.1
  4.4 0.0 copy-start.2
  4.4 77.2 %shard_map.77 = bf16[4,4,8,16,2688]{4,3,2,1,0:T(8,128)(2,1)} custom-call(bf16[16,2688]{1,0:T(8,128)(2,1)} %concatenate.11.x_ref), custom_call_target="tpu_custom_call" | custom-call | tf_op jit(solution)/shard_map/pallas_call | solution.py:143
  81.6 1.1 slice.37
  82.7 0.2 copy.15
  83.0 0.0 copy-done
  83.0 0.0 copy-done.1
  83.0 0.6 select_reduce_fusion.2
  83.7 0.0 collective-permute-done
  83.7 0.0 copy-done.2
  83.7 10.3 %fusion.21 = (f32[2048]{0:T(1024)S(1)}, f32[2048,576]{0,1:T(8,128)S(1)}) fusion(bf16[2560,288]{0,1:T(8,128)(2,1)S(1)} %collective-permute-done, bf16[2560,288]{0,1:T(8,128)(2,1)S(1)} %copy-done.2, pred[]{:T(512)S(6)} %eq.29, bf16[2048,2688]{1,0:T(8,128)(2,1)} %bitcast.33, pred[576]{0:T(1024)(128)(4,1)S(1)} %broadcast_compare_fusion), kind=kOutput, calls=%fused_computation.55 | convolution fusion | flops 6056605696 | bytes 18162240 | tf_op jit(solution)/shard_map/dot_general | solution.py:21
  94.0 2.3 %fusion.2 = (f32[2048]{0:T(1024)S(1)}, f32[2048]{0:T(1024)S(1)}, f32[2048]{0:T(1024)S(1)}) fusion(f32[2048,576]{0,1:T(8,128)S(1)} %get-tuple-element.11, f32[2048]{0:T(1024)S(1)} %get-tuple-element.10, pred[576]{0:T(1024)(128)(4,1)S(1)} %broadcast_compare_fusion, s32[2048]{0:T(1024)S(1)} %bitcast.34, s32[576]{0:T(1024)S(1)} %iota_add_fusion), kind=kLoop, calls=%fused_computation.5 | loop fusion | flops 10610688 | bytes 4762432 | tf_op jit(solution)/shard_map/reduce_sum | solution.py:25
  96.4 0.6 maximum_bitcast_fusion.a_ref
  97.0 18.8 %shard_map.78 = f32[4,128]{1,0:T(4,128)} custom-call(f32[4,4,512]{2,1,0:T(4,128)} %maximum_bitcast_fusion.a_ref), custom_call_target="tpu_custom_call" | custom-call | tf_op jit(solution)/shard_map/pallas_call | solution.py:219
  115.8 0.7 constant_dynamic-slice_fusion
  116.5 1.1 compare_select_fusion.2
  (6 shorter events, 0.1 us)
Async XLA Ops:
  0.6 83.0 %collective-permute-start = (bf16[2560,288]{0,1:T(8,128)(2,1)}, bf16[2560,288]{0,1:T(8,128)(2,1)S(1)}, u32[]{:S(2)}, u32[]{:S(2)}) collective-permute-start(bf16[2560,288]{0,1:T(8,128)(2,1)} %param.8), channel_id=1, source_target_pairs={{0,1},{1,0},{2,3},{3,2},{4,5},{5,4},{6,7},{7,6},{8,9},{9,8},{10,11... | collective-permute-start | bytes 4423688 | tf_op jit(solution)/shard_map/ppermute | solution.py:251
  4.4 78.6 %copy-start = (s32[512]{0:T(512)S(1)}, s32[512]{0:T(512)}, u32[]{:S(2)}) copy-start(s32[512]{0:T(512)} %param.10) | copy-start | bytes 6148
  4.4 78.6 %copy-start.1 = (s32[512]{0:T(512)S(1)}, s32[512]{0:T(512)}, u32[]{:S(2)}) copy-start(s32[512]{0:T(512)} %param.11) | copy-start | bytes 6148
  4.4 79.2 %copy-start.2 = (bf16[2560,288]{0,1:T(8,128)(2,1)S(1)}, bf16[2560,288]{0,1:T(8,128)(2,1)}, u32[]{:S(2)}) copy-start(bf16[2560,288]{0,1:T(8,128)(2,1)} %param.8) | copy-start | bytes 4423684

commit v8 on v5

--- a/solution.py
+++ b/solution.py
@@ -113,13 +113,20 @@
     steps = len(plans[0])
     sends = []
     for g in range(steps):
+        if g == 1:
+            own.wait()
         for s in range(len(STREAMS)):
+            out = step_copies(s, g, True)
+            if g > 0 and plans[s][g][0] == plans[s][g - 1][0]:
+                for arrived, copy in zip(step_copies(s, g - 1, False), out):
+                    arrived.wait_recv()
+                    copy.start()
+                    sends.append(copy)
+                continue
             if g > 0:
                 for copy in step_copies(s, g - 1, False):
                     copy.wait_recv()
-            if g == 1 and s == 0:
-                own.wait()
-            for copy in step_copies(s, g, True):
+            for copy in out:
                 copy.start()
                 sends.append(copy)
     for s in range(len(STREAMS)):

time: 116 us -> 117 us (level)
  transfers between devices with their start and end apart: 1 -> 1, of which waited for: 0 -> 0; matrix products, arithmetic and copies ran while one was open for 5% -> 5% of each run, Pallas kernels for 67% -> 66%
where the time goes in v8:
time: 117 us; the launch traced here: 116 us
  Pallas kernels  94.6 us (81%)
  matrix products  10.3 us (9%)
  other arithmetic  7.38 us (6%)
  local copies, waits for them, and re-layouts  3.05 us (3%)
    pallas_call x1, Pallas kernels, gather_rows(): pl.pallas_call(functools.partial(gather_kernel, sizes, spans), out_shape=...  76.8 us
    pallas_call x1, Pallas kernels, reduce_stats(): pl.pallas_call(functools.partial(reduce_kernel, sizes), out_shape=jax.Sha...  17.8 us
    dot_general x1, matrix products, slice_stats(): logits = jnp.dot(rows, head, preferred_element_type=jnp.float32) / 10.0  10.3 us
    reduce_sum x1, other arithmetic, slice_stats(): total = jnp.sum(expo, axis=1)  2.34 us
  transfers between devices with their start and end apart: 1, of which 0 were waited for; matrix products, arithmetic and copies ran while one was open for 5% of the time, Pallas kernels for 66%

profile of v8, /device:TPU:2, one launch (start us, length us, event | category | flops | bytes accessed | tf_op | source)
XLA Modules:
  0.0 116.3 jit_solution(10023199939734166406)
XLA Ops:
  0.6 0.1 collective-permute-start
  0.7 0.7 fusion.18
  1.4 1.0 fusion.11
  2.4 0.1 copy.11
  2.5 0.1 copy.12
  2.6 0.1 copy.13
  2.7 1.0 fusion.13
  3.7 0.7 concatenate.11.x_ref
  4.4 0.0 copy-start
  4.4 0.0 copy-start.1
  4.4 0.0 copy-start.2
  4.4 76.8 %shard_map.77 = bf16[4,4,8,16,2688]{4,3,2,1,0:T(8,128)(2,1)} custom-call(bf16[16,2688]{1,0:T(8,128)(2,1)} %concatenate.11.x_ref), custom_call_target="tpu_custom_call" | custom-call | tf_op jit(solution)/shard_map/pallas_call | solution.py:150
  81.3 1.1 slice.37
  82.4 0.2 copy.15
  82.7 0.0 copy-done
  82.7 0.0 copy-done.1
  82.7 0.6 select_reduce_fusion.2
  83.3 0.0 collective-permute-done
  83.3 0.0 copy-done.2
  83.3 10.3 %fusion.21 = (f32[2048]{0:T(1024)S(1)}, f32[2048,576]{0,1:T(8,128)S(1)}) fusion(bf16[2560,288]{0,1:T(8,128)(2,1)S(1)} %collective-permute-done, bf16[2560,288]{0,1:T(8,128)(2,1)S(1)} %copy-done.2, pred[]{:T(512)S(6)} %eq.29, bf16[2048,2688]{1,0:T(8,128)(2,1)} %bitcast.33, pred[576]{0:T(1024)(128)(4,1)S(1)} %broadcast_compare_fusion), kind=kOutput, calls=%fused_computation.55 | convolution fusion | flops 6056605696 | bytes 18162240 | tf_op jit(solution)/shard_map/dot_general | solution.py:21
  93.7 2.3 %fusion.2 = (f32[2048]{0:T(1024)S(1)}, f32[2048]{0:T(1024)S(1)}, f32[2048]{0:T(1024)S(1)}) fusion(f32[2048,576]{0,1:T(8,128)S(1)} %get-tuple-element.11, f32[2048]{0:T(1024)S(1)} %get-tuple-element.10, pred[576]{0:T(1024)(128)(4,1)S(1)} %broadcast_compare_fusion, s32[2048]{0:T(1024)S(1)} %bitcast.34, s32[576]{0:T(1024)S(1)} %iota_add_fusion), kind=kLoop, calls=%fused_computation.5 | loop fusion | flops 10610688 | bytes 4762432 | tf_op jit(solution)/shard_map/reduce_sum | solution.py:25
  96.0 0.6 maximum_bitcast_fusion.a_ref
  96.7 17.8 %shard_map.78 = f32[4,128]{1,0:T(4,128)} custom-call(f32[4,4,512]{2,1,0:T(4,128)} %maximum_bitcast_fusion.a_ref), custom_call_target="tpu_custom_call" | custom-call | tf_op jit(solution)/shard_map/pallas_call | solution.py:226
  114.5 0.7 constant_dynamic-slice_fusion
  115.2 1.1 compare_select_fusion.2
  (6 shorter events, 0.1 us)
Async XLA Ops:
  0.6 82.7 %collective-permute-start = (bf16[2560,288]{0,1:T(8,128)(2,1)}, bf16[2560,288]{0,1:T(8,128)(2,1)S(1)}, u32[]{:S(2)}, u32[]{:S(2)}) collective-permute-start(bf16[2560,288]{0,1:T(8,128)(2,1)} %param.8), channel_id=1, source_target_pairs={{0,1},{1,0},{2,3},{3,2},{4,5},{5,4},{6,7},{7,6},{8,9},{9,8},{10,11... | collective-permute-start | bytes 4423688 | tf_op jit(solution)/shard_map/ppermute | solution.py:258
  4.4 78.2 %copy-start = (s32[512]{0:T(512)S(1)}, s32[512]{0:T(512)}, u32[]{:S(2)}) copy-start(s32[512]{0:T(512)} %param.10) | copy-start | bytes 6148
  4.4 78.2 %copy-start.1 = (s32[512]{0:T(512)S(1)}, s32[512]{0:T(512)}, u32[]{:S(2)}) copy-start(s32[512]{0:T(512)} %param.11) | copy-start | bytes 6148
  4.4 78.9 %copy-start.2 = (bf16[2560,288]{0,1:T(8,128)(2,1)S(1)}, bf16[2560,288]{0,1:T(8,128)(2,1)}, u32[]{:S(2)}) copy-start(bf16[2560,288]{0,1:T(8,128)(2,1)} %param.8) | copy-start | bytes 4423684

commit v9 on v5

--- a/solution.py
+++ b/solution.py
@@ -232,6 +232,26 @@
     )(parts)
 
 
+def pack_kernel(h_ref, gain_ref, ids_ref, out_ref):
+    values = h_ref[...].astype(jnp.float32)
+    width = values.shape[1]
+    scale = lax.rsqrt(jnp.mean(values * values, axis=-1, keepdims=True) + EPS)
+    out_ref[:, :width] = (values * scale * gain_ref[...]).astype(jnp.bfloat16)
+    ids = ids_ref[...]
+    lane = lax.broadcasted_iota(jnp.int32, (ids.shape[0], LANES), 1)
+    digit = jnp.where(lane == 0, ids // (DIGIT * DIGIT), jnp.where(lane == 1, (ids // DIGIT) % DIGIT, ids % DIGIT))
+    digit = jnp.where(lane < 3, digit, 0)
+    out_ref[:, width:] = digit.astype(jnp.float32).astype(jnp.bfloat16)
+
+
+def pack_rows(hidden, norm_gain, token_ids):
+    rows, width = hidden.shape
+    return pl.pallas_call(
+        pack_kernel,
+        out_shape=jax.ShapeDtypeStruct((rows, width + LANES), jnp.bfloat16),
+    )(hidden, norm_gain.reshape(1, width), token_ids.reshape(rows, 1))
+
+
 def body(hidden, norm_gain, head, token_ids, req_len, req_owner):
     local_rows, width = hidden.shape
     columns = head.shape[1]
@@ -241,12 +261,7 @@
     core = pos["core"]
     me = chip * size["core"] + core
 
-    values = hidden.astype(jnp.float32)
-    scale = lax.rsqrt(jnp.mean(values * values, axis=-1, keepdims=True) + EPS)
-    normed = (values * scale * norm_gain[None, :]).astype(jnp.bfloat16)
-    coded = code_ids(token_ids)
-    pad = jnp.zeros((local_rows, LANES - coded.shape[1]), jnp.bfloat16)
-    packed = jnp.concatenate([normed, coded, pad], axis=1)
+    packed = pack_rows(hidden, norm_gain, token_ids)
 
     other = lax.ppermute(head, "core", [(0, 1), (1, 0)])
     chip_head = jnp.where(core == 0, jnp.concatenate([head, other], axis=1), jnp.concatenate([other, head], axis=1))

time: 116 us -> 117 us (level)
  other arithmetic: 7.38 us -> 4.7 us
  Pallas kernels: 94.2 us -> 95.9 us
  local copies, waits for them, and re-layouts: 3.05 us -> 4.66 us
    reshape x0 -> x2, local copies, waits for them, and re-layouts: none -> 2.63 us  [the longest x1 1.32 us: pack_rows(): token_ids.reshape(rows, 1)]
    pallas_call x0 -> x1, Pallas kernels: none -> 1.66 us  [pack_rows(): pl.pallas_call(pack_kernel, out_shape=jax.ShapeDtypeStruct((rows, width +...]
  transfers between devices with their start and end apart: 1 -> 1, of which waited for: 0 -> 0; matrix products, arithmetic and copies ran while one was open for 5% -> 4% of each run, Pallas kernels for 67% -> 68%
where the time goes in v9:
time: 117 us; the launch traced here: 116 us
  Pallas kernels  95.9 us (82%)
  matrix products  10.3 us (9%)
  other arithmetic  4.7 us (4%)
  local copies, waits for them, and re-layouts  4.66 us (4%)
    pallas_call x1, Pallas kernels, gather_rows(): pl.pallas_call(functools.partial(gather_kernel, sizes, spans), out_shape=...  77.4 us
    pallas_call x1, Pallas kernels, reduce_stats(): pl.pallas_call(functools.partial(reduce_kernel, sizes), out_shape=jax.Sha...  16.8 us
    dot_general x1, matrix products, slice_stats(): logits = jnp.dot(rows, head, preferred_element_type=jnp.float32) / 10.0  10.3 us
    reduce_sum x1, other arithmetic, slice_stats(): total = jnp.sum(expo, axis=1)  2.34 us
  transfers between devices with their start and end apart: 1, of which 0 were waited for; matrix products, arithmetic and copies ran while one was open for 4% of the time, Pallas kernels for 68%

profile of v9, /device:TPU:2, one launch (start us, length us, event | category | flops | bytes accessed | tf_op | source)
XLA Modules:
  0.0 116.5 jit_solution(15638367151044333078)
XLA Ops:
  0.6 0.1 collective-permute-start
  0.7 1.3 %reshape.32.gain_ref = f32[1,2560]{1,0:T(1,128)} reshape(f32[2560]{0:T(1024)} %param.7) | data formatting | bytes 20480 | tf_op jit(solution)/shard_map/reshape | solution.py:252
  2.1 1.3 %copy.9.ids_ref = s32[16,1]{1,0:T(8,128)} copy(s32[16,1]{0,1:T(1,128)} %bitcast.34) | data formatting | bytes 128 | tf_op jit(solution)/shard_map/reshape | solution.py:252
  3.4 1.7 %shard_map.77.x_ref = bf16[16,2688]{1,0:T(8,128)(2,1)} custom-call(bf16[16,2560]{1,0:T(8,128)(2,1)} %h_ref.1, f32[1,2560]{1,0:T(1,128)} %reshape.32.gain_ref, s32[16,1]{1,0:T(8,128)} %copy.9.ids_ref), custom_call_target="tpu_custom_call" | custom-call | tf_op jit(solution)/shard_map/pallas_call | solution.py:249
  5.0 0.0 copy-start
  5.0 0.0 copy-start.1
  5.0 0.0 copy-start.2
  5.0 77.4 %shard_map.78 = bf16[4,4,8,16,2688]{4,3,2,1,0:T(8,128)(2,1)} custom-call(bf16[16,2688]{1,0:T(8,128)(2,1)} %shard_map.77.x_ref), custom_call_target="tpu_custom_call" | custom-call | tf_op jit(solution)/shard_map/pallas_call | solution.py:143
  82.5 1.1 slice.37
  83.6 0.2 copy.11
  83.8 0.0 copy-done
  83.8 0.0 copy-done.1
  83.9 0.6 select_reduce_fusion.2
  84.5 0.0 collective-permute-done
  84.5 0.0 copy-done.2
  84.5 10.3 %fusion.13 = (f32[2048]{0:T(1024)S(1)}, f32[2048,576]{0,1:T(8,128)S(1)}) fusion(bf16[2560,288]{0,1:T(8,128)(2,1)S(1)} %collective-permute-done, bf16[2560,288]{0,1:T(8,128)(2,1)S(1)} %copy-done.2, pred[]{:T(512)S(6)} %eq.26, bf16[2048,2688]{1,0:T(8,128)(2,1)} %bitcast.28, pred[576]{0:T(1024)(128)(4,1)S(1)} %broadcast_compare_fusion), kind=kOutput, calls=%fused_computation.31 | convolution fusion | flops 6056605696 | bytes 18162240 | tf_op jit(solution)/shard_map/dot_general | solution.py:21
  94.9 2.3 %fusion.2 = (f32[2048]{0:T(1024)S(1)}, f32[2048]{0:T(1024)S(1)}, f32[2048]{0:T(1024)S(1)}) fusion(f32[2048,576]{0,1:T(8,128)S(1)} %get-tuple-element.8, f32[2048]{0:T(1024)S(1)} %get-tuple-element.7, pred[576]{0:T(1024)(128)(4,1)S(1)} %broadcast_compare_fusion, s32[2048]{0:T(1024)S(1)} %bitcast.29, s32[576]{0:T(1024)S(1)} %iota_add_fusion), kind=kLoop, calls=%fused_computation.5 | loop fusion | flops 10610688 | bytes 4762432 | tf_op jit(solution)/shard_map/reduce_sum | solution.py:25
  97.2 0.6 maximum_bitcast_fusion.a_ref
  97.8 16.8 %shard_map.79 = f32[4,128]{1,0:T(4,128)} custom-call(f32[4,4,512]{2,1,0:T(4,128)} %maximum_bitcast_fusion.a_ref), custom_call_target="tpu_custom_call" | custom-call | tf_op jit(solution)/shard_map/pallas_call | solution.py:219
  114.7 0.7 constant_dynamic-slice_fusion
  115.4 1.1 compare_select_fusion
  (4 shorter events, 0.1 us)
Async XLA Ops:
  0.6 83.9 %collective-permute-start = (bf16[2560,288]{0,1:T(8,128)(2,1)}, bf16[2560,288]{0,1:T(8,128)(2,1)S(1)}, u32[]{:S(2)}, u32[]{:S(2)}) collective-permute-start(bf16[2560,288]{0,1:T(8,128)(2,1)} %param.8), channel_id=1, source_target_pairs={{0,1},{1,0},{2,3},{3,2},{4,5},{5,4},{6,7},{7,6},{8,9},{9,8},{10,11... | collective-permute-start | bytes 4423688 | tf_op jit(solution)/shard_map/ppermute | solution.py:266
  5.0 78.8 %copy-start = (s32[512]{0:T(512)S(1)}, s32[512]{0:T(512)}, u32[]{:S(2)}) copy-start(s32[512]{0:T(512)} %param.10) | copy-start | bytes 6148
  5.0 78.8 %copy-start.1 = (s32[512]{0:T(512)S(1)}, s32[512]{0:T(512)}, u32[]{:S(2)}) copy-start(s32[512]{0:T(512)} %param.11) | copy-start | bytes 6148
  5.0 79.5 %copy-start.2 = (bf16[2560,288]{0,1:T(8,128)(2,1)S(1)}, bf16[2560,288]{0,1:T(8,128)(2,1)}, u32[]{:S(2)}) copy-start(bf16[2560,288]{0,1:T(8,128)(2,1)} %param.8) | copy-start | bytes 4423684

commit v10 on v9

--- a/solution.py
+++ b/solution.py
@@ -234,13 +234,16 @@
 
 def pack_kernel(h_ref, gain_ref, ids_ref, out_ref):
     values = h_ref[...].astype(jnp.float32)
-    width = values.shape[1]
+    rows, width = values.shape
     scale = lax.rsqrt(jnp.mean(values * values, axis=-1, keepdims=True) + EPS)
-    out_ref[:, :width] = (values * scale * gain_ref[...]).astype(jnp.bfloat16)
-    ids = ids_ref[...]
-    lane = lax.broadcasted_iota(jnp.int32, (ids.shape[0], LANES), 1)
-    digit = jnp.where(lane == 0, ids // (DIGIT * DIGIT), jnp.where(lane == 1, (ids // DIGIT) % DIGIT, ids % DIGIT))
-    digit = jnp.where(lane < 3, digit, 0)
+    out_ref[:, :width] = (values * scale * gain_ref[...][None, :]).astype(jnp.bfloat16)
+    row = lax.broadcasted_iota(jnp.int32, (rows, LANES), 0)
+    lane = lax.broadcasted_iota(jnp.int32, (rows, LANES), 1)
+    digit = jnp.zeros((rows, LANES), jnp.int32)
+    for r in range(rows):
+        v = ids_ref[r]
+        for i, d in enumerate((v // (DIGIT * DIGIT), (v // DIGIT) % DIGIT, v % DIGIT)):
+            digit = jnp.where((row == r) & (lane == i), d, digit)
     out_ref[:, width:] = digit.astype(jnp.float32).astype(jnp.bfloat16)
 
 
@@ -249,7 +252,12 @@
     return pl.pallas_call(
         pack_kernel,
         out_shape=jax.ShapeDtypeStruct((rows, width + LANES), jnp.bfloat16),
-    )(hidden, norm_gain.reshape(1, width), token_ids.reshape(rows, 1))
+        in_specs=[
+            pl.BlockSpec(memory_space=pltpu.VMEM),
+            pl.BlockSpec(memory_space=pltpu.VMEM),
+            pl.BlockSpec(memory_space=pltpu.SMEM),
+        ],
+    )(hidden, norm_gain, token_ids)
 
 
 def body(hidden, norm_gain, head, token_ids, req_len, req_owner):

time: 117 us -> 114 us (0.974)
  local copies, waits for them, and re-layouts: 4.66 us -> 2.04 us
    reshape x2 -> x0, local copies, waits for them, and re-layouts: 2.63 us -> none  [the longest x1 1.32 us: pack_rows(): token_ids.reshape(rows, 1)]
  transfers between devices with their start and end apart: 1 -> 1, of which waited for: 0 -> 0; matrix products, arithmetic and copies ran while one was open for 4% -> 2% of each run, Pallas kernels for 68% -> 70%
where the time goes in v10:
time: 114 us
  Pallas kernels  96.1 us (84%)
  matrix products  10.3 us (9%)
  other arithmetic  4.7 us (4%)
  local copies, waits for them, and re-layouts  2.04 us (2%)
    pallas_call x1, Pallas kernels, gather_rows(): pl.pallas_call(functools.partial(gather_kernel, sizes, spans), out_shape=...  77.6 us
    pallas_call x1, Pallas kernels, reduce_stats(): pl.pallas_call(functools.partial(reduce_kernel, sizes), out_shape=jax.Sha...  16.8 us
    dot_general x1, matrix products, slice_stats(): logits = jnp.dot(rows, head, preferred_element_type=jnp.float32) / 10.0  10.3 us
    reduce_sum x1, other arithmetic, slice_stats(): total = jnp.sum(expo, axis=1)  2.34 us
  transfers between devices with their start and end apart: 1, of which 0 were waited for; matrix products, arithmetic and copies ran while one was open for 2% of the time, Pallas kernels for 70%

profile of v10, /device:TPU:2, one launch (start us, length us, event | category | flops | bytes accessed | tf_op | source)
XLA Modules:
  0.0 114.1 jit_solution(11562108984629875898)
XLA Ops:
  0.6 0.1 collective-permute-start
  0.7 1.7 %shard_map.77.x_ref = bf16[16,2688]{1,0:T(8,128)(2,1)} custom-call(bf16[16,2560]{1,0:T(8,128)(2,1)} %h_ref.1, f32[2560]{0:T(1024)} %gain_ref.1, s32[16]{0:T(128)} %ids_ref.1), custom_call_target="tpu_custom_call" | custom-call | tf_op jit(solution)/shard_map/pallas_call | solution.py:252
  2.5 0.0 copy-start
  2.5 0.0 copy-start.1
  2.5 0.0 copy-start.2
  2.5 77.6 %shard_map.78 = bf16[4,4,8,16,2688]{4,3,2,1,0:T(8,128)(2,1)} custom-call(bf16[16,2688]{1,0:T(8,128)(2,1)} %shard_map.77.x_ref), custom_call_target="tpu_custom_call" | custom-call | tf_op jit(solution)/shard_map/pallas_call | solution.py:143
  80.1 1.1 slice.37
  81.1 0.2 copy.9
  81.4 0.0 copy-done
  81.4 0.0 copy-done.1
  81.5 0.6 select_reduce_fusion.2
  82.1 0.0 collective-permute-done
  82.1 0.0 copy-done.2
  82.1 10.3 %fusion.13 = (f32[2048]{0:T(1024)S(1)}, f32[2048,576]{0,1:T(8,128)S(1)}) fusion(bf16[2560,288]{0,1:T(8,128)(2,1)S(1)} %collective-permute-done, bf16[2560,288]{0,1:T(8,128)(2,1)S(1)} %copy-done.2, pred[]{:T(512)S(6)} %eq.26, bf16[2048,2688]{1,0:T(8,128)(2,1)} %bitcast.27, pred[576]{0:T(1024)(128)(4,1)S(1)} %broadcast_compare_fusion), kind=kOutput, calls=%fused_computation.31 | convolution fusion | flops 6056605696 | bytes 18162240 | tf_op jit(solution)/shard_map/dot_general | solution.py:21
  92.4 2.3 %fusion.2 = (f32[2048]{0:T(1024)S(1)}, f32[2048]{0:T(1024)S(1)}, f32[2048]{0:T(1024)S(1)}) fusion(f32[2048,576]{0,1:T(8,128)S(1)} %get-tuple-element.8, f32[2048]{0:T(1024)S(1)} %get-tuple-element.7, pred[576]{0:T(1024)(128)(4,1)S(1)} %broadcast_compare_fusion, s32[2048]{0:T(1024)S(1)} %bitcast.28, s32[576]{0:T(1024)S(1)} %iota_add_fusion), kind=kLoop, calls=%fused_computation.5 | loop fusion | flops 10610688 | bytes 4762432 | tf_op jit(solution)/shard_map/reduce_sum | solution.py:25
  94.8 0.6 maximum_bitcast_fusion.a_ref
  95.4 16.8 %shard_map.79 = f32[4,128]{1,0:T(4,128)} custom-call(f32[4,4,512]{2,1,0:T(4,128)} %maximum_bitcast_fusion.a_ref), custom_call_target="tpu_custom_call" | custom-call | tf_op jit(solution)/shard_map/pallas_call | solution.py:219
  112.3 0.7 constant_dynamic-slice_fusion
  113.0 1.1 compare_select_fusion
  (4 shorter events, 0.1 us)
Async XLA Ops:
  0.6 81.4 %collective-permute-start = (bf16[2560,288]{0,1:T(8,128)(2,1)}, bf16[2560,288]{0,1:T(8,128)(2,1)S(1)}, u32[]{:S(2)}, u32[]{:S(2)}) collective-permute-start(bf16[2560,288]{0,1:T(8,128)(2,1)} %param.8), channel_id=1, source_target_pairs={{0,1},{1,0},{2,3},{3,2},{4,5},{5,4},{6,7},{7,6},{8,9},{9,8},{10,11... | collective-permute-start | bytes 4423688 | tf_op jit(solution)/shard_map/ppermute | solution.py:274
  2.5 79.0 %copy-start = (s32[512]{0:T(512)S(1)}, s32[512]{0:T(512)}, u32[]{:S(2)}) copy-start(s32[512]{0:T(512)} %param.10) | copy-start | bytes 6148
  2.5 79.0 %copy-start.1 = (s32[512]{0:T(512)S(1)}, s32[512]{0:T(512)}, u32[]{:S(2)}) copy-start(s32[512]{0:T(512)} %param.11) | copy-start | bytes 6148
  2.5 79.6 %copy-start.2 = (bf16[2560,288]{0,1:T(8,128)(2,1)S(1)}, bf16[2560,288]{0,1:T(8,128)(2,1)}, u32[]{:S(2)}) copy-start(bf16[2560,288]{0,1:T(8,128)(2,1)} %param.8) | copy-start | bytes 4423684

commit v11 on v10

--- a/solution.py
+++ b/solution.py
@@ -132,7 +132,7 @@
 def gather_rows(packed, sizes):
     rows, width = packed.shape
     tiles = width // LANES
-    counts = [tiles * 8 // 21, tiles * 6 // 21]
+    counts = [tiles * 9 // 21, tiles * 5 // 21]
     counts.append(tiles - sum(counts))
     spans, at = [], 0
     for c in counts:

time: 114 us -> 112 us (0.982)
  Pallas kernels: 96.1 us -> 93.7 us
    pallas_call x1, Pallas kernels: 77.6 us -> 74.4 us  [gather_rows(): pl.pallas_call(functools.partial(gather_kernel, sizes, spans), out_shape=...]
  transfers between devices with their start and end apart: 1 -> 1, of which waited for: 0 -> 0; matrix products, arithmetic and copies ran while one was open for 2% -> 2% of each run, Pallas kernels for 70% -> 68%
where the time goes in v11:
time: 112 us
  Pallas kernels  93.7 us (84%)
  matrix products  10.3 us (9%)
  other arithmetic  4.7 us (4%)
  local copies, waits for them, and re-layouts  2.04 us (2%)
    pallas_call x1, Pallas kernels, gather_rows(): pl.pallas_call(functools.partial(gather_kernel, sizes, spans), out_shape=...  74.4 us
    pallas_call x1, Pallas kernels, reduce_stats(): pl.pallas_call(functools.partial(reduce_kernel, sizes), out_shape=jax.Sha...  17.6 us
    dot_general x1, matrix products, slice_stats(): logits = jnp.dot(rows, head, preferred_element_type=jnp.float32) / 10.0  10.3 us
    reduce_sum x1, other arithmetic, slice_stats(): total = jnp.sum(expo, axis=1)  2.34 us
  transfers between devices with their start and end apart: 1, of which 0 were waited for; matrix products, arithmetic and copies ran while one was open for 2% of the time, Pallas kernels for 68%

profile of v11, /device:TPU:2, one launch (start us, length us, event | category | flops | bytes accessed | tf_op | source)
XLA Modules:
  0.0 111.6 jit_solution(18042940990413753325)
XLA Ops:
  0.6 0.1 collective-permute-start
  0.7 1.7 %shard_map.77.x_ref = bf16[16,2688]{1,0:T(8,128)(2,1)} custom-call(bf16[16,2560]{1,0:T(8,128)(2,1)} %h_ref.1, f32[2560]{0:T(1024)} %gain_ref.1, s32[16]{0:T(128)} %ids_ref.1), custom_call_target="tpu_custom_call" | custom-call | tf_op jit(solution)/shard_map/pallas_call | solution.py:252
  2.5 0.0 copy-start
  2.5 0.0 copy-start.1
  2.5 0.0 copy-start.2
  2.5 74.4 %shard_map.78 = bf16[4,4,8,16,2688]{4,3,2,1,0:T(8,128)(2,1)} custom-call(bf16[16,2688]{1,0:T(8,128)(2,1)} %shard_map.77.x_ref), custom_call_target="tpu_custom_call" | custom-call | tf_op jit(solution)/shard_map/pallas_call | solution.py:143
  76.9 1.1 slice.37
  77.9 0.2 copy.9
  78.2 0.0 copy-done
  78.2 0.0 copy-done.1
  78.2 0.6 select_reduce_fusion.2
  78.9 0.0 collective-permute-done
  78.9 0.0 copy-done.2
  78.9 10.3 %fusion.13 = (f32[2048]{0:T(1024)S(1)}, f32[2048,576]{0,1:T(8,128)S(1)}) fusion(bf16[2560,288]{0,1:T(8,128)(2,1)S(1)} %collective-permute-done, bf16[2560,288]{0,1:T(8,128)(2,1)S(1)} %copy-done.2, pred[]{:T(512)S(6)} %eq.26, bf16[2048,2688]{1,0:T(8,128)(2,1)} %bitcast.27, pred[576]{0:T(1024)(128)(4,1)S(1)} %broadcast_compare_fusion), kind=kOutput, calls=%fused_computation.31 | convolution fusion | flops 6056605696 | bytes 18162240 | tf_op jit(solution)/shard_map/dot_general | solution.py:21
  89.2 2.3 %fusion.2 = (f32[2048]{0:T(1024)S(1)}, f32[2048]{0:T(1024)S(1)}, f32[2048]{0:T(1024)S(1)}) fusion(f32[2048,576]{0,1:T(8,128)S(1)} %get-tuple-element.8, f32[2048]{0:T(1024)S(1)} %get-tuple-element.7, pred[576]{0:T(1024)(128)(4,1)S(1)} %broadcast_compare_fusion, s32[2048]{0:T(1024)S(1)} %bitcast.28, s32[576]{0:T(1024)S(1)} %iota_add_fusion), kind=kLoop, calls=%fused_computation.5 | loop fusion | flops 10610688 | bytes 4762432 | tf_op jit(solution)/shard_map/reduce_sum | solution.py:25
  91.6 0.6 maximum_bitcast_fusion.a_ref
  92.2 17.6 %shard_map.79 = f32[4,128]{1,0:T(4,128)} custom-call(f32[4,4,512]{2,1,0:T(4,128)} %maximum_bitcast_fusion.a_ref), custom_call_target="tpu_custom_call" | custom-call | tf_op jit(solution)/shard_map/pallas_call | solution.py:219
  109.8 0.7 constant_dynamic-slice_fusion
  110.6 1.1 compare_select_fusion
  (4 shorter events, 0.1 us)
Async XLA Ops:
  0.6 78.2 %collective-permute-start = (bf16[2560,288]{0,1:T(8,128)(2,1)}, bf16[2560,288]{0,1:T(8,128)(2,1)S(1)}, u32[]{:S(2)}, u32[]{:S(2)}) collective-permute-start(bf16[2560,288]{0,1:T(8,128)(2,1)} %param.8), channel_id=1, source_target_pairs={{0,1},{1,0},{2,3},{3,2},{4,5},{5,4},{6,7},{7,6},{8,9},{9,8},{10,11... | collective-permute-start | bytes 4423688 | tf_op jit(solution)/shard_map/ppermute | solution.py:274
  2.5 75.8 %copy-start = (s32[512]{0:T(512)S(1)}, s32[512]{0:T(512)}, u32[]{:S(2)}) copy-start(s32[512]{0:T(512)} %param.10) | copy-start | bytes 6148
  2.5 75.8 %copy-start.1 = (s32[512]{0:T(512)S(1)}, s32[512]{0:T(512)}, u32[]{:S(2)}) copy-start(s32[512]{0:T(512)} %param.11) | copy-start | bytes 6148
  2.5 76.4 %copy-start.2 = (bf16[2560,288]{0,1:T(8,128)(2,1)S(1)}, bf16[2560,288]{0,1:T(8,128)(2,1)}, u32[]{:S(2)}) copy-start(bf16[2560,288]{0,1:T(8,128)(2,1)} %param.8) | copy-start | bytes 4423684

commit v12 on v11

--- a/solution.py
+++ b/solution.py
@@ -132,7 +132,7 @@
 def gather_rows(packed, sizes):
     rows, width = packed.shape
     tiles = width // LANES
-    counts = [tiles * 9 // 21, tiles * 5 // 21]
+    counts = [tiles * 10 // 21, tiles * 4 // 21]
     counts.append(tiles - sum(counts))
     spans, at = [], 0
     for c in counts:

time: 112 us -> 114 us (1.018)
  Pallas kernels: 93.7 us -> 96.2 us
    pallas_call x1, Pallas kernels: 74.4 us -> 78.2 us  [gather_rows(): pl.pallas_call(functools.partial(gather_kernel, sizes, spans), out_shape=...]
    pallas_call x1, Pallas kernels: 17.6 us -> 16.3 us  [reduce_stats(): pl.pallas_call(functools.partial(reduce_kernel, sizes), out_shape=jax.Sha...]
  transfers between devices with their start and end apart: 1 -> 1, of which waited for: 0 -> 0; matrix products, arithmetic and copies ran while one was open for 2% -> 2% of each run, Pallas kernels for 68% -> 70%
where the time goes in v12:
time: 114 us
  Pallas kernels  96.2 us (84%)
  matrix products  10.3 us (9%)
  other arithmetic  4.7 us (4%)
  local copies, waits for them, and re-layouts  2.04 us (2%)
    pallas_call x1, Pallas kernels, gather_rows(): pl.pallas_call(functools.partial(gather_kernel, sizes, spans), out_shape=...  78.2 us
    pallas_call x1, Pallas kernels, reduce_stats(): pl.pallas_call(functools.partial(reduce_kernel, sizes), out_shape=jax.Sha...  16.3 us
    dot_general x1, matrix products, slice_stats(): logits = jnp.dot(rows, head, preferred_element_type=jnp.float32) / 10.0  10.3 us
    reduce_sum x1, other arithmetic, slice_stats(): total = jnp.sum(expo, axis=1)  2.34 us
  transfers between devices with their start and end apart: 1, of which 0 were waited for; matrix products, arithmetic and copies ran while one was open for 2% of the time, Pallas kernels for 70%

profile of v12, /device:TPU:2, one launch (start us, length us, event | category | flops | bytes accessed | tf_op | source)
XLA Modules:
  0.0 114.2 jit_solution(3807024797187637424)
XLA Ops:
  0.6 0.1 collective-permute-start
  0.7 1.7 %shard_map.77.x_ref = bf16[16,2688]{1,0:T(8,128)(2,1)} custom-call(bf16[16,2560]{1,0:T(8,128)(2,1)} %h_ref.1, f32[2560]{0:T(1024)} %gain_ref.1, s32[16]{0:T(128)} %ids_ref.1), custom_call_target="tpu_custom_call" | custom-call | tf_op jit(solution)/shard_map/pallas_call | solution.py:252
  2.5 0.0 copy-start
  2.5 0.0 copy-start.1
  2.5 0.0 copy-start.2
  2.5 78.2 %shard_map.78 = bf16[4,4,8,16,2688]{4,3,2,1,0:T(8,128)(2,1)} custom-call(bf16[16,2688]{1,0:T(8,128)(2,1)} %shard_map.77.x_ref), custom_call_target="tpu_custom_call" | custom-call | tf_op jit(solution)/shard_map/pallas_call | solution.py:143
  80.7 1.1 slice.37
  81.8 0.2 copy.9
  82.1 0.0 copy-done
  82.1 0.0 copy-done.1
  82.1 0.6 select_reduce_fusion.2
  82.7 0.0 collective-permute-done
  82.7 0.0 copy-done.2
  82.7 10.3 %fusion.13 = (f32[2048]{0:T(1024)S(1)}, f32[2048,576]{0,1:T(8,128)S(1)}) fusion(bf16[2560,288]{0,1:T(8,128)(2,1)S(1)} %collective-permute-done, bf16[2560,288]{0,1:T(8,128)(2,1)S(1)} %copy-done.2, pred[]{:T(512)S(6)} %eq.26, bf16[2048,2688]{1,0:T(8,128)(2,1)} %bitcast.27, pred[576]{0:T(1024)(128)(4,1)S(1)} %broadcast_compare_fusion), kind=kOutput, calls=%fused_computation.31 | convolution fusion | flops 6056605696 | bytes 18162240 | tf_op jit(solution)/shard_map/dot_general | solution.py:21
  93.1 2.3 %fusion.2 = (f32[2048]{0:T(1024)S(1)}, f32[2048]{0:T(1024)S(1)}, f32[2048]{0:T(1024)S(1)}) fusion(f32[2048,576]{0,1:T(8,128)S(1)} %get-tuple-element.8, f32[2048]{0:T(1024)S(1)} %get-tuple-element.7, pred[576]{0:T(1024)(128)(4,1)S(1)} %broadcast_compare_fusion, s32[2048]{0:T(1024)S(1)} %bitcast.28, s32[576]{0:T(1024)S(1)} %iota_add_fusion), kind=kLoop, calls=%fused_computation.5 | loop fusion | flops 10610688 | bytes 4762432 | tf_op jit(solution)/shard_map/reduce_sum | solution.py:25
  95.4 0.6 maximum_bitcast_fusion.a_ref
  96.1 16.3 %shard_map.79 = f32[4,128]{1,0:T(4,128)} custom-call(f32[4,4,512]{2,1,0:T(4,128)} %maximum_bitcast_fusion.a_ref), custom_call_target="tpu_custom_call" | custom-call | tf_op jit(solution)/shard_map/pallas_call | solution.py:219
  112.4 0.7 constant_dynamic-slice_fusion
  113.1 1.1 compare_select_fusion
  (4 shorter events, 0.1 us)
Async XLA Ops:
  0.6 82.1 %collective-permute-start = (bf16[2560,288]{0,1:T(8,128)(2,1)}, bf16[2560,288]{0,1:T(8,128)(2,1)S(1)}, u32[]{:S(2)}, u32[]{:S(2)}) collective-permute-start(bf16[2560,288]{0,1:T(8,128)(2,1)} %param.8), channel_id=1, source_target_pairs={{0,1},{1,0},{2,3},{3,2},{4,5},{5,4},{6,7},{7,6},{8,9},{9,8},{10,11... | collective-permute-start | bytes 4423688 | tf_op jit(solution)/shard_map/ppermute | solution.py:274
  2.5 79.6 %copy-start = (s32[512]{0:T(512)S(1)}, s32[512]{0:T(512)}, u32[]{:S(2)}) copy-start(s32[512]{0:T(512)} %param.10) | copy-start | bytes 6148
  2.5 79.6 %copy-start.1 = (s32[512]{0:T(512)S(1)}, s32[512]{0:T(512)}, u32[]{:S(2)}) copy-start(s32[512]{0:T(512)} %param.11) | copy-start | bytes 6148
  2.5 80.3 %copy-start.2 = (bf16[2560,288]{0,1:T(8,128)(2,1)S(1)}, bf16[2560,288]{0,1:T(8,128)(2,1)}, u32[]{:S(2)}) copy-start(bf16[2560,288]{0,1:T(8,128)(2,1)} %param.8) | copy-start | bytes 4423684

commit v13 on v12

--- a/solution.py
+++ b/solution.py
@@ -132,7 +132,7 @@
 def gather_rows(packed, sizes):
     rows, width = packed.shape
     tiles = width // LANES
-    counts = [tiles * 10 // 21, tiles * 4 // 21]
+    counts = [tiles * 8 // 21, tiles * 5 // 21]
     counts.append(tiles - sum(counts))
     spans, at = [], 0
     for c in counts:

time: 114 us -> 115 us (level)
  no operation moved by 1% of the time
where the time goes in v13:
time: 115 us
  Pallas kernels  97.2 us (85%)
  matrix products  10.3 us (9%)
  other arithmetic  4.7 us (4%)
  local copies, waits for them, and re-layouts  2.04 us (2%)
    pallas_call x1, Pallas kernels, gather_rows(): pl.pallas_call(functools.partial(gather_kernel, sizes, spans), out_shape=...  78.4 us
    pallas_call x1, Pallas kernels, reduce_stats(): pl.pallas_call(functools.partial(reduce_kernel, sizes), out_shape=jax.Sha...  17.1 us
    dot_general x1, matrix products, slice_stats(): logits = jnp.dot(rows, head, preferred_element_type=jnp.float32) / 10.0  10.3 us
    reduce_sum x1, other arithmetic, slice_stats(): total = jnp.sum(expo, axis=1)  2.34 us
  transfers between devices with their start and end apart: 1, of which 0 were waited for; matrix products, arithmetic and copies ran while one was open for 2% of the time, Pallas kernels for 70%

profile of v13, /device:TPU:2, one launch (start us, length us, event | category | flops | bytes accessed | tf_op | source)
XLA Modules:
  0.0 115.1 jit_solution(1659673434512694568)
XLA Ops:
  0.6 0.1 collective-permute-start
  0.7 1.7 %shard_map.77.x_ref = bf16[16,2688]{1,0:T(8,128)(2,1)} custom-call(bf16[16,2560]{1,0:T(8,128)(2,1)} %h_ref.1, f32[2560]{0:T(1024)} %gain_ref.1, s32[16]{0:T(128)} %ids_ref.1), custom_call_target="tpu_custom_call" | custom-call | tf_op jit(solution)/shard_map/pallas_call | solution.py:252
  2.5 0.0 copy-start
  2.5 0.0 copy-start.1
  2.5 0.0 copy-start.2
  2.5 78.4 %shard_map.78 = bf16[4,4,8,16,2688]{4,3,2,1,0:T(8,128)(2,1)} custom-call(bf16[16,2688]{1,0:T(8,128)(2,1)} %shard_map.77.x_ref), custom_call_target="tpu_custom_call" | custom-call | tf_op jit(solution)/shard_map/pallas_call | solution.py:143
  80.9 1.1 slice.37
  81.9 0.2 copy.9
  82.2 0.0 copy-done
  82.2 0.0 copy-done.1
  82.2 0.6 select_reduce_fusion.2
  82.9 0.0 collective-permute-done
  82.9 0.0 copy-done.2
  82.9 10.3 %fusion.13 = (f32[2048]{0:T(1024)S(1)}, f32[2048,576]{0,1:T(8,128)S(1)}) fusion(bf16[2560,288]{0,1:T(8,128)(2,1)S(1)} %collective-permute-done, bf16[2560,288]{0,1:T(8,128)(2,1)S(1)} %copy-done.2, pred[]{:T(512)S(6)} %eq.26, bf16[2048,2688]{1,0:T(8,128)(2,1)} %bitcast.27, pred[576]{0:T(1024)(128)(4,1)S(1)} %broadcast_compare_fusion), kind=kOutput, calls=%fused_computation.31 | convolution fusion | flops 6056605696 | bytes 18162240 | tf_op jit(solution)/shard_map/dot_general | solution.py:21
  93.2 2.3 %fusion.2 = (f32[2048]{0:T(1024)S(1)}, f32[2048]{0:T(1024)S(1)}, f32[2048]{0:T(1024)S(1)}) fusion(f32[2048,576]{0,1:T(8,128)S(1)} %get-tuple-element.8, f32[2048]{0:T(1024)S(1)} %get-tuple-element.7, pred[576]{0:T(1024)(128)(4,1)S(1)} %broadcast_compare_fusion, s32[2048]{0:T(1024)S(1)} %bitcast.28, s32[576]{0:T(1024)S(1)} %iota_add_fusion), kind=kLoop, calls=%fused_computation.5 | loop fusion | flops 10610688 | bytes 4762432 | tf_op jit(solution)/shard_map/reduce_sum | solution.py:25
  95.6 0.6 maximum_bitcast_fusion.a_ref
  96.2 17.1 %shard_map.79 = f32[4,128]{1,0:T(4,128)} custom-call(f32[4,4,512]{2,1,0:T(4,128)} %maximum_bitcast_fusion.a_ref), custom_call_target="tpu_custom_call" | custom-call | tf_op jit(solution)/shard_map/pallas_call | solution.py:219
  113.3 0.7 constant_dynamic-slice_fusion
  114.1 1.1 compare_select_fusion
  (4 shorter events, 0.1 us)
Async XLA Ops:
  0.6 82.2 %collective-permute-start = (bf16[2560,288]{0,1:T(8,128)(2,1)}, bf16[2560,288]{0,1:T(8,128)(2,1)S(1)}, u32[]{:S(2)}, u32[]{:S(2)}) collective-permute-start(bf16[2560,288]{0,1:T(8,128)(2,1)} %param.8), channel_id=1, source_target_pairs={{0,1},{1,0},{2,3},{3,2},{4,5},{5,4},{6,7},{7,6},{8,9},{9,8},{10,11... | collective-permute-start | bytes 4423688 | tf_op jit(solution)/shard_map/ppermute | solution.py:274
  2.5 79.8 %copy-start = (s32[512]{0:T(512)S(1)}, s32[512]{0:T(512)}, u32[]{:S(2)}) copy-start(s32[512]{0:T(512)} %param.10) | copy-start | bytes 6148
  2.5 79.8 %copy-start.1 = (s32[512]{0:T(512)S(1)}, s32[512]{0:T(512)}, u32[]{:S(2)}) copy-start(s32[512]{0:T(512)} %param.11) | copy-start | bytes 6148
  2.5 80.4 %copy-start.2 = (bf16[2560,288]{0,1:T(8,128)(2,1)S(1)}, bf16[2560,288]{0,1:T(8,128)(2,1)}, u32[]{:S(2)}) copy-start(bf16[2560,288]{0,1:T(8,128)(2,1)} %param.8) | copy-start | bytes 4423684

commit v14 on v11

--- a/solution.py
+++ b/solution.py
@@ -278,7 +278,8 @@
 
     gathered = gather_rows(packed, size).reshape(-1, packed.shape[1])
     all_rows = gathered[:, :width]
-    all_ids = decode_ids(gathered[:, width:width + 3])
+    place = jnp.zeros((gathered.shape[1] - width,), jnp.bfloat16).at[:3].set(jnp.array([DIGIT * DIGIT, DIGIT, 1], jnp.bfloat16))
+    all_ids = jnp.dot(gathered[:, width:], place, preferred_element_type=jnp.float32).astype(jnp.int32)
     stats = jnp.stack(slice_stats(all_rows, all_ids, chip_head, col_index, real_cols), axis=0)
 
     parts = jnp.transpose(stats.reshape(4, size["y"], -1), (1, 0, 2))

time: 112 us -> 112 us (level)
  matrix products: 10.3 us -> 11.6 us
  local copies, waits for them, and re-layouts: 2.04 us -> 0.75 us
    dot_general x0 -> x1, matrix products: none -> 1.27 us  [body(): jnp.dot(gathered[:, width:], place, preferred_element_type=jnp.float32)]
where the time goes in v14:
time: 112 us
  Pallas kernels  93.7 us (84%)
  matrix products  11.6 us (10%)
  other arithmetic  4.68 us (4%)
    pallas_call x1, Pallas kernels, gather_rows(): pl.pallas_call(functools.partial(gather_kernel, sizes, spans), out_shape=...  74.4 us
    pallas_call x1, Pallas kernels, reduce_stats(): pl.pallas_call(functools.partial(reduce_kernel, sizes), out_shape=jax.Sha...  17.6 us
    dot_general x1, matrix products, slice_stats(): logits = jnp.dot(rows, head, preferred_element_type=jnp.float32) / 10.0  10.3 us
    reduce_sum x1, other arithmetic, slice_stats(): total = jnp.sum(expo, axis=1)  2.34 us
  transfers between devices with their start and end apart: 1, of which 0 were waited for; matrix products, arithmetic and copies ran while one was open for 2% of the time, Pallas kernels for 68%

profile of v14, /device:TPU:2, one launch (start us, length us, event | category | flops | bytes accessed | tf_op | source)
XLA Modules:
  0.0 111.6 jit_solution(16536693554028844487)
XLA Ops:
  0.6 0.1 collective-permute-start
  0.7 1.7 %shard_map.86.x_ref = bf16[16,2688]{1,0:T(8,128)(2,1)} custom-call(bf16[16,2560]{1,0:T(8,128)(2,1)} %h_ref.1, f32[2560]{0:T(1024)} %gain_ref.1, s32[16]{0:T(128)} %ids_ref.1), custom_call_target="tpu_custom_call" | custom-call | tf_op jit(solution)/shard_map/pallas_call | solution.py:252
  2.5 0.0 copy-start.3
  2.5 0.0 copy-start
  2.5 0.0 copy-start.1
  2.5 0.0 copy-start.2
  2.5 74.4 %shard_map.87 = bf16[4,4,8,16,2688]{4,3,2,1,0:T(8,128)(2,1)} custom-call(bf16[16,2688]{1,0:T(8,128)(2,1)} %shard_map.86.x_ref), custom_call_target="tpu_custom_call" | custom-call | tf_op jit(solution)/shard_map/pallas_call | solution.py:143
  76.9 0.0 copy-done.3
  76.9 1.3 %fusion.11 = f32[1,2048]{1,0:T(1,128)S(1)} fusion(bf16[128,1]{0,1:T(2,128)(2,1)S(1)} %copy-done.3, bf16[2048,2688]{1,0:T(8,128)(2,1)} %bitcast.28), kind=kOutput, calls=%fused_computation.14 | convolution fusion | flops 524288 | bytes 532736 | tf_op jit(solution)/shard_map/dot_general | solution.py:282
  78.2 0.0 copy-done
  78.2 0.0 copy-done.1
  78.2 0.6 select_reduce_fusion.2
  78.8 0.0 collective-permute-done
  78.8 0.0 copy-done.2
  78.8 10.3 %fusion.14 = (f32[2048]{0:T(1024)S(1)}, f32[2048,576]{0,1:T(8,128)S(1)}) fusion(bf16[2560,288]{0,1:T(8,128)(2,1)S(1)} %collective-permute-done, bf16[2560,288]{0,1:T(8,128)(2,1)S(1)} %copy-done.2, pred[]{:T(512)S(6)} %eq.24, bf16[2048,2688]{1,0:T(8,128)(2,1)} %bitcast.29, pred[576]{0:T(1024)(128)(4,1)S(1)} %broadcast_compare_fusion), kind=kOutput, calls=%fused_computation.29 | convolution fusion | flops 6056605696 | bytes 18162240 | tf_op jit(solution)/shard_map/dot_general | solution.py:21
  89.2 2.3 %fusion.2 = (f32[2048]{0:T(1024)S(1)}, f32[2048]{0:T(1024)S(1)}, f32[2048]{0:T(1024)S(1)}) fusion(f32[2048,576]{0,1:T(8,128)S(1)} %get-tuple-element.20, f32[2048]{0:T(1024)S(1)} %get-tuple-element.19, pred[576]{0:T(1024)(128)(4,1)S(1)} %broadcast_compare_fusion, s32[2048]{0:T(1024)S(1)} %convert_element_type.3, s32[576]{0:T(1024)S(1)} %iota_add_fusion), kind=kLoop, calls=%fused_computation.5 | loop fusion | flops 10610688 | bytes 4762432 | tf_op jit(solution)/shard_map/reduce_sum | solution.py:25
  91.5 0.6 maximum_bitcast_fusion.a_ref
  92.2 17.6 %shard_map.88 = f32[4,128]{1,0:T(4,128)} custom-call(f32[4,4,512]{2,1,0:T(4,128)} %maximum_bitcast_fusion.a_ref), custom_call_target="tpu_custom_call" | custom-call | tf_op jit(solution)/shard_map/pallas_call | solution.py:219
  109.8 0.7 constant_dynamic-slice_fusion
  110.5 1.1 compare_select_fusion
  (3 shorter events, 0.0 us)
Async XLA Ops:
  0.6 78.2 %collective-permute-start = (bf16[2560,288]{0,1:T(8,128)(2,1)}, bf16[2560,288]{0,1:T(8,128)(2,1)S(1)}, u32[]{:S(2)}, u32[]{:S(2)}) collective-permute-start(bf16[2560,288]{0,1:T(8,128)(2,1)} %param.11), channel_id=1, source_target_pairs={{0,1},{1,0},{2,3},{3,2},{4,5},{5,4},{6,7},{7,6},{8,9},{9,8},{10,11... | collective-permute-start | bytes 4423688 | tf_op jit(solution)/shard_map/ppermute | solution.py:274
  2.5 74.4 %copy-start.3 = (bf16[128,1]{0,1:T(2,128)(2,1)S(1)}, bf16[128,1]{0,1:T(2,128)(2,1)}, u32[]{:S(2)}) copy-start(bf16[128,1]{0,1:T(2,128)(2,1)} %constant.73) | copy-start | bytes 772
  2.5 75.7 %copy-start = (s32[512]{0:T(512)S(1)}, s32[512]{0:T(512)}, u32[]{:S(2)}) copy-start(s32[512]{0:T(512)} %param.13) | copy-start | bytes 6148
  2.5 75.7 %copy-start.1 = (s32[512]{0:T(512)S(1)}, s32[512]{0:T(512)}, u32[]{:S(2)}) copy-start(s32[512]{0:T(512)} %param.14) | copy-start | bytes 6148
  2.5 76.3 %copy-start.2 = (bf16[2560,288]{0,1:T(8,128)(2,1)S(1)}, bf16[2560,288]{0,1:T(8,128)(2,1)}, u32[]{:S(2)}) copy-start(bf16[2560,288]{0,1:T(8,128)(2,1)} %param.11) | copy-start | bytes 4423684

commit v15 on v11

--- a/solution.py
+++ b/solution.py
@@ -113,11 +113,11 @@
     steps = len(plans[0])
     sends = []
     for g in range(steps):
-        for s in range(len(STREAMS)):
+        for s in (1, 2, 0):
             if g > 0:
                 for copy in step_copies(s, g - 1, False):
                     copy.wait_recv()
-            if g == 1 and s == 0:
+            if g == 1 and s == 1:
                 own.wait()
             for copy in step_copies(s, g, True):
                 copy.start()

time: 112 us -> 120 us (1.071)
  Pallas kernels: 93.7 us -> 101 us
    pallas_call x1, Pallas kernels: 74.4 us -> 81.3 us  [gather_rows(): pl.pallas_call(functools.partial(gather_kernel, sizes, spans), out_shape=...]
  transfers between devices with their start and end apart: 1 -> 1, of which waited for: 0 -> 0; matrix products, arithmetic and copies ran while one was open for 2% -> 2% of each run, Pallas kernels for 68% -> 70%
where the time goes in v15:
time: 120 us; the launch traced here: 119 us
  Pallas kernels  101 us (84%)
  matrix products  10.3 us (9%)
  other arithmetic  4.7 us (4%)
  local copies, waits for them, and re-layouts  2.04 us (2%)
    pallas_call x1, Pallas kernels, gather_rows(): pl.pallas_call(functools.partial(gather_kernel, sizes, spans), out_shape=...  81.3 us
    pallas_call x1, Pallas kernels, reduce_stats(): pl.pallas_call(functools.partial(reduce_kernel, sizes), out_shape=jax.Sha...  18.2 us
    dot_general x1, matrix products, slice_stats(): logits = jnp.dot(rows, head, preferred_element_type=jnp.float32) / 10.0  10.3 us
  transfers between devices with their start and end apart: 1, of which 0 were waited for; matrix products, arithmetic and copies ran while one was open for 2% of the time, Pallas kernels for 70%

profile of v15, /device:TPU:2, one launch (start us, length us, event | category | flops | bytes accessed | tf_op | source)
XLA Modules:
  0.0 119.2 jit_solution(9546858056984151783)
XLA Ops:
  0.6 0.1 collective-permute-start
  0.7 1.7 %shard_map.77.x_ref = bf16[16,2688]{1,0:T(8,128)(2,1)} custom-call(bf16[16,2560]{1,0:T(8,128)(2,1)} %h_ref.1, f32[2560]{0:T(1024)} %gain_ref.1, s32[16]{0:T(128)} %ids_ref.1), custom_call_target="tpu_custom_call" | custom-call | tf_op jit(solution)/shard_map/pallas_call | solution.py:252
  2.5 0.0 copy-start
  2.5 0.0 copy-start.1
  2.5 0.0 copy-start.2
  2.5 81.3 %shard_map.78 = bf16[4,4,8,16,2688]{4,3,2,1,0:T(8,128)(2,1)} custom-call(bf16[16,2688]{1,0:T(8,128)(2,1)} %shard_map.77.x_ref), custom_call_target="tpu_custom_call" | custom-call | tf_op jit(solution)/shard_map/pallas_call | solution.py:143
  83.8 1.1 slice.37
  84.9 0.2 copy.9
  85.2 0.0 copy-done
  85.2 0.0 copy-done.1
  85.2 0.6 select_reduce_fusion.2
  85.8 0.0 collective-permute-done
  85.8 0.0 copy-done.2
  85.9 10.3 %fusion.13 = (f32[2048]{0:T(1024)S(1)}, f32[2048,576]{0,1:T(8,128)S(1)}) fusion(bf16[2560,288]{0,1:T(8,128)(2,1)S(1)} %collective-permute-done, bf16[2560,288]{0,1:T(8,128)(2,1)S(1)} %copy-done.2, pred[]{:T(512)S(6)} %eq.26, bf16[2048,2688]{1,0:T(8,128)(2,1)} %bitcast.27, pred[576]{0:T(1024)(128)(4,1)S(1)} %broadcast_compare_fusion), kind=kOutput, calls=%fused_computation.31 | convolution fusion | flops 6056605696 | bytes 18162240 | tf_op jit(solution)/shard_map/dot_general | solution.py:21
  96.2 2.3 %fusion.2 = (f32[2048]{0:T(1024)S(1)}, f32[2048]{0:T(1024)S(1)}, f32[2048]{0:T(1024)S(1)}) fusion(f32[2048,576]{0,1:T(8,128)S(1)} %get-tuple-element.8, f32[2048]{0:T(1024)S(1)} %get-tuple-element.7, pred[576]{0:T(1024)(128)(4,1)S(1)} %broadcast_compare_fusion, s32[2048]{0:T(1024)S(1)} %bitcast.28, s32[576]{0:T(1024)S(1)} %iota_add_fusion), kind=kLoop, calls=%fused_computation.5 | loop fusion | flops 10610688 | bytes 4762432 | tf_op jit(solution)/shard_map/reduce_sum | solution.py:25
  98.6 0.6 maximum_bitcast_fusion.a_ref
  99.2 18.2 %shard_map.79 = f32[4,128]{1,0:T(4,128)} custom-call(f32[4,4,512]{2,1,0:T(4,128)} %maximum_bitcast_fusion.a_ref), custom_call_target="tpu_custom_call" | custom-call | tf_op jit(solution)/shard_map/pallas_call | solution.py:219
  117.4 0.7 constant_dynamic-slice_fusion
  118.2 1.1 compare_select_fusion
  (4 shorter events, 0.1 us)
Async XLA Ops:
  0.6 85.2 %collective-permute-start = (bf16[2560,288]{0,1:T(8,128)(2,1)}, bf16[2560,288]{0,1:T(8,128)(2,1)S(1)}, u32[]{:S(2)}, u32[]{:S(2)}) collective-permute-start(bf16[2560,288]{0,1:T(8,128)(2,1)} %param.8), channel_id=1, source_target_pairs={{0,1},{1,0},{2,3},{3,2},{4,5},{5,4},{6,7},{7,6},{8,9},{9,8},{10,11... | collective-permute-start | bytes 4423688 | tf_op jit(solution)/shard_map/ppermute | solution.py:274
  2.5 82.7 %copy-start = (s32[512]{0:T(512)S(1)}, s32[512]{0:T(512)}, u32[]{:S(2)}) copy-start(s32[512]{0:T(512)} %param.10) | copy-start | bytes 6148
  2.5 82.7 %copy-start.1 = (s32[512]{0:T(512)S(1)}, s32[512]{0:T(512)}, u32[]{:S(2)}) copy-start(s32[512]{0:T(512)} %param.11) | copy-start | bytes 6148
  2.5 83.4 %copy-start.2 = (bf16[2560,288]{0,1:T(8,128)(2,1)S(1)}, bf16[2560,288]{0,1:T(8,128)(2,1)}, u32[]{:S(2)}) copy-start(bf16[2560,288]{0,1:T(8,128)(2,1)} %param.8) | copy-start | bytes 4423684

commit v16 on v11

--- a/solution.py
+++ b/solution.py
@@ -113,7 +113,7 @@
     steps = len(plans[0])
     sends = []
     for g in range(steps):
-        for s in range(len(STREAMS)):
+        for s in (0, 2, 1):
             if g > 0:
                 for copy in step_copies(s, g - 1, False):
                     copy.wait_recv()

time: 112 us -> 112 us (level)
  no operation moved by 1% of the time
where the time goes in v16:
time: 112 us
  Pallas kernels  93.6 us (84%)
  matrix products  10.3 us (9%)
  other arithmetic  4.7 us (4%)
  local copies, waits for them, and re-layouts  2.04 us (2%)
    pallas_call x1, Pallas kernels, gather_rows(): pl.pallas_call(functools.partial(gather_kernel, sizes, spans), out_shape=...  74.3 us
    pallas_call x1, Pallas kernels, reduce_stats(): pl.pallas_call(functools.partial(reduce_kernel, sizes), out_shape=jax.Sha...  17.6 us
    dot_general x1, matrix products, slice_stats(): logits = jnp.dot(rows, head, preferred_element_type=jnp.float32) / 10.0  10.3 us
    reduce_sum x1, other arithmetic, slice_stats(): total = jnp.sum(expo, axis=1)  2.34 us
  transfers between devices with their start and end apart: 1, of which 0 were waited for; matrix products, arithmetic and copies ran while one was open for 2% of the time, Pallas kernels for 68%

profile of v16, /device:TPU:2, one launch (start us, length us, event | category | flops | bytes accessed | tf_op | source)
XLA Modules:
  0.0 111.6 jit_solution(4463994767994846331)
XLA Ops:
  0.6 0.1 collective-permute-start
  0.7 1.7 %shard_map.77.x_ref = bf16[16,2688]{1,0:T(8,128)(2,1)} custom-call(bf16[16,2560]{1,0:T(8,128)(2,1)} %h_ref.1, f32[2560]{0:T(1024)} %gain_ref.1, s32[16]{0:T(128)} %ids_ref.1), custom_call_target="tpu_custom_call" | custom-call | tf_op jit(solution)/shard_map/pallas_call | solution.py:252
  2.5 0.0 copy-start
  2.5 0.0 copy-start.1
  2.5 0.0 copy-start.2
  2.5 74.3 %shard_map.78 = bf16[4,4,8,16,2688]{4,3,2,1,0:T(8,128)(2,1)} custom-call(bf16[16,2688]{1,0:T(8,128)(2,1)} %shard_map.77.x_ref), custom_call_target="tpu_custom_call" | custom-call | tf_op jit(solution)/shard_map/pallas_call | solution.py:143
  76.8 1.1 slice.37
  77.9 0.2 copy.9
  78.2 0.0 copy-done
  78.2 0.0 copy-done.1
  78.2 0.6 select_reduce_fusion.2
  78.8 0.0 collective-permute-done
  78.8 0.0 copy-done.2
  78.8 10.3 %fusion.13 = (f32[2048]{0:T(1024)S(1)}, f32[2048,576]{0,1:T(8,128)S(1)}) fusion(bf16[2560,288]{0,1:T(8,128)(2,1)S(1)} %collective-permute-done, bf16[2560,288]{0,1:T(8,128)(2,1)S(1)} %copy-done.2, pred[]{:T(512)S(6)} %eq.26, bf16[2048,2688]{1,0:T(8,128)(2,1)} %bitcast.27, pred[576]{0:T(1024)(128)(4,1)S(1)} %broadcast_compare_fusion), kind=kOutput, calls=%fused_computation.31 | convolution fusion | flops 6056605696 | bytes 18162240 | tf_op jit(solution)/shard_map/dot_general | solution.py:21
  89.2 2.3 %fusion.2 = (f32[2048]{0:T(1024)S(1)}, f32[2048]{0:T(1024)S(1)}, f32[2048]{0:T(1024)S(1)}) fusion(f32[2048,576]{0,1:T(8,128)S(1)} %get-tuple-element.8, f32[2048]{0:T(1024)S(1)} %get-tuple-element.7, pred[576]{0:T(1024)(128)(4,1)S(1)} %broadcast_compare_fusion, s32[2048]{0:T(1024)S(1)} %bitcast.28, s32[576]{0:T(1024)S(1)} %iota_add_fusion), kind=kLoop, calls=%fused_computation.5 | loop fusion | flops 10610688 | bytes 4762432 | tf_op jit(solution)/shard_map/reduce_sum | solution.py:25
  91.5 0.6 maximum_bitcast_fusion.a_ref
  92.2 17.6 %shard_map.79 = f32[4,128]{1,0:T(4,128)} custom-call(f32[4,4,512]{2,1,0:T(4,128)} %maximum_bitcast_fusion.a_ref), custom_call_target="tpu_custom_call" | custom-call | tf_op jit(solution)/shard_map/pallas_call | solution.py:219
  109.8 0.7 constant_dynamic-slice_fusion
  110.5 1.1 compare_select_fusion
  (4 shorter events, 0.1 us)
Async XLA Ops:
  0.6 78.2 %collective-permute-start = (bf16[2560,288]{0,1:T(8,128)(2,1)}, bf16[2560,288]{0,1:T(8,128)(2,1)S(1)}, u32[]{:S(2)}, u32[]{:S(2)}) collective-permute-start(bf16[2560,288]{0,1:T(8,128)(2,1)} %param.8), channel_id=1, source_target_pairs={{0,1},{1,0},{2,3},{3,2},{4,5},{5,4},{6,7},{7,6},{8,9},{9,8},{10,11... | collective-permute-start | bytes 4423688 | tf_op jit(solution)/shard_map/ppermute | solution.py:274
  2.5 75.7 %copy-start = (s32[512]{0:T(512)S(1)}, s32[512]{0:T(512)}, u32[]{:S(2)}) copy-start(s32[512]{0:T(512)} %param.10) | copy-start | bytes 6148
  2.5 75.7 %copy-start.1 = (s32[512]{0:T(512)S(1)}, s32[512]{0:T(512)}, u32[]{:S(2)}) copy-start(s32[512]{0:T(512)} %param.11) | copy-start | bytes 6148
  2.5 76.3 %copy-start.2 = (bf16[2560,288]{0,1:T(8,128)(2,1)S(1)}, bf16[2560,288]{0,1:T(8,128)(2,1)}, u32[]{:S(2)}) copy-start(bf16[2560,288]{0,1:T(8,128)(2,1)} %param.8) | copy-start | bytes 4423684

commit v17 on v13

--- a/solution.py
+++ b/solution.py
@@ -132,7 +132,7 @@
 def gather_rows(packed, sizes):
     rows, width = packed.shape
     tiles = width // LANES
-    counts = [tiles * 8 // 21, tiles * 5 // 21]
+    counts = [tiles * 9 // 21, tiles * 4 // 21]
     counts.append(tiles - sum(counts))
     spans, at = [], 0
     for c in counts:

time: 115 us -> 113 us (0.983)
  Pallas kernels: 97.2 us -> 94.5 us
    pallas_call x1, Pallas kernels: 78.4 us -> 75.9 us  [gather_rows(): pl.pallas_call(functools.partial(gather_kernel, sizes, spans), out_shape=...]
  transfers between devices with their start and end apart: 1 -> 1, of which waited for: 0 -> 0; matrix products, arithmetic and copies ran while one was open for 2% -> 2% of each run, Pallas kernels for 70% -> 69%
where the time goes in v17:
time: 113 us; the launch traced here: 112 us
  Pallas kernels  94.5 us (84%)
  matrix products  10.3 us (9%)
  other arithmetic  4.7 us (4%)
  local copies, waits for them, and re-layouts  2.04 us (2%)
    pallas_call x1, Pallas kernels, gather_rows(): pl.pallas_call(functools.partial(gather_kernel, sizes, spans), out_shape=...  75.9 us
    pallas_call x1, Pallas kernels, reduce_stats(): pl.pallas_call(functools.partial(reduce_kernel, sizes), out_shape=jax.Sha...  16.8 us
    dot_general x1, matrix products, slice_stats(): logits = jnp.dot(rows, head, preferred_element_type=jnp.float32) / 10.0  10.3 us
    reduce_sum x1, other arithmetic, slice_stats(): total = jnp.sum(expo, axis=1)  2.34 us
  transfers between devices with their start and end apart: 1, of which 0 were waited for; matrix products, arithmetic and copies ran while one was open for 2% of the time, Pallas kernels for 69%

profile of v17, /device:TPU:2, one launch (start us, length us, event | category | flops | bytes accessed | tf_op | source)
XLA Modules:
  0.0 112.4 jit_solution(16159343931610424530)
XLA Ops:
  0.6 0.1 collective-permute-start
  0.7 1.7 %shard_map.77.x_ref = bf16[16,2688]{1,0:T(8,128)(2,1)} custom-call(bf16[16,2560]{1,0:T(8,128)(2,1)} %h_ref.1, f32[2560]{0:T(1024)} %gain_ref.1, s32[16]{0:T(128)} %ids_ref.1), custom_call_target="tpu_custom_call" | custom-call | tf_op jit(solution)/shard_map/pallas_call | solution.py:252
  2.5 0.0 copy-start
  2.5 0.0 copy-start.1
  2.5 0.0 copy-start.2
  2.5 75.9 %shard_map.78 = bf16[4,4,8,16,2688]{4,3,2,1,0:T(8,128)(2,1)} custom-call(bf16[16,2688]{1,0:T(8,128)(2,1)} %shard_map.77.x_ref), custom_call_target="tpu_custom_call" | custom-call | tf_op jit(solution)/shard_map/pallas_call | solution.py:143
  78.4 1.1 slice.37
  79.5 0.2 copy.9
  79.8 0.0 copy-done
  79.8 0.0 copy-done.1
  79.8 0.6 select_reduce_fusion.2
  80.4 0.0 collective-permute-done
  80.4 0.0 copy-done.2
  80.4 10.3 %fusion.13 = (f32[2048]{0:T(1024)S(1)}, f32[2048,576]{0,1:T(8,128)S(1)}) fusion(bf16[2560,288]{0,1:T(8,128)(2,1)S(1)} %collective-permute-done, bf16[2560,288]{0,1:T(8,128)(2,1)S(1)} %copy-done.2, pred[]{:T(512)S(6)} %eq.26, bf16[2048,2688]{1,0:T(8,128)(2,1)} %bitcast.27, pred[576]{0:T(1024)(128)(4,1)S(1)} %broadcast_compare_fusion), kind=kOutput, calls=%fused_computation.31 | convolution fusion | flops 6056605696 | bytes 18162240 | tf_op jit(solution)/shard_map/dot_general | solution.py:21
  90.8 2.3 %fusion.2 = (f32[2048]{0:T(1024)S(1)}, f32[2048]{0:T(1024)S(1)}, f32[2048]{0:T(1024)S(1)}) fusion(f32[2048,576]{0,1:T(8,128)S(1)} %get-tuple-element.8, f32[2048]{0:T(1024)S(1)} %get-tuple-element.7, pred[576]{0:T(1024)(128)(4,1)S(1)} %broadcast_compare_fusion, s32[2048]{0:T(1024)S(1)} %bitcast.28, s32[576]{0:T(1024)S(1)} %iota_add_fusion), kind=kLoop, calls=%fused_computation.5 | loop fusion | flops 10610688 | bytes 4762432 | tf_op jit(solution)/shard_map/reduce_sum | solution.py:25
  93.1 0.6 maximum_bitcast_fusion.a_ref
  93.8 16.8 %shard_map.79 = f32[4,128]{1,0:T(4,128)} custom-call(f32[4,4,512]{2,1,0:T(4,128)} %maximum_bitcast_fusion.a_ref), custom_call_target="tpu_custom_call" | custom-call | tf_op jit(solution)/shard_map/pallas_call | solution.py:219
  110.6 0.7 constant_dynamic-slice_fusion
  111.3 1.1 compare_select_fusion
  (4 shorter events, 0.1 us)
Async XLA Ops:
  0.6 79.8 %collective-permute-start = (bf16[2560,288]{0,1:T(8,128)(2,1)}, bf16[2560,288]{0,1:T(8,128)(2,1)S(1)}, u32[]{:S(2)}, u32[]{:S(2)}) collective-permute-start(bf16[2560,288]{0,1:T(8,128)(2,1)} %param.8), channel_id=1, source_target_pairs={{0,1},{1,0},{2,3},{3,2},{4,5},{5,4},{6,7},{7,6},{8,9},{9,8},{10,11... | collective-permute-start | bytes 4423688 | tf_op jit(solution)/shard_map/ppermute | solution.py:274
  2.5 77.3 %copy-start = (s32[512]{0:T(512)S(1)}, s32[512]{0:T(512)}, u32[]{:S(2)}) copy-start(s32[512]{0:T(512)} %param.10) | copy-start | bytes 6148
  2.5 77.3 %copy-start.1 = (s32[512]{0:T(512)S(1)}, s32[512]{0:T(512)}, u32[]{:S(2)}) copy-start(s32[512]{0:T(512)} %param.11) | copy-start | bytes 6148
  2.5 77.9 %copy-start.2 = (bf16[2560,288]{0,1:T(8,128)(2,1)S(1)}, bf16[2560,288]{0,1:T(8,128)(2,1)}, u32[]{:S(2)}) copy-start(bf16[2560,288]{0,1:T(8,128)(2,1)} %param.8) | copy-start | bytes 4423684

commit v18 on v11

--- a/solution.py
+++ b/solution.py
@@ -113,13 +113,20 @@
     steps = len(plans[0])
     sends = []
     for g in range(steps):
+        if g == 1:
+            own.wait()
         for s in range(len(STREAMS)):
+            out = step_copies(s, g, True)
+            if g > 0 and plans[s][g][0] == plans[s][g - 1][0]:
+                for arrived, copy in zip(step_copies(s, g - 1, False), out):
+                    arrived.wait_recv()
+                    copy.start()
+                    sends.append(copy)
+                continue
             if g > 0:
                 for copy in step_copies(s, g - 1, False):
                     copy.wait_recv()
-            if g == 1 and s == 0:
-                own.wait()
-            for copy in step_copies(s, g, True):
+            for copy in out:
                 copy.start()
                 sends.append(copy)
     for s in range(len(STREAMS)):

time: 112 us -> 112 us (level)
  no operation moved by 1% of the time
where the time goes in v18:
time: 112 us; the launch traced here: 111 us
  Pallas kernels  93.3 us (83%)
  matrix products  10.3 us (9%)
  other arithmetic  4.7 us (4%)
  local copies, waits for them, and re-layouts  2.04 us (2%)
    pallas_call x1, Pallas kernels, gather_rows(): pl.pallas_call(functools.partial(gather_kernel, sizes, spans), out_shape=...  74.4 us
    pallas_call x1, Pallas kernels, reduce_stats(): pl.pallas_call(functools.partial(reduce_kernel, sizes), out_shape=jax.Sha...  17.2 us
    dot_general x1, matrix products, slice_stats(): logits = jnp.dot(rows, head, preferred_element_type=jnp.float32) / 10.0  10.3 us
    reduce_sum x1, other arithmetic, slice_stats(): total = jnp.sum(expo, axis=1)  2.34 us
  transfers between devices with their start and end apart: 1, of which 0 were waited for; matrix products, arithmetic and copies ran while one was open for 2% of the time, Pallas kernels for 68%

profile of v18, /device:TPU:2, one launch (start us, length us, event | category | flops | bytes accessed | tf_op | source)
XLA Modules:
  0.0 111.3 jit_solution(3477642504122318027)
XLA Ops:
  0.6 0.1 collective-permute-start
  0.7 1.7 %shard_map.77.x_ref = bf16[16,2688]{1,0:T(8,128)(2,1)} custom-call(bf16[16,2560]{1,0:T(8,128)(2,1)} %h_ref.1, f32[2560]{0:T(1024)} %gain_ref.1, s32[16]{0:T(128)} %ids_ref.1), custom_call_target="tpu_custom_call" | custom-call | tf_op jit(solution)/shard_map/pallas_call | solution.py:259
  2.5 0.0 copy-start
  2.5 0.0 copy-start.1
  2.5 0.0 copy-start.2
  2.5 74.4 %shard_map.78 = bf16[4,4,8,16,2688]{4,3,2,1,0:T(8,128)(2,1)} custom-call(bf16[16,2688]{1,0:T(8,128)(2,1)} %shard_map.77.x_ref), custom_call_target="tpu_custom_call" | custom-call | tf_op jit(solution)/shard_map/pallas_call | solution.py:150
  76.9 1.1 slice.37
  78.0 0.2 copy.9
  78.3 0.0 copy-done
  78.3 0.0 copy-done.1
  78.3 0.6 select_reduce_fusion.2
  78.9 0.0 collective-permute-done
  78.9 0.0 copy-done.2
  79.0 10.3 %fusion.13 = (f32[2048]{0:T(1024)S(1)}, f32[2048,576]{0,1:T(8,128)S(1)}) fusion(bf16[2560,288]{0,1:T(8,128)(2,1)S(1)} %collective-permute-done, bf16[2560,288]{0,1:T(8,128)(2,1)S(1)} %copy-done.2, pred[]{:T(512)S(6)} %eq.26, bf16[2048,2688]{1,0:T(8,128)(2,1)} %bitcast.27, pred[576]{0:T(1024)(128)(4,1)S(1)} %broadcast_compare_fusion), kind=kOutput, calls=%fused_computation.31 | convolution fusion | flops 6056605696 | bytes 18162240 | tf_op jit(solution)/shard_map/dot_general | solution.py:21
  89.3 2.3 %fusion.2 = (f32[2048]{0:T(1024)S(1)}, f32[2048]{0:T(1024)S(1)}, f32[2048]{0:T(1024)S(1)}) fusion(f32[2048,576]{0,1:T(8,128)S(1)} %get-tuple-element.8, f32[2048]{0:T(1024)S(1)} %get-tuple-element.7, pred[576]{0:T(1024)(128)(4,1)S(1)} %broadcast_compare_fusion, s32[2048]{0:T(1024)S(1)} %bitcast.28, s32[576]{0:T(1024)S(1)} %iota_add_fusion), kind=kLoop, calls=%fused_computation.5 | loop fusion | flops 10610688 | bytes 4762432 | tf_op jit(solution)/shard_map/reduce_sum | solution.py:25
  91.7 0.6 maximum_bitcast_fusion.a_ref
  92.3 17.2 %shard_map.79 = f32[4,128]{1,0:T(4,128)} custom-call(f32[4,4,512]{2,1,0:T(4,128)} %maximum_bitcast_fusion.a_ref), custom_call_target="tpu_custom_call" | custom-call | tf_op jit(solution)/shard_map/pallas_call | solution.py:226
  109.5 0.7 constant_dynamic-slice_fusion
  110.2 1.1 compare_select_fusion
  (4 shorter events, 0.1 us)
Async XLA Ops:
  0.6 78.3 %collective-permute-start = (bf16[2560,288]{0,1:T(8,128)(2,1)}, bf16[2560,288]{0,1:T(8,128)(2,1)S(1)}, u32[]{:S(2)}, u32[]{:S(2)}) collective-permute-start(bf16[2560,288]{0,1:T(8,128)(2,1)} %param.8), channel_id=1, source_target_pairs={{0,1},{1,0},{2,3},{3,2},{4,5},{5,4},{6,7},{7,6},{8,9},{9,8},{10,11... | collective-permute-start | bytes 4423688 | tf_op jit(solution)/shard_map/ppermute | solution.py:281
  2.5 75.8 %copy-start = (s32[512]{0:T(512)S(1)}, s32[512]{0:T(512)}, u32[]{:S(2)}) copy-start(s32[512]{0:T(512)} %param.10) | copy-start | bytes 6148
  2.5 75.8 %copy-start.1 = (s32[512]{0:T(512)S(1)}, s32[512]{0:T(512)}, u32[]{:S(2)}) copy-start(s32[512]{0:T(512)} %param.11) | copy-start | bytes 6148
  2.5 76.5 %copy-start.2 = (bf16[2560,288]{0,1:T(8,128)(2,1)S(1)}, bf16[2560,288]{0,1:T(8,128)(2,1)}, u32[]{:S(2)}) copy-start(bf16[2560,288]{0,1:T(8,128)(2,1)} %param.8) | copy-start | bytes 4423684

commit v19 on v11

--- a/solution.py
+++ b/solution.py
@@ -163,70 +163,73 @@
     return jnp.stack([top, total, weighted, picked], axis=0)
 
 
-def reduce_kernel(sizes, a_ref, out_ref, r1, c1, r2, c2, r3, send_sem, recv_sem):
+def reduce_kernel(sizes, a_ref, out_ref, r1, c1, r2, send_sem, recv_sem):
     pos = {a: lax.axis_index(a) for a in AXES}
-
-    def peer(axis, k):
+    ny, nx, nz = sizes["y"], sizes["x"], sizes["z"]
+
+    def peer(offsets):
         at = dict(pos)
-        at[axis] = lax.rem(pos[axis] + k, sizes[axis])
+        for a, k in offsets.items():
+            at[a] = lax.rem(pos[a] + k, sizes[a])
         return tuple(at[a] for a in AXES)
 
+    plane = [(ky, kx) for ky in range(ny) for kx in range(nx) if (ky, kx) != (0, 0)]
     barrier = pltpu.get_barrier_semaphore()
-    count = 0
-    for axis in CHIP_AXES:
-        for k in range(1, sizes[axis]):
-            pl.semaphore_signal(barrier, inc=1, device_id=peer(axis, k), device_id_type=pl.DeviceIdType.MESH)
-            count += 1
-    pl.semaphore_wait(barrier, count)
+    targets = [{"y": ky, "x": kx} for ky, kx in plane] + [{"z": k} for k in range(1, nz)]
+    for offsets in targets:
+        pl.semaphore_signal(barrier, inc=1, device_id=peer(offsets), device_id_type=pl.DeviceIdType.MESH)
+    pl.semaphore_wait(barrier, len(targets))
 
     sends = []
-
-    def stage(t, axis, src_of, land):
-        n = sizes[axis]
-        for k in range(1, n):
-            copy = pltpu.make_async_remote_copy(
-                src_ref=src_of(lax.rem(pos[axis] + k, n)), dst_ref=land.at[pos[axis]],
-                send_sem=send_sem.at[t, k], recv_sem=recv_sem.at[t, (n - k) % n],
-                device_id=peer(axis, k), device_id_type=pl.DeviceIdType.MESH,
-            )
-            copy.start()
-            sends.append(copy)
-        for j in range(1, n):
-            slot = land.at[lax.rem(pos[axis] + j, n)]
-            pltpu.make_async_remote_copy(
-                src_ref=slot, dst_ref=slot, send_sem=send_sem.at[t, j], recv_sem=recv_sem.at[t, j],
-                device_id=peer(axis, j), device_id_type=pl.DeviceIdType.MESH,
-            ).wait_recv()
-
-    r1[pos["y"]] = a_ref[pos["y"]]
-    stage(0, "y", lambda i: a_ref.at[i], r1)
+    mine = pos["y"] * nx + pos["x"]
+    r1[mine] = a_ref[mine]
+    for ky, kx in plane:
+        there = lax.rem(pos["y"] + ky, ny) * nx + lax.rem(pos["x"] + kx, nx)
+        copy = pltpu.make_async_remote_copy(
+            src_ref=a_ref.at[there], dst_ref=r1.at[mine], send_sem=send_sem.at[0, ky * nx + kx],
+            recv_sem=recv_sem.at[0, ((ny - ky) % ny) * nx + (nx - kx) % nx],
+            device_id=peer({"y": ky, "x": kx}), device_id_type=pl.DeviceIdType.MESH,
+        )
+        copy.start()
+        sends.append(copy)
+    for jy, jx in plane:
+        slot = r1.at[lax.rem(pos["y"] + jy, ny) * nx + lax.rem(pos["x"] + jx, nx)]
+        pltpu.make_async_remote_copy(
+            src_ref=slot, dst_ref=slot, send_sem=send_sem.at[0, jy * nx + jx], recv_sem=recv_sem.at[0, jy * nx + jx],
+            device_id=peer({"y": jy, "x": jx}), device_id_type=pl.DeviceIdType.MESH,
+        ).wait_recv()
     c1[...] = combine(r1[...])
-    own_x = pl.multiple_of(pos["x"] * LANES, LANES)
-    r2[pos["x"]] = c1[:, pl.ds(own_x, LANES)]
-    stage(1, "x", lambda i: c1.at[:, pl.ds(pl.multiple_of(i * LANES, LANES), LANES)], r2)
-    c2[...] = combine(r2[...])
-    r3[pos["z"]] = c2[...]
-    stage(2, "z", lambda i: c2, r3)
-    out_ref[...] = combine(r3[...])
+    r2[pos["z"]] = c1[...]
+    for k in range(1, nz):
+        copy = pltpu.make_async_remote_copy(
+            src_ref=c1, dst_ref=r2.at[pos["z"]], send_sem=send_sem.at[1, k], recv_sem=recv_sem.at[1, (nz - k) % nz],
+            device_id=peer({"z": k}), device_id_type=pl.DeviceIdType.MESH,
+        )
+        copy.start()
+        sends.append(copy)
+    for j in range(1, nz):
+        slot = r2.at[lax.rem(pos["z"] + j, nz)]
+        pltpu.make_async_remote_copy(
+            src_ref=slot, dst_ref=slot, send_sem=send_sem.at[1, j], recv_sem=recv_sem.at[1, j],
+            device_id=peer({"z": j}), device_id_type=pl.DeviceIdType.MESH,
+        ).wait_recv()
+    out_ref[...] = combine(r2[...])
     for copy in sends:
         copy.wait_send()
 
 
 def reduce_stats(parts, sizes):
-    ny, nx, nz = sizes["y"], sizes["x"], sizes["z"]
-    longest = max(ny, nx, nz)
-    width = parts.shape[-1]
+    planes, nz = parts.shape[0], sizes["z"]
+    labels = max(planes, nz)
     return pl.pallas_call(
         functools.partial(reduce_kernel, sizes),
         out_shape=jax.ShapeDtypeStruct((4, LANES), jnp.float32),
         scratch_shapes=[
-            pltpu.VMEM((ny, 4, width), jnp.float32),
-            pltpu.VMEM((4, width), jnp.float32),
-            pltpu.VMEM((nx, 4, LANES), jnp.float32),
+            pltpu.VMEM((planes, 4, LANES), jnp.float32),
             pltpu.VMEM((4, LANES), jnp.float32),
             pltpu.VMEM((nz, 4, LANES), jnp.float32),
-            pltpu.SemaphoreType.DMA((3, longest)),
-            pltpu.SemaphoreType.DMA((3, longest)),
+            pltpu.SemaphoreType.DMA((2, labels)),
+            pltpu.SemaphoreType.DMA((2, labels)),
         ],
         compiler_params=pltpu.CompilerParams(collective_id=1, has_side_effects=True),
     )(parts)
@@ -281,7 +284,7 @@
     all_ids = decode_ids(gathered[:, width:width + 3])
     stats = jnp.stack(slice_stats(all_rows, all_ids, chip_head, col_index, real_cols), axis=0)
 
-    parts = jnp.transpose(stats.reshape(4, size["y"], -1), (1, 0, 2))
+    parts = jnp.transpose(stats.reshape(4, size["y"] * size["x"], -1), (1, 0, 2))
     reduced = reduce_stats(parts, size)
     mine = lax.dynamic_slice_in_dim(reduced, pos["z"] * local_rows, local_rows, axis=1)
     top, total_all, weighted_all, picked_all = mine[0], mine[1], mine[2], mine[3]

time: 112 us -> 110 us (0.982)
  Pallas kernels: 93.7 us -> 91.7 us
    pallas_call x1, Pallas kernels: 17.6 us -> 15.6 us  [reduce_stats(): pl.pallas_call(functools.partial(reduce_kernel, sizes), out_shape=jax.Sha...]
  transfers between devices with their start and end apart: 1 -> 1, of which waited for: 0 -> 0; matrix products, arithmetic and copies ran while one was open for 2% -> 2% of each run, Pallas kernels for 68% -> 69%
where the time goes in v19:
time: 110 us
  Pallas kernels  91.7 us (83%)
  matrix products  10.3 us (9%)
  other arithmetic  4.7 us (4%)
  local copies, waits for them, and re-layouts  2.04 us (2%)
    pallas_call x1, Pallas kernels, gather_rows(): pl.pallas_call(functools.partial(gather_kernel, sizes, spans), out_shape=...  74.4 us
    pallas_call x1, Pallas kernels, reduce_stats(): pl.pallas_call(functools.partial(reduce_kernel, sizes), out_shape=jax.Sha...  15.6 us
    dot_general x1, matrix products, slice_stats(): logits = jnp.dot(rows, head, preferred_element_type=jnp.float32) / 10.0  10.3 us
    reduce_sum x1, other arithmetic, slice_stats(): total = jnp.sum(expo, axis=1)  2.34 us
  transfers between devices with their start and end apart: 1, of which 0 were waited for; matrix products, arithmetic and copies ran while one was open for 2% of the time, Pallas kernels for 69%

profile of v19, /device:TPU:2, one launch (start us, length us, event | category | flops | bytes accessed | tf_op | source)
XLA Modules:
  0.0 109.6 jit_solution(18386596334862900781)
XLA Ops:
  0.6 0.1 collective-permute-start
  0.7 1.7 %shard_map.77.x_ref = bf16[16,2688]{1,0:T(8,128)(2,1)} custom-call(bf16[16,2560]{1,0:T(8,128)(2,1)} %h_ref.1, f32[2560]{0:T(1024)} %gain_ref.1, s32[16]{0:T(128)} %ids_ref.1), custom_call_target="tpu_custom_call" | custom-call | tf_op jit(solution)/shard_map/pallas_call | solution.py:255
  2.5 0.0 copy-start
  2.5 0.0 copy-start.1
  2.5 0.0 copy-start.2
  2.5 74.4 %shard_map.78 = bf16[4,4,8,16,2688]{4,3,2,1,0:T(8,128)(2,1)} custom-call(bf16[16,2688]{1,0:T(8,128)(2,1)} %shard_map.77.x_ref), custom_call_target="tpu_custom_call" | custom-call | tf_op jit(solution)/shard_map/pallas_call | solution.py:143
  76.9 1.1 slice.37
  77.9 0.2 copy.9
  78.2 0.0 copy-done
  78.2 0.0 copy-done.1
  78.2 0.6 select_reduce_fusion.2
  78.9 0.0 collective-permute-done
  78.9 0.0 copy-done.2
  78.9 10.3 %fusion.13 = (f32[2048]{0:T(1024)S(1)}, f32[2048,576]{0,1:T(8,128)S(1)}) fusion(bf16[2560,288]{0,1:T(8,128)(2,1)S(1)} %collective-permute-done, bf16[2560,288]{0,1:T(8,128)(2,1)S(1)} %copy-done.2, pred[]{:T(512)S(6)} %eq.26, bf16[2048,2688]{1,0:T(8,128)(2,1)} %bitcast.27, pred[576]{0:T(1024)(128)(4,1)S(1)} %broadcast_compare_fusion), kind=kOutput, calls=%fused_computation.31 | convolution fusion | flops 6056605696 | bytes 18162240 | tf_op jit(solution)/shard_map/dot_general | solution.py:21
  89.2 2.3 %fusion.2 = (f32[2048]{0:T(1024)S(1)}, f32[2048]{0:T(1024)S(1)}, f32[2048]{0:T(1024)S(1)}) fusion(f32[2048,576]{0,1:T(8,128)S(1)} %get-tuple-element.8, f32[2048]{0:T(1024)S(1)} %get-tuple-element.7, pred[576]{0:T(1024)(128)(4,1)S(1)} %broadcast_compare_fusion, s32[2048]{0:T(1024)S(1)} %bitcast.28, s32[576]{0:T(1024)S(1)} %iota_add_fusion), kind=kLoop, calls=%fused_computation.5 | loop fusion | flops 10610688 | bytes 4762432 | tf_op jit(solution)/shard_map/reduce_sum | solution.py:25
  91.6 0.6 maximum_bitcast_fusion.a_ref
  92.2 15.6 %shard_map.79 = f32[4,128]{1,0:T(4,128)} custom-call(f32[16,4,128]{2,1,0:T(4,128)} %maximum_bitcast_fusion.a_ref), custom_call_target="tpu_custom_call" | custom-call | tf_op jit(solution)/shard_map/pallas_call | solution.py:224
  107.8 0.7 constant_dynamic-slice_fusion
  108.5 1.1 compare_select_fusion
  (4 shorter events, 0.1 us)
Async XLA Ops:
  0.6 78.2 %collective-permute-start = (bf16[2560,288]{0,1:T(8,128)(2,1)}, bf16[2560,288]{0,1:T(8,128)(2,1)S(1)}, u32[]{:S(2)}, u32[]{:S(2)}) collective-permute-start(bf16[2560,288]{0,1:T(8,128)(2,1)} %param.8), channel_id=1, source_target_pairs={{0,1},{1,0},{2,3},{3,2},{4,5},{5,4},{6,7},{7,6},{8,9},{9,8},{10,11... | collective-permute-start | bytes 4423688 | tf_op jit(solution)/shard_map/ppermute | solution.py:277
  2.5 75.8 %copy-start = (s32[512]{0:T(512)S(1)}, s32[512]{0:T(512)}, u32[]{:S(2)}) copy-start(s32[512]{0:T(512)} %param.10) | copy-start | bytes 6148
  2.5 75.8 %copy-start.1 = (s32[512]{0:T(512)S(1)}, s32[512]{0:T(512)}, u32[]{:S(2)}) copy-start(s32[512]{0:T(512)} %param.11) | copy-start | bytes 6148
  2.5 76.4 %copy-start.2 = (bf16[2560,288]{0,1:T(8,128)(2,1)S(1)}, bf16[2560,288]{0,1:T(8,128)(2,1)}, u32[]{:S(2)}) copy-start(bf16[2560,288]{0,1:T(8,128)(2,1)} %param.8) | copy-start | bytes 4423684

commit v20 on v11

--- a/solution.py
+++ b/solution.py
@@ -163,70 +163,78 @@
     return jnp.stack([top, total, weighted, picked], axis=0)
 
 
-def reduce_kernel(sizes, a_ref, out_ref, r1, c1, r2, c2, r3, send_sem, recv_sem):
+def reduce_kernel(sizes, a_ref, out_ref, r, send_sem, recv_sem):
     pos = {a: lax.axis_index(a) for a in AXES}
-
-    def peer(axis, k):
-        at = dict(pos)
-        at[axis] = lax.rem(pos[axis] + k, sizes[axis])
-        return tuple(at[a] for a in AXES)
+    ny, nx, nz = sizes["y"], sizes["x"], sizes["z"]
+    count = ny * nx * nz
+
+    def offsets(i):
+        return i // (nx * nz), (i // nz) % nx, i % nz
+
+    def chip(dy, dx, dz):
+        return (lax.rem(pos["y"] + dy, ny) * nx + lax.rem(pos["x"] + dx, nx)) * nz + lax.rem(pos["z"] + dz, nz)
+
+    def device(dy, dx, dz):
+        return (lax.rem(pos["z"] + dz, nz), lax.rem(pos["x"] + dx, nx), lax.rem(pos["y"] + dy, ny), pos["core"])
+
+    def label(dy, dx, dz):
+        return ((ny - dy) % ny * nx + (nx - dx) % nx) * nz + (nz - dz) % nz
+
+    def copy_to(i):
+        dy, dx, dz = offsets(i)
+        return pltpu.make_async_remote_copy(
+            src_ref=a_ref.at[chip(dy, dx, dz)], dst_ref=r.at[chip(0, 0, 0)], send_sem=send_sem.at[i],
+            recv_sem=recv_sem.at[label(dy, dx, dz)], device_id=device(dy, dx, dz),
+            device_id_type=pl.DeviceIdType.MESH,
+        )
+
+    def copy_from(j):
+        dy, dx, dz = offsets(j)
+        slot = r.at[chip(dy, dx, dz)]
+        return pltpu.make_async_remote_copy(
+            src_ref=slot, dst_ref=slot, send_sem=send_sem.at[j], recv_sem=recv_sem.at[j],
+            device_id=device(dy, dx, dz), device_id_type=pl.DeviceIdType.MESH,
+        )
 
     barrier = pltpu.get_barrier_semaphore()
-    count = 0
-    for axis in CHIP_AXES:
-        for k in range(1, sizes[axis]):
-            pl.semaphore_signal(barrier, inc=1, device_id=peer(axis, k), device_id_type=pl.DeviceIdType.MESH)
-            count += 1
-    pl.semaphore_wait(barrier, count)
-
-    sends = []
-
-    def stage(t, axis, src_of, land):
-        n = sizes[axis]
-        for k in range(1, n):
-            copy = pltpu.make_async_remote_copy(
-                src_ref=src_of(lax.rem(pos[axis] + k, n)), dst_ref=land.at[pos[axis]],
-                send_sem=send_sem.at[t, k], recv_sem=recv_sem.at[t, (n - k) % n],
-                device_id=peer(axis, k), device_id_type=pl.DeviceIdType.MESH,
-            )
-            copy.start()
-            sends.append(copy)
-        for j in range(1, n):
-            slot = land.at[lax.rem(pos[axis] + j, n)]
-            pltpu.make_async_remote_copy(
-                src_ref=slot, dst_ref=slot, send_sem=send_sem.at[t, j], recv_sem=recv_sem.at[t, j],
-                device_id=peer(axis, j), device_id_type=pl.DeviceIdType.MESH,
-            ).wait_recv()
-
-    r1[pos["y"]] = a_ref[pos["y"]]
-    stage(0, "y", lambda i: a_ref.at[i], r1)
-    c1[...] = combine(r1[...])
-    own_x = pl.multiple_of(pos["x"] * LANES, LANES)
-    r2[pos["x"]] = c1[:, pl.ds(own_x, LANES)]
-    stage(1, "x", lambda i: c1.at[:, pl.ds(pl.multiple_of(i * LANES, LANES), LANES)], r2)
-    c2[...] = combine(r2[...])
-    r3[pos["z"]] = c2[...]
-    stage(2, "z", lambda i: c2, r3)
-    out_ref[...] = combine(r3[...])
-    for copy in sends:
-        copy.wait_send()
+
+    def greet(i, carry):
+        pl.semaphore_signal(barrier, inc=1, device_id=device(*offsets(i)), device_id_type=pl.DeviceIdType.MESH)
+        return carry
+
+    lax.fori_loop(1, count, greet, 0)
+    pl.semaphore_wait(barrier, count - 1)
+
+    mine = chip(0, 0, 0)
+    r[mine] = a_ref[mine]
+
+    def send(i, carry):
+        copy_to(i).start()
+        return carry
+
+    def receive(j, carry):
+        copy_from(j).wait_recv()
+        return carry
+
+    def sent(i, carry):
+        copy_to(i).wait_send()
+        return carry
+
+    lax.fori_loop(1, count, send, 0)
+    lax.fori_loop(1, count, receive, 0)
+    out_ref[...] = combine(r[...])
+    lax.fori_loop(1, count, sent, 0)
 
 
 def reduce_stats(parts, sizes):
-    ny, nx, nz = sizes["y"], sizes["x"], sizes["z"]
-    longest = max(ny, nx, nz)
-    width = parts.shape[-1]
+    count = parts.shape[0]
     return pl.pallas_call(
         functools.partial(reduce_kernel, sizes),
-        out_shape=jax.ShapeDtypeStruct((4, LANES), jnp.float32),
+        out_shape=jax.ShapeDtypeStruct(parts.shape[1:], jnp.float32),
         scratch_shapes=[
-            pltpu.VMEM((ny, 4, width), jnp.float32),
-            pltpu.VMEM((4, width), jnp.float32),
-            pltpu.VMEM((nx, 4, LANES), jnp.float32),
-            pltpu.VMEM((4, LANES), jnp.float32),
-            pltpu.VMEM((nz, 4, LANES), jnp.float32),
-            pltpu.SemaphoreType.DMA((3, longest)),
-            pltpu.SemaphoreType.DMA((3, longest)),
+            pltpu.VMEM(parts.shape, jnp.float32),
+            pltpu.SemaphoreType.DMA((count,)),
+            pltpu.SemaphoreType.DMA((count,)),
         ],
         compiler_params=pltpu.CompilerParams(collective_id=1, has_side_effects=True),
     )(parts)
@@ -281,9 +289,8 @@
     all_ids = decode_ids(gathered[:, width:width + 3])
     stats = jnp.stack(slice_stats(all_rows, all_ids, chip_head, col_index, real_cols), axis=0)
 
-    parts = jnp.transpose(stats.reshape(4, size["y"], -1), (1, 0, 2))
-    reduced = reduce_stats(parts, size)
-    mine = lax.dynamic_slice_in_dim(reduced, pos["z"] * local_rows, local_rows, axis=1)
+    parts = jnp.transpose(stats.reshape(4, -1, local_rows), (1, 0, 2))
+    mine = reduce_stats(parts, size)
     top, total_all, weighted_all, picked_all = mine[0], mine[1], mine[2], mine[3]
 
     load = jnp.sum(jnp.where(req_owner == me, req_len, 0))

time: 112 us -> 123 us (1.098)
  Pallas kernels: 93.7 us -> 99.7 us
  other arithmetic: 4.7 us -> 7.6 us
  matrix products: 10.3 us -> 12.5 us
    pallas_call x1, Pallas kernels: 17.6 us -> 23.6 us  [reduce_stats(): pl.pallas_call(functools.partial(reduce_kernel, sizes), out_shape=jax.Sha...]
    dot_general x1, matrix products: 10.3 us -> 12.5 us  [slice_stats(): logits = jnp.dot(rows, head, preferred_element_type=jnp.float32) / 10.0]
    reduce_sum x1, other arithmetic: 2.34 us -> 3.93 us  [slice_stats(): total = jnp.sum(expo, axis=1)]
  transfers between devices with their start and end apart: 1 -> 1, of which waited for: 0 -> 0; matrix products, arithmetic and copies ran while one was open for 2% -> 2% of each run, Pallas kernels for 68% -> 62%
where the time goes in v20:
time: 123 us; the launch traced here: 122 us
  Pallas kernels  99.7 us (81%)
  matrix products  12.5 us (10%)
  other arithmetic  7.6 us (6%)
  local copies, waits for them, and re-layouts  1.61 us (1%)
    pallas_call x1, Pallas kernels, gather_rows(): pl.pallas_call(functools.partial(gather_kernel, sizes, spans), out_shape=...  74.4 us
    pallas_call x1, Pallas kernels, reduce_stats(): pl.pallas_call(functools.partial(reduce_kernel, sizes), out_shape=jax.Sha...  23.6 us
    dot_general x1, matrix products, slice_stats(): logits = jnp.dot(rows, head, preferred_element_type=jnp.float32) / 10.0  12.5 us
    reduce_sum x1, other arithmetic, slice_stats(): total = jnp.sum(expo, axis=1)  3.93 us
  transfers between devices with their start and end apart: 1, of which 0 were waited for; matrix products, arithmetic and copies ran while one was open for 2% of the time, Pallas kernels for 62%

profile of v20, /device:TPU:2, one launch (start us, length us, event | category | flops | bytes accessed | tf_op | source)
XLA Modules:
  0.0 122.4 jit_solution(12775660427917850581)
XLA Ops:
  0.6 0.1 collective-permute-start
  0.7 1.7 %shard_map.77.x_ref = bf16[16,2688]{1,0:T(8,128)(2,1)} custom-call(bf16[16,2560]{1,0:T(8,128)(2,1)} %h_ref.1, f32[2560]{0:T(1024)} %gain_ref.1, s32[16]{0:T(128)} %ids_ref.1), custom_call_target="tpu_custom_call" | custom-call | tf_op jit(solution)/shard_map/pallas_call | solution.py:260
  2.5 0.0 copy-start
  2.5 0.0 copy-start.1
  2.5 0.0 copy-start.2
  2.5 74.4 %shard_map.78 = bf16[4,4,8,16,2688]{4,3,2,1,0:T(8,128)(2,1)} custom-call(bf16[16,2688]{1,0:T(8,128)(2,1)} %shard_map.77.x_ref), custom_call_target="tpu_custom_call" | custom-call | tf_op jit(solution)/shard_map/pallas_call | solution.py:143
  76.9 1.1 slice.37
  77.9 0.2 copy.24
  78.2 0.0 copy-done
  78.2 0.0 copy-done.1
  78.2 0.7 select_reduce_fusion.2
  78.9 0.0 collective-permute-done
  78.9 0.0 copy-done.2
  78.9 12.5 %fusion.13 = (f32[2048]{0:T(1024)S(1)}, f32[2048,576]{0,1:T(8,128)}) fusion(bf16[2560,288]{0,1:T(8,128)(2,1)S(1)} %collective-permute-done, bf16[2560,288]{0,1:T(8,128)(2,1)S(1)} %copy-done.2, pred[]{:T(512)S(6)} %eq.26, bf16[2048,2688]{1,0:T(8,128)(2,1)} %bitcast.27, pred[576]{0:T(1024)(128)(4,1)S(1)} %broadcast_compare_fusion), kind=kOutput, calls=%fused_computation.30 | convolution fusion | flops 6056605696 | bytes 18162240 | tf_op jit(solution)/shard_map/dot_general | solution.py:21
  91.5 0.1 stack.15
  91.6 3.9 %fusion.2 = (f32[2048]{0:T(1024)S(1)}, f32[2048]{0:T(1024)S(1)}, f32[2048]{0:T(1024)S(1)}) fusion(f32[2048,576]{0,1:T(8,128)} %get-tuple-element.8, f32[2048]{0:T(1024)S(1)} %get-tuple-element.7, pred[576]{0:T(1024)(128)(4,1)S(1)} %broadcast_compare_fusion, s32[2048]{0:T(1024)S(1)} %bitcast.32, s32[576]{0:T(1024)S(1)} %iota_add_fusion), kind=kLoop, calls=%fused_computation.5 | loop fusion | flops 10610688 | bytes 4762432 | tf_op jit(solution)/shard_map/reduce_sum | solution.py:25
  95.5 0.1 stack.16
  95.6 0.1 stack.17
  95.7 0.1 stack.18
  95.8 1.0 maximum_bitcast_fusion.a_ref
  96.7 23.6 %shard_map.79 = f32[4,16]{1,0:T(4,128)} custom-call(f32[128,4,16]{2,1,0:T(4,128)} %maximum_bitcast_fusion.a_ref), custom_call_target="tpu_custom_call" | custom-call | tf_op jit(solution)/shard_map/pallas_call | solution.py:231
  120.4 2.0 %compare_select_fusion = (f32[16]{0:T(128)}, f32[16]{0:T(128)}) fusion(f32[4,16]{1,0:T(4,128)} %shard_map.79, s32[]{:T(128)} %select_reduce_fusion.2), kind=kLoop, calls=%fused_computation.22 | loop fusion | flops 128 | bytes 388 | tf_op jit(solution)/shard_map/jit(_where)/select_n | solution.py:300
  (4 shorter events, 0.1 us)
Async XLA Ops:
  0.6 78.3 %collective-permute-start = (bf16[2560,288]{0,1:T(8,128)(2,1)}, bf16[2560,288]{0,1:T(8,128)(2,1)S(1)}, u32[]{:S(2)}, u32[]{:S(2)}) collective-permute-start(bf16[2560,288]{0,1:T(8,128)(2,1)} %param.8), channel_id=1, source_target_pairs={{0,1},{1,0},{2,3},{3,2},{4,5},{5,4},{6,7},{7,6},{8,9},{9,8},{10,11... | collective-permute-start | bytes 4423688 | tf_op jit(solution)/shard_map/ppermute | solution.py:282
  2.5 75.7 %copy-start = (s32[512]{0:T(512)S(1)}, s32[512]{0:T(512)}, u32[]{:S(2)}) copy-start(s32[512]{0:T(512)} %param.10) | copy-start | bytes 6148
  2.5 75.8 %copy-start.1 = (s32[512]{0:T(512)S(1)}, s32[512]{0:T(512)}, u32[]{:S(2)}) copy-start(s32[512]{0:T(512)} %param.11) | copy-start | bytes 6148
  2.5 76.5 %copy-start.2 = (bf16[2560,288]{0,1:T(8,128)(2,1)S(1)}, bf16[2560,288]{0,1:T(8,128)(2,1)}, u32[]{:S(2)}) copy-start(bf16[2560,288]{0,1:T(8,128)(2,1)} %param.8) | copy-start | bytes 4423684

commit v21 on v19

--- a/solution.py
+++ b/solution.py
@@ -64,7 +64,8 @@
     barrier = pltpu.get_barrier_semaphore()
     count = 0
     for axis in CHIP_AXES:
-        for k in (1, -1):
+        reach = range(1, sizes[axis]) if axis == STREAMS[1][0] else (1, -1)
+        for k in reach:
             pl.semaphore_signal(barrier, inc=1, device_id=peer(axis, k), device_id_type=pl.DeviceIdType.MESH)
             count += 1
     pl.semaphore_wait(barrier, count)
@@ -74,8 +75,9 @@
 
     plans = []
     for order in STREAMS:
-        plan = []
-        for t, axis in enumerate(order):
+        direct = order == STREAMS[1]
+        plan = [(0, order[0], 0, False)] if direct else []
+        for t, axis in enumerate(order[1:] if direct else order, start=1 if direct else 0):
             n = sizes[axis]
             for q in range(1, n // 2 + 1):
                 plan.append((t, axis, q, n % 2 == 0 and q == n // 2))
@@ -86,12 +88,29 @@
         c0, w = spans[s]
         order = STREAMS[s]
         held = order[:t]
+        n = sizes[axis]
+        out = []
+        if q == 0:
+            cols = pl.ds(c0, w)
+            for k in range(1, n):
+                if sending:
+                    dst = view(g_ref, held, axis, 0, cols)
+                    src = x_ref.at[:, cols] if t == 0 else dst
+                    target, label = peer(axis, k), (n - k) % n
+                else:
+                    src = dst = view(g_ref, held, axis, k, cols)
+                    target, label = peer(axis, k), k
+                out.append(pltpu.make_async_remote_copy(
+                    src_ref=src, dst_ref=dst, send_sem=send_sem.at[s, step, k if sending else label],
+                    recv_sem=recv_sem.at[s, step, label], device_id=target,
+                    device_id_type=pl.DeviceIdType.MESH,
+                ))
+            return out
         if split:
             cut = (w // LANES // 2) * LANES
             col_of = [pl.ds(c0, cut), pl.ds(c0 + cut, w - cut)]
         else:
             col_of = [pl.ds(c0, w), pl.ds(c0, w)]
-        out = []
         for d, sign in enumerate((1, -1)):
             cols = col_of[d]
             if sending:
@@ -110,10 +129,12 @@
             ))
         return out
 
-    steps = len(plans[0])
+    steps = max(len(p) for p in plans)
     sends = []
     for g in range(steps):
         for s in range(len(STREAMS)):
+            if g >= len(plans[s]):
+                continue
             if g > 0:
                 for copy in step_copies(s, g - 1, False):
                     copy.wait_recv()
@@ -123,7 +144,7 @@
                 copy.start()
                 sends.append(copy)
     for s in range(len(STREAMS)):
-        for copy in step_copies(s, steps - 1, False):
+        for copy in step_copies(s, len(plans[s]) - 1, False):
             copy.wait_recv()
     for copy in sends:
         copy.wait_send()
@@ -140,14 +161,15 @@
         at += c
     shape = (sizes["y"], sizes["x"], sizes["z"], rows, width)
     steps = sum(sizes[a] // 2 for a in CHIP_AXES)
+    longest = max(sizes[a] for a in CHIP_AXES)
     return pl.pallas_call(
         functools.partial(gather_kernel, sizes, spans),
         out_shape=jax.ShapeDtypeStruct(shape, packed.dtype),
         in_specs=[pl.BlockSpec(memory_space=pl.ANY)],
         out_specs=pl.BlockSpec(memory_space=pl.ANY),
         scratch_shapes=[
-            pltpu.SemaphoreType.DMA((3, steps, 2)),
-            pltpu.SemaphoreType.DMA((3, steps, 2)),
+            pltpu.SemaphoreType.DMA((3, steps, longest)),
+            pltpu.SemaphoreType.DMA((3, steps, longest)),
             pltpu.SemaphoreType.DMA(()),
         ],
         compiler_params=pltpu.CompilerParams(collective_id=0, has_side_effects=True),

time: 110 us -> 119 us (1.082)
  Pallas kernels: 91.7 us -> 101 us
    pallas_call x1, Pallas kernels: 74.4 us -> 84.3 us  [gather_rows(): pl.pallas_call(functools.partial(gather_kernel, sizes, spans), out_shape=...]
  transfers between devices with their start and end apart: 1 -> 1, of which waited for: 0 -> 0; matrix products, arithmetic and copies ran while one was open for 2% -> 2% of each run, Pallas kernels for 69% -> 72%
where the time goes in v21:
time: 119 us
  Pallas kernels  101 us (85%)
  matrix products  10.3 us (9%)
  other arithmetic  4.7 us (4%)
  local copies, waits for them, and re-layouts  2.04 us (2%)
    pallas_call x1, Pallas kernels, gather_rows(): pl.pallas_call(functools.partial(gather_kernel, sizes, spans), out_shape=...  84.3 us
    pallas_call x1, Pallas kernels, reduce_stats(): pl.pallas_call(functools.partial(reduce_kernel, sizes), out_shape=jax.Sha...  15.1 us
    dot_general x1, matrix products, slice_stats(): logits = jnp.dot(rows, head, preferred_element_type=jnp.float32) / 10.0  10.3 us
  transfers between devices with their start and end apart: 1, of which 0 were waited for; matrix products, arithmetic and copies ran while one was open for 2% of the time, Pallas kernels for 72%

profile of v21, /device:TPU:2, one launch (start us, length us, event | category | flops | bytes accessed | tf_op | source)
XLA Modules:
  0.0 119.1 jit_solution(240773048564376245)
XLA Ops:
  0.6 0.1 collective-permute-start
  0.7 1.7 %shard_map.77.x_ref = bf16[16,2688]{1,0:T(8,128)(2,1)} custom-call(bf16[16,2560]{1,0:T(8,128)(2,1)} %h_ref.1, f32[2560]{0:T(1024)} %gain_ref.1, s32[16]{0:T(128)} %ids_ref.1), custom_call_target="tpu_custom_call" | custom-call | tf_op jit(solution)/shard_map/pallas_call | solution.py:277
  2.5 0.0 copy-start
  2.5 0.0 copy-start.1
  2.5 0.0 copy-start.2
  2.5 84.3 %shard_map.78 = bf16[4,4,8,16,2688]{4,3,2,1,0:T(8,128)(2,1)} custom-call(bf16[16,2688]{1,0:T(8,128)(2,1)} %shard_map.77.x_ref), custom_call_target="tpu_custom_call" | custom-call | tf_op jit(solution)/shard_map/pallas_call | solution.py:165
  86.7 1.1 slice.37
  87.8 0.2 copy.9
  88.1 0.0 copy-done
  88.1 0.0 copy-done.1
  88.1 0.6 select_reduce_fusion.2
  88.8 0.0 collective-permute-done
  88.8 0.0 copy-done.2
  88.8 10.3 %fusion.13 = (f32[2048]{0:T(1024)S(1)}, f32[2048,576]{0,1:T(8,128)S(1)}) fusion(bf16[2560,288]{0,1:T(8,128)(2,1)S(1)} %collective-permute-done, bf16[2560,288]{0,1:T(8,128)(2,1)S(1)} %copy-done.2, pred[]{:T(512)S(6)} %eq.26, bf16[2048,2688]{1,0:T(8,128)(2,1)} %bitcast.27, pred[576]{0:T(1024)(128)(4,1)S(1)} %broadcast_compare_fusion), kind=kOutput, calls=%fused_computation.31 | convolution fusion | flops 6056605696 | bytes 18162240 | tf_op jit(solution)/shard_map/dot_general | solution.py:21
  99.1 2.3 %fusion.2 = (f32[2048]{0:T(1024)S(1)}, f32[2048]{0:T(1024)S(1)}, f32[2048]{0:T(1024)S(1)}) fusion(f32[2048,576]{0,1:T(8,128)S(1)} %get-tuple-element.8, f32[2048]{0:T(1024)S(1)} %get-tuple-element.7, pred[576]{0:T(1024)(128)(4,1)S(1)} %broadcast_compare_fusion, s32[2048]{0:T(1024)S(1)} %bitcast.28, s32[576]{0:T(1024)S(1)} %iota_add_fusion), kind=kLoop, calls=%fused_computation.5 | loop fusion | flops 10610688 | bytes 4762432 | tf_op jit(solution)/shard_map/reduce_sum | solution.py:25
  101.5 0.6 maximum_bitcast_fusion.a_ref
  102.1 15.1 %shard_map.79 = f32[4,128]{1,0:T(4,128)} custom-call(f32[16,4,128]{2,1,0:T(4,128)} %maximum_bitcast_fusion.a_ref), custom_call_target="tpu_custom_call" | custom-call | tf_op jit(solution)/shard_map/pallas_call | solution.py:246
  117.3 0.7 constant_dynamic-slice_fusion
  118.0 1.1 compare_select_fusion
  (4 shorter events, 0.1 us)
Async XLA Ops:
  0.6 88.1 %collective-permute-start = (bf16[2560,288]{0,1:T(8,128)(2,1)}, bf16[2560,288]{0,1:T(8,128)(2,1)S(1)}, u32[]{:S(2)}, u32[]{:S(2)}) collective-permute-start(bf16[2560,288]{0,1:T(8,128)(2,1)} %param.8), channel_id=1, source_target_pairs={{0,1},{1,0},{2,3},{3,2},{4,5},{5,4},{6,7},{7,6},{8,9},{9,8},{10,11... | collective-permute-start | bytes 4423688 | tf_op jit(solution)/shard_map/ppermute | solution.py:299
  2.5 85.6 %copy-start = (s32[512]{0:T(512)S(1)}, s32[512]{0:T(512)}, u32[]{:S(2)}) copy-start(s32[512]{0:T(512)} %param.10) | copy-start | bytes 6148
  2.5 85.6 %copy-start.1 = (s32[512]{0:T(512)S(1)}, s32[512]{0:T(512)}, u32[]{:S(2)}) copy-start(s32[512]{0:T(512)} %param.11) | copy-start | bytes 6148
  2.5 86.3 %copy-start.2 = (bf16[2560,288]{0,1:T(8,128)(2,1)S(1)}, bf16[2560,288]{0,1:T(8,128)(2,1)}, u32[]{:S(2)}) copy-start(bf16[2560,288]{0,1:T(8,128)(2,1)} %param.8) | copy-start | bytes 4423684
